TPU v7x, 1024 devices: a whole 4x4x32 slice. The times are simulated.
1024 devices in a mesh: group: 256 (over y, x, z_lo, core), member: 4 (over z_hi).
Axes of the slice: x: 4, y: 4, z: 32 (z_hi: 4, z_lo: 8; z = z_hi * 8 + z_lo), core: 2. Of those that a mesh axis runs over, the one named last changes fastest.
Arguments:
- residual: float32 [2, 4096, 128, 128], P(None, 'group', 'member'), may hold values from -6 to 6
- horiz_vectors: float32 [2, 18, 18], replicated, may hold values from -1.5 to 1.5
- horiz_values: float32 [2, 18], replicated, may hold values from 0.2 to 4
- upward_eigen_tables: float32 [8, 18, 18], replicated, may hold values from -1.5 to 1.5
- upward_eigen_values: float32 [8, 18], replicated, may hold values from 0.2 to 4
- aggregate_map: int32 [256, 8, 8], P('group', 'member'), may hold values from 0 to 4095, as said below
- coarse_inverse: float32 [4096, 4096], P('group', 'member')
Outputs:
- preconditioned: float32 [2, 4096, 128, 128], P(None, 'group', 'member')
Inputs may be any that keep to these rules, and one draw needn't show every extreme that they name: `aggregate_map`: the aggregate of each element; an element's aggregate holds elements next to it; every aggregate holds some element.
All inputs are finite; a program needn't handle non-finite values.
Results may differ from a plain program's by a relative error of at most 0.0003.
Values sent between devices are 32-bit elements; how exact they have to be, the bound alone decides.
No kernel may reach another device: no remote copies, remote signals or barrier semaphores. Data moves between devices by JAX's collectives and lax.ppermute only.
A program may use at most 64 MiB of HBM per device.

v0:
```python
import jax
import jax.numpy as jnp
import numpy as np
from jax import lax
from jax.sharding import PartitionSpec as P

ELEMENT_POINTS = 16


def with_halo(shard, sides, width):
    for axis, dim in sides:
        devices, length = (lax.axis_size(axis), shard.shape[dim])
        up = [(i, (i + 1) % devices) for i in range(devices)]
        down = [(j, i) for i, j in up]
        last = lax.slice_in_dim(shard, length - width, length, axis=dim)
        leading = lax.slice_in_dim(shard, 0, width, axis=dim)
        before = lax.ppermute(last, axis, up)
        after = lax.ppermute(leading, axis, down)
        shard = jnp.concatenate([before, shard, after], axis=dim)
    return shard


def build_boxes(padded, span, count_y, count_z):
    extent = span + 2
    upward_rows = np.array(
        [k * span + c for k in range(count_z) for c in range(extent)], dtype=np.int32
    )
    second_rows = np.array(
        [j * span + b for j in range(count_y) for b in range(extent)], dtype=np.int32
    )
    stacked = jnp.take(padded, jnp.asarray(upward_rows), axis=3)
    stacked = jnp.take(stacked, jnp.asarray(second_rows), axis=2)
    vector_count = padded.shape[0]
    stacked = stacked.reshape(vector_count, extent, count_y, extent, count_z, extent)
    stacked = jnp.transpose(stacked, (1, 3, 0, 2, 4, 5))
    return stacked.reshape(extent, extent, vector_count * count_y * count_z * extent)


def fdm_solve(
    boxes,
    horiz_vectors,
    horiz_values,
    upward_eigen_tables,
    upward_eigen_values,
    batch_rows,
    count_z,
):
    highest = lax.Precision.HIGHEST
    extent = boxes.shape[0]
    lanes = boxes.shape[2]
    block_eye = jnp.eye(count_z, dtype=jnp.float32)
    block_table = (block_eye[:, None, :, None] * upward_eigen_tables[:, :, None, :]).reshape(
        count_z * extent, count_z * extent
    )
    hat = jnp.einsum("xyl,xa->ayl", boxes, horiz_vectors[0], precision=highest)
    hat = jnp.einsum("ayl,yb->abl", hat, horiz_vectors[1], precision=highest)
    hat = jnp.dot(
        hat.reshape(-1, count_z * extent),
        block_table,
        precision=highest,
        preferred_element_type=jnp.float32,
    )
    denominator = (
        horiz_values[0][:, None, None, None, None]
        + horiz_values[1][None, :, None, None, None]
        + upward_eigen_values[None, None, None, :, :]
    )
    scaled = hat.reshape(extent, extent, batch_rows, count_z, extent) / denominator
    solved = jnp.dot(
        scaled.reshape(-1, count_z * extent),
        block_table.T,
        precision=highest,
        preferred_element_type=jnp.float32,
    )
    solved = solved.reshape(extent, extent, lanes)
    solved = jnp.einsum("abl,yb->ayl", solved, horiz_vectors[1], precision=highest)
    solved = jnp.einsum("ayl,xa->xyl", solved, horiz_vectors[0], precision=highest)
    return solved


def on_device(
    residual,
    horiz_vectors,
    horiz_values,
    upward_eigen_tables,
    upward_eigen_values,
    aggregate_map,
    coarse_inverse,
):
    vector_count, points_x, span_y, span_z = residual.shape
    count_y = span_y // ELEMENT_POINTS
    count_z = span_z // ELEMENT_POINTS
    extent = ELEMENT_POINTS + 2
    partition_weight = float(ELEMENT_POINTS) ** (-1.5)
    aggregate_labels = aggregate_map.reshape(-1)
    slice_cols = coarse_inverse.shape[1]
    total_aggregates = coarse_inverse.shape[0] * lax.axis_size("group")
    padded = with_halo(residual, (("group", 1), ("member", 2)), 1)
    padded = jnp.pad(padded, ((0, 0), (0, 0), (0, 0), (1, 1)))
    boxes = build_boxes(padded, ELEMENT_POINTS, count_y, count_z)
    solved = fdm_solve(
        boxes,
        horiz_vectors,
        horiz_values,
        upward_eigen_tables,
        upward_eigen_values,
        vector_count * count_y,
        count_z,
    )
    solved = solved.reshape(extent, extent, vector_count, count_y, count_z, extent)
    solved = solved[1:-1, 1:-1, :, :, :, 1:-1]
    subdomain_part = jnp.transpose(solved, (2, 0, 3, 1, 4, 5))
    element_totals = residual.reshape(
        vector_count, ELEMENT_POINTS, count_y, ELEMENT_POINTS, count_z, ELEMENT_POINTS
    ).sum(axis=(1, 3, 5))
    element_totals = element_totals.reshape(vector_count, -1)
    partial_rhs = (
        partition_weight
        * jax.ops.segment_sum(element_totals.T, aggregate_labels, num_segments=total_aggregates).T
    )
    whole_rhs = lax.psum(partial_rhs, ("group", "member"))
    share_rhs = lax.dynamic_slice_in_dim(
        whole_rhs, lax.axis_index("member") * slice_cols, slice_cols, 1
    )
    row_terms = jnp.dot(
        share_rhs,
        coarse_inverse.T,
        precision=lax.Precision.HIGHEST,
        preferred_element_type=jnp.float32,
    )
    row_values = lax.psum(row_terms, "member")
    coarse_full = lax.all_gather(row_values, "group", axis=1, tiled=True)
    update_term = partition_weight * jnp.take(coarse_full, aggregate_labels, axis=1)
    update_term = update_term.reshape(vector_count, 1, count_y, 1, count_z, 1)
    merged_result = subdomain_part + update_term
    return merged_result.reshape(vector_count, points_x, span_y, span_z)


def solution(mesh):
    in_specs = (
        P(None, "group", "member", None),
        P(),
        P(),
        P(),
        P(),
        P("group", "member", None),
        P("group", "member"),
    )
    out_specs = P(None, "group", "member", None)
    return jax.shard_map(
        on_device, mesh=mesh, in_specs=in_specs, out_specs=out_specs, check_vma=False
    )
```

profile of v0, /device:TPU:1, one launch (start us, length us, event | category | flops | bytes accessed | tf_op | source)
XLA Modules:
  0.0 856.9 jit_solution(5790596910903294609)
XLA Ops:
  0.9 4.9 collective-permute-start
  5.8 13.0 %collective-permute-start.1 = (f32[2,1,32,128]{3,2,1,0:T(8,128)S(1)}, f32[2,1,32,128]{3,2,1,0:T(8,128)S(1)}, u32[]{:S(2)}, u32[]{:S(2)}) collective-permute-start(f32[2,1,32,128]{3,2,1,0:T(8,128)S(1)} %get-tuple-element.9), channel_id=1, source_target_pairs={{4,0},{8,4},{12,8},{16,12},{20,16},{24,20},{28,24},{32,28},{36,32}... | collective-permute-start | bytes 98312 | tf_op jit(solution)/shard_map/ppermute | solution.py:18
  27.2 4.3 collective-permute-start.2
  31.6 9.7 %collective-permute-start.3 = (f32[2,18,1,128]{3,0,2,1:T(2,128)S(1)}, f32[2,18,1,128]{3,0,2,1:T(2,128)S(1)}, u32[]{:S(2)}, u32[]{:S(2)}) collective-permute-start(f32[2,18,1,128]{3,0,2,1:T(2,128)S(1)} %copy.92), channel_id=1, source_target_pairs={{1,0},{2,1},{3,2},{0,3},{5,4},{6,5},{7,6},{4,7},{9,8},{10,9},{11,1... | collective-permute-start | bytes 55304 | tf_op jit(solution)/shard_map/ppermute | solution.py:18
  44.3 173.2 %psum.14 = f32[2,4096]{0,1:T(8,128)S(1)} all-reduce(f32[2,4096]{0,1:T(8,128)} %multiply_bitcast_fusion), channel_id=1, replica_groups=mesh['group'=256,'member'=4] {'group','member'}, use_global_device_ids=true, to_apply=%region_3.4 | all-reduce | flops 8192 | bytes 65536 | tf_op jit(solution)/shard_map/psum | solution.py:121
  218.5 19.9 %psum.15 = f32[2,16]{1,0:T(2,128)S(1)} all-reduce(f32[2,16]{1,0:T(2,128)S(1)} %fusion.6), channel_id=1, replica_groups=mesh['group'=256,'member'=4] {'member'}, use_global_device_ids=true, to_apply=%region_4.5 | all-reduce | flops 32 | bytes 256 | tf_op jit(solution)/shard_map/psum | solution.py:131
  238.4 520.3 %all-gather = f32[256,16,2]{1,2,0:T(2,128)S(1)} all-gather(f32[1,16,2]{1,2,0:T(2,128)S(1)} %bitcast.82), channel_id=1, replica_groups=mesh['group'=256,'member'=4] {'group'}, dimensions={0}, use_global_device_ids=true | all-gather | bytes 32896 | tf_op jit(solution)/shard_map/all_gather | solution.py:132
  760.9 3.8 copy.59
  764.7 2.5 copy.58
  767.3 2.4 copy.60
  769.7 7.4 select_maximum_fusion
  777.1 15.3 %gather_fusion = f32[144,2,18,34]{3,1,2,0:T(2,128)S(1)} fusion(f32[2,18,34,130]{2,0,3,1:T(2,128)} %select_maximum_fusion, s32[1024]{0:T(1024)S(1)} %pad_clamp_fusion.2), kind=kCustom, calls=%fused_computation | custom fusion | bytes 1410624 | tf_op jit(solution)/shard_map/jit(_take)/gather | solution.py:31
  792.4 3.6 copy.61
  796.0 3.4 gather_fusion.1
  799.9 4.3 gather.18
  804.2 5.6 copy.84
  809.8 5.8 reshape.206
  819.9 7.7 broadcast_divide_fusion
  827.6 3.2 copy.70
  830.8 4.2 reshape.159
  839.4 7.4 reshape.161
  846.8 3.3 fusion
  850.2 2.5 copy.78
  852.7 3.9 reshape.164
  (60 shorter events, 24.4 us)
Async XLA Ops:
  0.0 217.6 %copy-start = (f32[16,1024]{1,0:T(8,128)S(1)}, f32[16,1024]{1,0:T(8,128)}, u32[]{:S(2)}) copy-start(f32[16,1024]{1,0:T(8,128)} %param.15) | copy-start | bytes 196612
  0.0 27.1 %copy-start.4 = (f32[2,16,32,128]{3,2,1,0:T(8,128)S(1)}, f32[2,16,32,128]{3,2,1,0:T(8,128)}, u32[]{:S(2)}) copy-start(f32[2,16,32,128]{3,2,1,0:T(8,128)} %param.9) | copy-start | bytes 1572868
  0.0 26.5 %copy-start.5 = (s32[1,2,8]{2,1,0:T(2,128)S(1)}, s32[1,2,8]{2,1,0:T(2,128)}, u32[]{:S(2)}) copy-start(s32[1,2,8]{2,1,0:T(2,128)} %param.14) | copy-start | bytes 196
  0.9 26.2 %collective-permute-start = (f32[2,1,32,128]{3,2,1,0:T(8,128)S(1)}, f32[2,1,32,128]{3,2,1,0:T(8,128)S(1)}, u32[]{:S(2)}, u32[]{:S(2)}) collective-permute-start(f32[2,1,32,128]{3,2,1,0:T(8,128)S(1)} %get-tuple-element.10), channel_id=1, source_target_pairs={{0,4},{4,8},{8,12},{12,16},{16,20},{20,24},{24,28},{28,32},{32,36}... | collective-permute-start | bytes 98312 | tf_op jit(solution)/shard_map/ppermute | solution.py:17
  5.8 21.3 %collective-permute-start.1 = (f32[2,1,32,128]{3,2,1,0:T(8,128)S(1)}, f32[2,1,32,128]{3,2,1,0:T(8,128)S(1)}, u32[]{:S(2)}, u32[]{:S(2)}) collective-permute-start(f32[2,1,32,128]{3,2,1,0:T(8,128)S(1)} %get-tuple-element.9), channel_id=1, source_target_pairs={{4,0},{8,4},{12,8},{16,12},{20,16},{24,20},{28,24},{32,28},{36,32}... | collective-permute-start | bytes 98312 | tf_op jit(solution)/shard_map/ppermute | solution.py:18
  27.1 14.1 %copy-start.3 = (f32[2,18,32,128]{3,2,1,0:T(8,128)}, f32[2,18,32,128]{3,2,1,0:T(8,128)S(1)}, u32[]{:S(2)}) copy-start(f32[2,18,32,128]{3,2,1,0:T(8,128)S(1)} %constant_dynamic-update-slice_fusion) | copy-start | bytes 1769476
  27.2 737.5 %collective-permute-start.2 = (f32[2,18,1,128]{3,0,2,1:T(2,128)S(1)}, f32[2,18,1,128]{3,0,2,1:T(2,128)S(1)}, u32[]{:S(2)}, u32[]{:S(2)}) collective-permute-start(f32[2,18,1,128]{3,0,2,1:T(2,128)S(1)} %copy.91), channel_id=1, source_target_pairs={{0,1},{1,2},{2,3},{3,0},{4,5},{5,6},{6,7},{7,4},{8,9},{9,10},{10,1... | collective-permute-start | bytes 55304 | tf_op jit(solution)/shard_map/ppermute | solution.py:17
  31.6 735.7 %collective-permute-start.3 = (f32[2,18,1,128]{3,0,2,1:T(2,128)S(1)}, f32[2,18,1,128]{3,0,2,1:T(2,128)S(1)}, u32[]{:S(2)}, u32[]{:S(2)}) collective-permute-start(f32[2,18,1,128]{3,0,2,1:T(2,128)S(1)} %copy.92), channel_id=1, source_target_pairs={{1,0},{2,1},{3,2},{0,3},{5,4},{6,5},{7,6},{4,7},{9,8},{10,9},{11,1... | collective-permute-start | bytes 55304 | tf_op jit(solution)/shard_map/ppermute | solution.py:18
  816.7 3.2 copy-start.2
  850.2 6.5 copy-start.1
where the time goes:
time: 863 us; the launch traced here: 857 us
  blocking collectives  713 us (83%)
  local copies, waits for them, and re-layouts  78.8 us (9%)
  starting transfers between devices  32 us (4%)
  other arithmetic  17.8 us (2%)
  matrix products  14.3 us (2%)
    all_gather x1, blocking collectives, on_device(): coarse_full = lax.all_gather(row_values, 'group', axis=1, tiled=True)  520 us
    psum x1, blocking collectives, on_device(): whole_rhs = lax.psum(partial_rhs, ('group', 'member'))  173 us
    ppermute x2, starting transfers between devices, with_halo(): after = lax.ppermute(leading, axis, down)  22.7 us
    psum x1, blocking collectives, on_device(): row_values = lax.psum(row_terms, 'member')  19.9 us
    gather x2, local copies, waits for them, and re-layouts, build_boxes(): stacked = jnp.take(padded, jnp.asarray(upward_rows), axis=3)  18.9 us
  transfers between devices with their start and end apart: 4, of which 0 were waited for; matrix products, arithmetic and copies ran while one was open for 2% of the time, Pallas kernels for 0%

commit v1 on v0

v1 whole, which is shorter than its diff:
```python
import jax
import jax.numpy as jnp
from jax import lax
from jax.experimental import pallas as pl
from jax.experimental.pallas import tpu as pltpu
from jax.sharding import Mesh, PartitionSpec as P

SPAN = 16
EXTENT = 18
WEIGHT = float(SPAN) ** -1.5
PAIRS = 336
POINTS = 336
GROUP = ("y", "x", "low", "core")
PLANE = ("y", "x", "core")
LINE = ("high", "low")
LINE_SIZE = 32
PLANE_SIZE = 32


def iota(shape, dim):
    return lax.broadcasted_iota(jnp.int32, shape, dim)


def split(value):
    high = value.astype(jnp.bfloat16)
    low = (value - high.astype(jnp.float32)).astype(jnp.bfloat16)
    return high, low


def dot3(left, right, dims):
    (lh, ll), (rh, rl) = left, right

    def one(a, b):
        return lax.dot_general(a, b, (dims, ((), ())), preferred_element_type=jnp.float32)

    return one(lh, rh) + (one(lh, rl) + one(ll, rh))


def exact(left, right, dims=((1,), (0,))):
    return lax.dot_general(
        left, right, (dims, ((), ())),
        precision=lax.Precision.HIGHEST, preferred_element_type=jnp.float32,
    )


def point_index(shape, dim):
    row = iota(shape, dim)
    own = row < 256
    plane = row < 288
    far = row >= 312
    x_side = jnp.where(row < 272, 0, EXTENT - 1)
    x = jnp.where(own, (row >> 4) + 1, jnp.where(plane, x_side, row - jnp.where(far, 312, 288)))
    y = jnp.where(own | plane, (row & 15) + 1, jnp.where(far, EXTENT - 1, 0))
    return x, y


def pair_index(shape, dim):
    pair = iota(shape, dim)
    first = (pair * 3641) >> 16
    return first, pair - EXTENT * first


def contributions_kernel(labels_ref, residual_ref, out_ref):
    out_ref[...] = jnp.zeros_like(out_ref)
    lane = iota((2, 128), 1)
    for j in range(2):
        sums = jnp.concatenate(
            [
                jnp.sum(
                    jnp.sum(residual_ref[v, :, j * SPAN : (j + 1) * SPAN, :], axis=0),
                    axis=0,
                    keepdims=True,
                )
                for v in range(2)
            ],
            axis=0,
        )
        for k in range(8):
            total = jnp.sum(jnp.where((lane >> 4) == k, sums, 0.0), axis=1, keepdims=True)
            label = labels_ref[j * 8 + k]
            block = label >> 7
            out_ref[block] += jnp.where(lane == (label & 127), total * WEIGHT, 0.0)


def local_kernel(
    residual_ref, x_low_ref, x_high_ref, y_low_ref, y_high_ref,
    horiz_ref, horiz_values_ref, upward_ref, upward_values_ref,
    out_ref, box_ref, hat_ref, line_ref, line_values_ref,
):
    line_ref[...] = jnp.zeros_like(line_ref)
    for k in range(8):
        begin = 16 * k - 1
        skip = 1 if k == 0 else 0
        stop = 17 if k == 7 else 18
        line_ref[begin + skip : begin + stop, 18 * k : 18 * k + 18] = upward_ref[k, skip:stop, :]
        line_values_ref[0:1, 18 * k : 18 * k + 18] = upward_values_ref[k : k + 1, :]
    line = line_ref[...]
    z = iota((128, 144), 0)
    layer, _ = pair_index((128, 144), 1)
    line_own = split(jnp.where((z >> 4) == layer, line, 0.0))
    line = split(line)

    x_of, y_of = point_index((POINTS, EXTENT), 0)
    mode = iota((POINTS, EXTENT), 1)
    pair_a, pair_b = pair_index((EXTENT, PAIRS), 1)
    table = iota((EXTENT, PAIRS), 0)
    pick_a = jnp.where(pair_a == table, 1.0, 0.0)
    pick_b = jnp.where((pair_b == table) & (pair_a < EXTENT), 1.0, 0.0)
    rows_x = exact(jnp.where(x_of == mode, 1.0, 0.0), exact(horiz_ref[0], pick_a))
    rows_y = exact(jnp.where(y_of == mode, 1.0, 0.0), exact(horiz_ref[1], pick_b))
    plane = split(rows_x * rows_y)
    plane_own = (plane[0][:256], plane[1][:256])

    pair_first, pair_second = pair_index((PAIRS, EXTENT), 0)
    table = iota((PAIRS, EXTENT), 1)
    values = jnp.sum(
        jnp.where(pair_first == table, horiz_values_ref[0:1, :], 0.0)
        + jnp.where(pair_second == table, horiz_values_ref[1:2, :], 0.0),
        axis=1,
        keepdims=True,
    )
    inverse = 1.0 / (values + line_values_ref[...])

    for v in range(2):
        for j in range(2):
            lanes = slice(128 * (2 * v + j), 128 * (2 * v + j + 1))
            ys = slice(j * SPAN, (j + 1) * SPAN)
            box_ref[0:256, lanes] = residual_ref[v, :, ys, :].reshape(256, 128)
            box_ref[256:272, lanes] = x_low_ref[v, 0, ys, :]
            box_ref[272:288, lanes] = x_high_ref[v, 0, ys, :]
            box_ref[304:312, lanes] = jnp.zeros((8, 128), jnp.float32)
            box_ref[328:336, lanes] = jnp.zeros((8, 128), jnp.float32)
            for begin, edge, outer in ((288, 15, y_low_ref), (312, 16, y_high_ref)):
                if (edge == 15) == (j == 0):
                    box_ref[begin : begin + 18, lanes] = outer[v, :, 0, :]
                else:
                    box_ref[begin : begin + 1, lanes] = x_low_ref[v, 0, edge : edge + 1, :]
                    box_ref[begin + 1 : begin + 17, lanes] = residual_ref[v, :, edge, :]
                    box_ref[begin + 17 : begin + 18, lanes] = x_high_ref[v, 0, edge : edge + 1, :]

    hat_ref[...] = dot3(plane, split(box_ref[...]), ((0,), (0,)))
    for part in range(4):
        lanes = slice(128 * part, 128 * (part + 1))
        hat = dot3(split(hat_ref[:, lanes]), line, ((1,), (0,)))
        back = dot3(split(hat * inverse), line_own, ((1,), (1,)))
        solved = dot3(plane_own, split(back), ((1,), (0,)))
        v, j = divmod(part, 2)
        out_ref[v, :, j * SPAN : (j + 1) * SPAN, :] = solved.reshape(SPAN, SPAN, 128)


def merge_kernel(labels_ref, local_ref, coarse_ref, out_ref):
    lane = iota((2, 128), 1)
    for j in range(2):
        update = jnp.zeros((2, 128), jnp.float32)
        for k in range(8):
            label = labels_ref[j * 8 + k]
            block = ((label >> 8) << 1) | ((label >> 4) & 1)
            place = (((label >> 5) & 7) << 4) | (label & 15)
            value = jnp.sum(
                jnp.where(lane == place, coarse_ref[block], 0.0), axis=1, keepdims=True
            )
            update = update + jnp.where((lane >> 4) == k, value * WEIGHT, 0.0)
        ys = slice(j * SPAN, (j + 1) * SPAN)
        for v in range(2):
            out_ref[v, :, ys, :] = local_ref[v, :, ys, :] + update[v : v + 1][None]


def call(kernel, out_shape, scalars, arrays, scratch=()):
    return pl.pallas_call(
        kernel,
        out_shape=jax.ShapeDtypeStruct(out_shape, jnp.float32),
        in_specs=[pl.BlockSpec(memory_space=pltpu.SMEM)] * len(scalars)
        + [pl.BlockSpec(memory_space=pltpu.VMEM)] * len(arrays),
        out_specs=pl.BlockSpec(memory_space=pltpu.VMEM),
        scratch_shapes=list(scratch),
        compiler_params=pltpu.CompilerParams(vmem_limit_bytes=40 << 20),
    )(*scalars, *arrays)


def neighbours(axis, size, low_side, high_side):
    up = [(i, (i + 1) % size) for i in range(size)]
    down = [(j, i) for i, j in up]
    return lax.ppermute(high_side, axis, up), lax.ppermute(low_side, axis, down)


def to_all(value, axes, size):
    copies = jnp.broadcast_to(value[None], (size,) + value.shape)
    return lax.all_to_all(copies, axes, 0, 0)


def on_device(
    residual, horiz_vectors, horiz_values, upward_eigen_tables, upward_eigen_values,
    aggregate_map, coarse_inverse,
):
    labels = aggregate_map.reshape(16)

    x_low, x_high = neighbours(GROUP, 256, residual[:, :1], residual[:, -1:])
    low_side = jnp.concatenate([x_low[:, :, :1], residual[:, :, :1], x_high[:, :, :1]], axis=1)
    high_side = jnp.concatenate([x_low[:, :, -1:], residual[:, :, -1:], x_high[:, :, -1:]], axis=1)
    y_low, y_high = neighbours("high", 4, low_side, high_side)

    tiles = jnp.swapaxes(coarse_inverse.reshape(16, 8, 128), 0, 1)
    tile = lax.all_to_all(tiles, "low", 0, 0).reshape(128, 128)

    parts = call(contributions_kernel, (LINE_SIZE, 2, 128), [labels], [residual])
    line_sum = lax.all_to_all(parts, LINE, 0, 0).sum(axis=0)
    rhs = to_all(line_sum, PLANE, PLANE_SIZE).sum(axis=0)
    terms = lax.dot_general(
        rhs, tile, (((1,), (1,)), ((), ())),
        precision=lax.Precision.HIGHEST, preferred_element_type=jnp.float32,
    )
    rows = to_all(terms, LINE, LINE_SIZE).sum(axis=0)
    coarse = to_all(rows, PLANE, PLANE_SIZE)

    local = call(
        local_kernel, residual.shape, [],
        [residual, x_low, x_high, y_low, y_high, horiz_vectors, horiz_values,
         upward_eigen_tables, upward_eigen_values],
        [pltpu.VMEM((POINTS, 512), jnp.float32), pltpu.VMEM((PAIRS, 512), jnp.float32),
         pltpu.VMEM((128, 144), jnp.float32), pltpu.VMEM((1, 144), jnp.float32)],
    )
    return call(merge_kernel, residual.shape, [labels], [local, coarse])


def solution(mesh):
    fine = Mesh(mesh.devices.reshape(4, 4, 8, 2, 4), ("y", "x", "low", "core", "high"))
    in_specs = (
        P(None, GROUP, "high", None),
        P(), P(), P(), P(),
        P(GROUP, "high", None),
        P(GROUP, "high"),
    )
    return jax.shard_map(
        on_device, mesh=fine, in_specs=in_specs, out_specs=in_specs[0], check_vma=False
    )
```

time: 863 us -> 150 us (0.17)
  blocking collectives: 713 us -> 51 us
  local copies, waits for them, and re-layouts: 78.8 us -> 4.48 us
  waiting for transfers between devices: 0.01 us -> 33.2 us
  starting transfers between devices: 32 us -> 52.1 us
  other arithmetic: 17.8 us -> 0.17 us
  matrix products: 14.3 us -> 0.17 us
    all_gather x1 -> x0, blocking collectives: 520 us -> none  [on_device(): coarse_full = lax.all_gather(row_values, 'group', axis=1, tiled=True)]
    psum x2 -> x0, blocking collectives: 193 us -> none  [the longest x1 173 us: on_device(): whole_rhs = lax.psum(partial_rhs, ('group', 'member'))]
    all_to_all x0 -> x1, blocking collectives: none -> 51 us  [on_device(): line_sum = lax.all_to_all(parts, LINE, 0, 0).sum(axis=0)]
    all_to_all x0 -> x4, starting transfers between devices: none -> 32.3 us  [the longest x3 29 us: to_all(): return lax.all_to_all(copies, axes, 0, 0)]
    gather x7 -> x0, local copies, waits for them, and re-layouts: 27.8 us -> none  [the longest x2 18.9 us: build_boxes(): stacked = jnp.take(padded, jnp.asarray(upward_rows), axis=3)]
    reshape x7 -> x1, local copies, waits for them, and re-layouts: 28 us -> 0.76 us  [on_device(): labels = aggregate_map.reshape(16)]
    all_to_all x0 -> x4, waiting for transfers between devices: none -> 21.1 us  [the longest x3 17.2 us: to_all(): return lax.all_to_all(copies, axes, 0, 0)]
    dot_general x7 -> x1, matrix products: 14.3 us -> 0.17 us  [on_device(): lax.dot_general(rhs, tile, (((1,), (1,)), ((), ())), precision=lax.Precis...]
  transfers between devices with their start and end apart: 4 -> 8, of which waited for: 0 -> 4; matrix products, arithmetic and copies ran while one was open for 2% -> 2% of each run, Pallas kernels for 0% -> 3%
where the time goes in v1:
time: 150 us; the launch traced here: 149 us
  starting transfers between devices  52.1 us (35%)
  blocking collectives  51 us (34%)
  waiting for transfers between devices  33.2 us (22%)
  Pallas kernels  7.38 us (5%)
  local copies, waits for them, and re-layouts  4.48 us (3%)
    all_to_all x1, blocking collectives, on_device(): line_sum = lax.all_to_all(parts, LINE, 0, 0).sum(axis=0)  51 us
    all_to_all x3, starting transfers between devices, to_all(): return lax.all_to_all(copies, axes, 0, 0)  29 us
    all_to_all x3, waiting for transfers between devices, to_all(): return lax.all_to_all(copies, axes, 0, 0)  17.2 us
    ppermute x2, starting transfers between devices, neighbours(): lax.ppermute(high_side, axis, up)  15.3 us
    ppermute x2, waiting for transfers between devices, neighbours(): lax.ppermute(low_side, axis, down)  12.1 us
    pallas_call x3, Pallas kernels, call(): pl.pallas_call(kernel, out_shape=jax.ShapeDtypeStruct(out_shape, jnp.floa...  7.38 us
    ppermute x2, starting transfers between devices, neighbours(): lax.ppermute(low_side, axis, down)  4.54 us
    all_to_all x1, waiting for transfers between devices, on_device(): tile = lax.all_to_all(tiles, 'low', 0, 0).reshape(128, 128)  3.91 us
  transfers between devices with their start and end apart: 8, of which 4 were waited for; matrix products, arithmetic and copies ran while one was open for 2% of the time, Pallas kernels for 3%

profile of v1, /device:TPU:1, one launch (start us, length us, event | category | flops | bytes accessed | tf_op | source)
XLA Modules:
  0.0 148.8 jit_solution(7499820790953353753)
XLA Ops:
  0.0 0.8 reshape.12.labels_ref
  0.8 1.0 copy-done
  1.8 0.7 shard_map.74
  2.5 51.0 %all_to_all.25 = f32[32,2,128]{2,1,0:T(2,128)S(1)} all-to-all(f32[32,2,128]{2,1,0:T(2,128)S(1)} %shard_map.74), channel_id=1, replica_groups=mesh['y'=4,'x'=4,'low'=8,'core'=2,'high'=4] {'high','low'}, dimensions={0} | all-to-all | bytes 65536 | tf_op jit(solution)/shard_map/all_to_all | solution.py:206
  53.5 0.6 broadcast_in_dim.6
  54.2 9.3 %all-to-all-start.1 = ((f32[32,2,128]{2,1,0:T(2,128)}), f32[32,2,128]{2,1,0:T(2,128)S(1)}, u32[]{:S(2)}, u32[]{:S(2)}) async-start(f32[32,2,128]{2,1,0:T(2,128)} %broadcast_in_dim.6), calls=%async_computation.1 | async-start | bytes 65536 | tf_op jit(solution)/shard_map/all_to_all | solution.py:188
  63.5 0.6 copy.24
  64.1 6.6 %all-to-all-done.1 = f32[32,2,128]{2,1,0:T(2,128)S(1)} async-done(((f32[32,2,128]{2,1,0:T(2,128)}), f32[32,2,128]{2,1,0:T(2,128)S(1)}, u32[]{:S(2)}, u32[]{:S(2)}) %all-to-all-start.1) | async-done | bytes 32800 | tf_op jit(solution)/shard_map/all_to_all | solution.py:188
  70.7 3.4 %all-to-all-start.2 = ((f32[8,16,128]{2,1,0:T(8,128)}), f32[8,16,128]{2,1,0:T(8,128)S(1)}, u32[]{:S(2)}, u32[]{:S(2)}) async-start(f32[8,16,128]{2,1,0:T(8,128)} %copy.24), calls=%async_computation.2 | async-start | bytes 131072 | tf_op jit(solution)/shard_map/all_to_all | solution.py:203
  74.1 2.3 %collective-permute-start.1 = (f32[2,1,32,128]{3,2,1,0:T(8,128)S(1)}, f32[2,1,32,128]{3,2,1,0:T(8,128)S(1)}, u32[]{:S(2)}, u32[]{:S(2)}) collective-permute-start(f32[2,1,32,128]{3,2,1,0:T(8,128)S(1)} %get-tuple-element.7), channel_id=1, source_target_pairs={{4,0},{8,4},{12,8},{16,12},{20,16},{24,20},{28,24},{32,28},{36,32}... | collective-permute-start | bytes 98312 | tf_op jit(solution)/shard_map/ppermute | solution.py:183
  76.4 3.4 %collective-permute-start = (f32[2,1,32,128]{3,2,1,0:T(8,128)S(1)}, f32[2,1,32,128]{3,2,1,0:T(8,128)S(1)}, u32[]{:S(2)}, u32[]{:S(2)}) collective-permute-start(f32[2,1,32,128]{3,2,1,0:T(8,128)S(1)} %get-tuple-element.8), channel_id=1, source_target_pairs={{0,4},{4,8},{8,12},{12,16},{16,20},{20,24},{24,28},{28,32},{32,36}... | collective-permute-start | bytes 98312 | tf_op jit(solution)/shard_map/ppermute | solution.py:183
  80.0 3.9 %all-to-all-done.2 = f32[8,16,128]{2,1,0:T(8,128)S(1)} async-done(((f32[8,16,128]{2,1,0:T(8,128)}), f32[8,16,128]{2,1,0:T(8,128)S(1)}, u32[]{:S(2)}, u32[]{:S(2)}) %all-to-all-start.2) | async-done | bytes 65568 | tf_op jit(solution)/shard_map/all_to_all | solution.py:203
  83.9 0.2 fusion.4
  84.0 0.7 broadcast_in_dim.7
  84.7 13.1 %all-to-all-start.3 = ((f32[32,2,128]{2,1,0:T(2,128)}), f32[32,2,128]{2,1,0:T(2,128)S(1)}, u32[]{:S(2)}, u32[]{:S(2)}) async-start(f32[32,2,128]{2,1,0:T(2,128)} %broadcast_in_dim.7), calls=%async_computation.3 | async-start | bytes 65536 | tf_op jit(solution)/shard_map/all_to_all | solution.py:188
  97.9 11.9 %collective-permute-start.2 = (f32[2,18,1,128]{3,2,1,0:T(1,128)S(1)}, f32[2,18,1,128]{3,2,1,0:T(1,128)S(1)}, u32[]{:S(2)}, u32[]{:S(2)}) collective-permute-start(f32[2,18,1,128]{3,2,1,0:T(1,128)S(1)} %pad_maximum_fusion), channel_id=1, source_target_pairs={{0,1},{1,2},{2,3},{3,0},{4,5},{5,6},{6,7},{7,4},{8,9},{9,10},{10,1... | collective-permute-start | bytes 55304 | tf_op jit(solution)/shard_map/ppermute | solution.py:183
  109.7 10.6 %all-to-all-done.3 = f32[32,2,128]{2,1,0:T(2,128)S(1)} async-done(((f32[32,2,128]{2,1,0:T(2,128)}), f32[32,2,128]{2,1,0:T(2,128)S(1)}, u32[]{:S(2)}, u32[]{:S(2)}) %all-to-all-start.3) | async-done | bytes 32800 | tf_op jit(solution)/shard_map/all_to_all | solution.py:188
  120.3 0.6 broadcast_in_dim.8
  121.0 6.6 %all-to-all-start.4 = ((f32[32,2,128]{2,1,0:T(2,128)}), f32[32,2,128]{2,1,0:T(2,128)S(1)}, u32[]{:S(2)}, u32[]{:S(2)}) async-start(f32[32,2,128]{2,1,0:T(2,128)} %broadcast_in_dim.8), calls=%async_computation.4 | async-start | bytes 65536 | tf_op jit(solution)/shard_map/all_to_all | solution.py:188
  127.6 0.0 copy-start.6
  127.6 2.2 %collective-permute-start.3 = (f32[2,18,1,128]{3,2,1,0:T(1,128)S(1)}, f32[2,18,1,128]{3,2,1,0:T(1,128)S(1)}, u32[]{:S(2)}, u32[]{:S(2)}) collective-permute-start(f32[2,18,1,128]{3,2,1,0:T(1,128)S(1)} %pad_maximum_fusion.1), channel_id=1, source_target_pairs={{1,0},{2,1},{3,2},{0,3},{5,4},{6,5},{7,6},{4,7},{9,8},{10,9},{11,1... | collective-permute-start | bytes 55304 | tf_op jit(solution)/shard_map/ppermute | solution.py:183
  130.0 12.1 %collective-permute-done.3.y_high_ref = f32[2,18,1,128]{3,2,1,0:T(1,128)S(1)} collective-permute-done((f32[2,18,1,128]{3,2,1,0:T(1,128)S(1)}, f32[2,18,1,128]{3,2,1,0:T(1,128)S(1)}, u32[]{:S(2)}, u32[]{:S(2)}) %collective-permute-start.3) | collective-permute-done | bytes 18464 | tf_op jit(solution)/shard_map/ppermute | solution.py:183
  142.1 5.2 %shard_map.73.local_ref = f32[2,16,32,128]{3,2,1,0:T(8,128)S(1)} custom-call(f32[2,16,32,128]{3,2,1,0:T(8,128)S(1)} %copy-done.1, f32[2,1,32,128]{3,2,1,0:T(8,128)S(1)} %collective-permute-done.x_low_ref, f32[2,1,32,128]{3,2,1,0:T(8,128)S(1)} %collective-permute-done.1.x_high_ref, f32[2,18,1,128]{3,2,1,0:T(1,128)S(1)} %collective-permute-done.2.y_low_ref, ...), custom_call_target="tpu_custom_call" | custom-call | tf_op jit(solution)/shard_map/pallas_call | solution.py:169
  147.3 1.5 %shard_map.75 = f32[2,16,32,128]{3,2,1,0:T(8,128)} custom-call(s32[16]{0:T(128)S(1)} %reshape.12.labels_ref, f32[2,16,32,128]{3,2,1,0:T(8,128)S(1)} %shard_map.73.local_ref, f32[32,2,128]{2,1,0:T(2,128)S(1)} %all-to-all-done.4.coarse_ref), custom_call_target="tpu_custom_call" | custom-call | tf_op jit(solution)/shard_map/pallas_call | solution.py:169
  (28 shorter events, 0.3 us)
Async XLA Ops:
  0.8 1.0 copy-start
  1.8 72.3 %copy-start.1 = (f32[2,16,32,128]{3,2,1,0:T(8,128)S(1)}, f32[2,16,32,128]{3,2,1,0:T(8,128)}, u32[]{:S(2)}) copy-start(f32[2,16,32,128]{3,2,1,0:T(8,128)} %residual_ref.3) | copy-start | bytes 1572868
  53.5 10.0 %copy-start.5 = (f32[16,1024]{1,0:T(8,128)S(1)}, f32[16,1024]{1,0:T(8,128)}, u32[]{:S(2)}) copy-start(f32[16,1024]{1,0:T(8,128)} %param.13) | copy-start | bytes 196612
  54.2 16.5 %all-to-all-start.1 = ((f32[32,2,128]{2,1,0:T(2,128)}), f32[32,2,128]{2,1,0:T(2,128)S(1)}, u32[]{:S(2)}, u32[]{:S(2)}) async-start(f32[32,2,128]{2,1,0:T(2,128)} %broadcast_in_dim.6), calls=%async_computation.1 | async-start | bytes 65536 | tf_op jit(solution)/shard_map/all_to_all | solution.py:188
  70.7 13.1 %all-to-all-start.2 = ((f32[8,16,128]{2,1,0:T(8,128)}), f32[8,16,128]{2,1,0:T(8,128)S(1)}, u32[]{:S(2)}, u32[]{:S(2)}) async-start(f32[8,16,128]{2,1,0:T(8,128)} %copy.24), calls=%async_computation.2 | async-start | bytes 131072 | tf_op jit(solution)/shard_map/all_to_all | solution.py:203
  74.1 5.8 %collective-permute-start.1 = (f32[2,1,32,128]{3,2,1,0:T(8,128)S(1)}, f32[2,1,32,128]{3,2,1,0:T(8,128)S(1)}, u32[]{:S(2)}, u32[]{:S(2)}) collective-permute-start(f32[2,1,32,128]{3,2,1,0:T(8,128)S(1)} %get-tuple-element.7), channel_id=1, source_target_pairs={{4,0},{8,4},{12,8},{16,12},{20,16},{24,20},{28,24},{32,28},{36,32}... | collective-permute-start | bytes 98312 | tf_op jit(solution)/shard_map/ppermute | solution.py:183
  76.4 21.4 %collective-permute-start = (f32[2,1,32,128]{3,2,1,0:T(8,128)S(1)}, f32[2,1,32,128]{3,2,1,0:T(8,128)S(1)}, u32[]{:S(2)}, u32[]{:S(2)}) collective-permute-start(f32[2,1,32,128]{3,2,1,0:T(8,128)S(1)} %get-tuple-element.8), channel_id=1, source_target_pairs={{0,4},{4,8},{8,12},{12,16},{16,20},{20,24},{24,28},{28,32},{32,36}... | collective-permute-start | bytes 98312 | tf_op jit(solution)/shard_map/ppermute | solution.py:183
  84.7 35.6 %all-to-all-start.3 = ((f32[32,2,128]{2,1,0:T(2,128)}), f32[32,2,128]{2,1,0:T(2,128)S(1)}, u32[]{:S(2)}, u32[]{:S(2)}) async-start(f32[32,2,128]{2,1,0:T(2,128)} %broadcast_in_dim.7), calls=%async_computation.3 | async-start | bytes 65536 | tf_op jit(solution)/shard_map/all_to_all | solution.py:188
  97.9 32.1 %collective-permute-start.2 = (f32[2,18,1,128]{3,2,1,0:T(1,128)S(1)}, f32[2,18,1,128]{3,2,1,0:T(1,128)S(1)}, u32[]{:S(2)}, u32[]{:S(2)}) collective-permute-start(f32[2,18,1,128]{3,2,1,0:T(1,128)S(1)} %pad_maximum_fusion), channel_id=1, source_target_pairs={{0,1},{1,2},{2,3},{3,0},{4,5},{5,6},{6,7},{7,4},{8,9},{9,10},{10,1... | collective-permute-start | bytes 55304 | tf_op jit(solution)/shard_map/ppermute | solution.py:183
  121.0 8.9 %copy-start.4 = (f32[8,18,18]{2,0,1:T(8,128)S(1)}, f32[8,18,18]{2,0,1:T(8,128)}, u32[]{:S(2)}) copy-start(f32[8,18,18]{2,0,1:T(8,128)} %param.10) | copy-start | bytes 31108
  121.0 26.3 %all-to-all-start.4 = ((f32[32,2,128]{2,1,0:T(2,128)}), f32[32,2,128]{2,1,0:T(2,128)S(1)}, u32[]{:S(2)}, u32[]{:S(2)}) async-start(f32[32,2,128]{2,1,0:T(2,128)} %broadcast_in_dim.8), calls=%async_computation.4 | async-start | bytes 65536 | tf_op jit(solution)/shard_map/all_to_all | solution.py:188
  127.6 2.3 %copy-start.6 = (f32[2,18,18]{2,0,1:T(2,128)S(1)}, f32[2,18,18]{2,0,1:T(2,128)}, u32[]{:S(2)}) copy-start(f32[2,18,18]{2,0,1:T(2,128)} %param.8) | copy-start | bytes 7780
  127.6 14.4 %collective-permute-start.3 = (f32[2,18,1,128]{3,2,1,0:T(1,128)S(1)}, f32[2,18,1,128]{3,2,1,0:T(1,128)S(1)}, u32[]{:S(2)}, u32[]{:S(2)}) collective-permute-start(f32[2,18,1,128]{3,2,1,0:T(1,128)S(1)} %pad_maximum_fusion.1), channel_id=1, source_target_pairs={{1,0},{2,1},{3,2},{0,3},{5,4},{6,5},{7,6},{4,7},{9,8},{10,9},{11,1... | collective-permute-start | bytes 55304 | tf_op jit(solution)/shard_map/ppermute | solution.py:183
  129.9 12.2 %copy-start.2 = (f32[8,18]{1,0:T(8,128)S(1)}, f32[8,18]{1,0:T(8,128)}, u32[]{:S(2)}) copy-start(f32[8,18]{1,0:T(8,128)} %upward_values_ref.1) | copy-start | bytes 1732
  129.9 12.2 %copy-start.3 = (f32[2,18]{1,0:T(2,128)S(1)}, f32[2,18]{1,0:T(2,128)}, u32[]{:S(2)}) copy-start(f32[2,18]{1,0:T(2,128)} %horiz_values_ref.1) | copy-start | bytes 436

commit v2 on v1

--- a/solution.py
+++ b/solution.py
@@ -77,9 +77,31 @@
         )
         for k in range(8):
             total = jnp.sum(jnp.where((lane >> 4) == k, sums, 0.0), axis=1, keepdims=True)
-            label = labels_ref[j * 8 + k]
+            label = labels_ref[0, j, k]
             block = label >> 7
             out_ref[block] += jnp.where(lane == (label & 127), total * WEIGHT, 0.0)
+
+
+def tiles_kernel(place_ref, matrix_ref, *out_refs):
+    for flip, out_ref in enumerate(out_refs):
+        begin = pl.multiple_of((place_ref[0] ^ flip) * 128, 128)
+        out_ref[...] = matrix_ref[:, pl.ds(begin, 128)]
+
+
+def terms_kernel(place_ref, parts_ref, *refs):
+    tile_refs, out_ref = refs[:8], refs[8]
+    tile = jnp.concatenate([ref[...] for ref in tile_refs], axis=0)
+    rhs = jnp.sum(parts_ref[...], axis=0)
+    rhs = jnp.concatenate([rhs, jnp.zeros((6, 128), jnp.float32)], axis=0)
+    terms = exact(rhs, tile, ((1,), (1,)))
+    lane = iota((8, 128), 1)
+    for bit in range(3):
+        width = SPAN << bit
+        other = jnp.where(
+            (lane & width) != 0, pltpu.roll(terms, width, 1), pltpu.roll(terms, 128 - width, 1)
+        )
+        terms = jnp.where(((place_ref[0] >> bit) & 1) != 0, other, terms)
+    out_ref[...] = jnp.broadcast_to(terms[:2][None], out_ref.shape)
 
 
 def local_kernel(
@@ -153,7 +175,7 @@
     for j in range(2):
         update = jnp.zeros((2, 128), jnp.float32)
         for k in range(8):
-            label = labels_ref[j * 8 + k]
+            label = labels_ref[0, j, k]
             block = ((label >> 8) << 1) | ((label >> 4) & 1)
             place = (((label >> 5) & 7) << 4) | (label & 15)
             value = jnp.sum(
@@ -188,30 +210,40 @@
     return lax.all_to_all(copies, axes, 0, 0)
 
 
+def regroup(place, matrix):
+    tiles = pl.pallas_call(
+        tiles_kernel,
+        out_shape=[jax.ShapeDtypeStruct((16, 128), jnp.float32)] * 8,
+        in_specs=[pl.BlockSpec(memory_space=pltpu.SMEM), pl.BlockSpec(memory_space=pltpu.VMEM)],
+        out_specs=[pl.BlockSpec(memory_space=pltpu.VMEM)] * 8,
+    )(place, matrix)
+    return [tiles[0]] + [
+        lax.ppermute(tiles[flip], "low", [(i, i ^ flip) for i in range(8)]) for flip in range(1, 8)
+    ]
+
+
 def on_device(
     residual, horiz_vectors, horiz_values, upward_eigen_tables, upward_eigen_values,
     aggregate_map, coarse_inverse,
 ):
-    labels = aggregate_map.reshape(16)
-
-    x_low, x_high = neighbours(GROUP, 256, residual[:, :1], residual[:, -1:])
+    labels = aggregate_map
+    place = lax.axis_index("low").reshape(1)
+
+    parts = call(contributions_kernel, (LINE_SIZE, 2, 128), [labels], [residual])
+    sides = (parts, residual[:, :1], residual[:, -1:], coarse_inverse)
+    parts, low_side, high_side, matrix = lax.optimization_barrier(sides)
+    line_parts = lax.all_to_all(parts, LINE, 0, 0)
+    x_low, x_high = neighbours(GROUP, 256, low_side, high_side)
+    tiles = regroup(place, matrix)
+    line_parts, x_low, x_high, tiles = lax.optimization_barrier((line_parts, x_low, x_high, tiles))
+
+    plane_parts = to_all(line_parts.sum(axis=0), PLANE, PLANE_SIZE)
+    plane_parts, x_low, x_high = lax.optimization_barrier((plane_parts, x_low, x_high))
+    terms = call(terms_kernel, (LINE_SIZE, 2, 128), [place], [plane_parts] + tiles)
+    row_parts = lax.all_to_all(terms, LINE, 0, 0)
     low_side = jnp.concatenate([x_low[:, :, :1], residual[:, :, :1], x_high[:, :, :1]], axis=1)
     high_side = jnp.concatenate([x_low[:, :, -1:], residual[:, :, -1:], x_high[:, :, -1:]], axis=1)
     y_low, y_high = neighbours("high", 4, low_side, high_side)
-
-    tiles = jnp.swapaxes(coarse_inverse.reshape(16, 8, 128), 0, 1)
-    tile = lax.all_to_all(tiles, "low", 0, 0).reshape(128, 128)
-
-    parts = call(contributions_kernel, (LINE_SIZE, 2, 128), [labels], [residual])
-    line_sum = lax.all_to_all(parts, LINE, 0, 0).sum(axis=0)
-    rhs = to_all(line_sum, PLANE, PLANE_SIZE).sum(axis=0)
-    terms = lax.dot_general(
-        rhs, tile, (((1,), (1,)), ((), ())),
-        precision=lax.Precision.HIGHEST, preferred_element_type=jnp.float32,
-    )
-    rows = to_all(terms, LINE, LINE_SIZE).sum(axis=0)
-    coarse = to_all(rows, PLANE, PLANE_SIZE)
-
     local = call(
         local_kernel, residual.shape, [],
         [residual, x_low, x_high, y_low, y_high, horiz_vectors, horiz_values,
@@ -219,6 +251,8 @@
         [pltpu.VMEM((POINTS, 512), jnp.float32), pltpu.VMEM((PAIRS, 512), jnp.float32),
          pltpu.VMEM((128, 144), jnp.float32), pltpu.VMEM((1, 144), jnp.float32)],
     )
+    row_parts, local = lax.optimization_barrier((row_parts, local))
+    coarse = to_all(row_parts.sum(axis=0), PLANE, PLANE_SIZE)
     return call(merge_kernel, residual.shape, [labels], [local, coarse])
 
 

time: 150 us -> 165 us (1.10)
  starting transfers between devices: 52.1 us -> 112 us
  blocking collectives: 51 us -> 12.7 us
  waiting for transfers between devices: 33.2 us -> 25.7 us
  Pallas kernels: 7.38 us -> 10.5 us
  local copies, waits for them, and re-layouts: 4.48 us -> 2.56 us
    all_to_all x1 -> x2, starting transfers between devices: 3.35 us -> 50.5 us  [the longest x1 29.3 us: on_device(): line_parts = lax.all_to_all(parts, LINE, 0, 0)]
    all_to_all x1, blocking collectives: 51 us -> 12.7 us  [to_all(): return lax.all_to_all(copies, axes, 0, 0)]
    ppermute x0 -> x7, starting transfers between devices: none -> 30.5 us  [regroup(): lax.ppermute(tiles[flip], 'low', [(i, i ^ flip) for i in range(8)])]
    all_to_all x3 -> x1, starting transfers between devices: 29 us -> 10.9 us  [to_all(): return lax.all_to_all(copies, axes, 0, 0)]
    all_to_all x3 -> x1, waiting for transfers between devices: 17.2 us -> 7.2 us  [to_all(): return lax.all_to_all(copies, axes, 0, 0)]
    ppermute x0 -> x7, waiting for transfers between devices: none -> 7.54 us  [regroup(): lax.ppermute(tiles[flip], 'low', [(i, i ^ flip) for i in range(8)])]
    all_to_all x1 -> x2, waiting for transfers between devices: 3.91 us -> 0.01 us  [the longest x1 0.01 us: on_device(): line_parts = lax.all_to_all(parts, LINE, 0, 0)]
    pallas_call x3 -> x4, Pallas kernels: 7.38 us -> 9.06 us  [call(): pl.pallas_call(kernel, out_shape=jax.ShapeDtypeStruct(out_shape, jnp.floa...]
  transfers between devices with their start and end apart: 8 -> 14, of which waited for: 4 -> 3; matrix products, arithmetic and copies ran while one was open for 2% -> 0% of each run, Pallas kernels for 3% -> 4%
where the time goes in v2:
time: 165 us; the launch traced here: 164 us
  starting transfers between devices  112 us (68%)
  waiting for transfers between devices  25.7 us (16%)
  blocking collectives  12.7 us (8%)
  Pallas kernels  10.5 us (6%)
  local copies, waits for them, and re-layouts  2.56 us (2%)
    ppermute x7, starting transfers between devices, regroup(): lax.ppermute(tiles[flip], 'low', [(i, i ^ flip) for i in range(8)])  30.5 us
    all_to_all x1, starting transfers between devices, on_device(): line_parts = lax.all_to_all(parts, LINE, 0, 0)  29.3 us
    all_to_all x1, starting transfers between devices, on_device(): row_parts = lax.all_to_all(terms, LINE, 0, 0)  21.2 us
    ppermute x2, starting transfers between devices, neighbours(): lax.ppermute(high_side, axis, up)  16.1 us
    all_to_all x1, blocking collectives, to_all(): return lax.all_to_all(copies, axes, 0, 0)  12.7 us
    ppermute x2, waiting for transfers between devices, neighbours(): lax.ppermute(low_side, axis, down)  11 us
    all_to_all x1, starting transfers between devices, to_all(): return lax.all_to_all(copies, axes, 0, 0)  10.9 us
    pallas_call x4, Pallas kernels, call(): pl.pallas_call(kernel, out_shape=jax.ShapeDtypeStruct(out_shape, jnp.floa...  9.06 us
  transfers between devices with their start and end apart: 14, of which 3 were waited for; matrix products, arithmetic and copies ran while one was open for 0% of the time, Pallas kernels for 4%

profile of v2, /device:TPU:1, one launch (start us, length us, event | category | flops | bytes accessed | tf_op | source)
XLA Modules:
  0.0 164.1 jit_solution(365456790027360832)
XLA Ops:
  0.8 1.0 copy-done
  1.8 1.3 shard_map.73
  3.2 29.3 %all-to-all-start = ((f32[32,2,128]{2,1,0:T(2,128)}), f32[32,2,128]{2,1,0:T(2,128)S(1)}, u32[]{:S(2)}, u32[]{:S(2)}) async-start(f32[32,2,128]{2,1,0:T(2,128)} %shard_map.73), calls=%async_computation | async-start | bytes 65536 | tf_op jit(solution)/shard_map/all_to_all | solution.py:235
  32.5 4.3 %collective-permute-start = (f32[2,1,32,128]{3,2,1,0:T(8,128)S(1)}, f32[2,1,32,128]{3,2,1,0:T(8,128)S(1)}, u32[]{:S(2)}, u32[]{:S(2)}) collective-permute-start(f32[2,1,32,128]{3,2,1,0:T(8,128)S(1)} %get-tuple-element.34), channel_id=1, source_target_pairs={{0,4},{4,8},{8,12},{12,16},{16,20},{20,24},{24,28},{28,32},{32,36}... | collective-permute-start | bytes 98312 | tf_op jit(solution)/shard_map/ppermute | solution.py:205
  36.7 1.9 %collective-permute-start.1 = (f32[2,1,32,128]{3,2,1,0:T(8,128)S(1)}, f32[2,1,32,128]{3,2,1,0:T(8,128)S(1)}, u32[]{:S(2)}, u32[]{:S(2)}) collective-permute-start(f32[2,1,32,128]{3,2,1,0:T(8,128)S(1)} %get-tuple-element.35), channel_id=1, source_target_pairs={{4,0},{8,4},{12,8},{16,12},{20,16},{24,20},{28,24},{32,28},{36,32}... | collective-permute-start | bytes 98312 | tf_op jit(solution)/shard_map/ppermute | solution.py:205
  38.7 1.5 shard_map.74
  40.1 3.2 %collective-permute-start.2 = (f32[16,128]{1,0:T(8,128)}, f32[16,128]{1,0:T(8,128)S(1)}, u32[]{:S(2)}, u32[]{:S(2)}) collective-permute-start(f32[16,128]{1,0:T(8,128)} %get-tuple-element.38), channel_id=1, source_target_pairs={{0,8},{8,0},{16,24},{24,16},{32,40},{40,32},{48,56},{56,48},{1,9},... | collective-permute-start | bytes 24584 | tf_op jit(solution)/shard_map/ppermute | solution.py:221
  43.4 5.2 %collective-permute-start.3 = (f32[16,128]{1,0:T(8,128)}, f32[16,128]{1,0:T(8,128)S(1)}, u32[]{:S(2)}, u32[]{:S(2)}) collective-permute-start(f32[16,128]{1,0:T(8,128)} %get-tuple-element.39), channel_id=1, source_target_pairs={{0,16},{8,24},{16,0},{24,8},{32,48},{40,56},{48,32},{56,40},{1,17}... | collective-permute-start | bytes 24584 | tf_op jit(solution)/shard_map/ppermute | solution.py:221
  48.6 1.9 %collective-permute-start.4 = (f32[16,128]{1,0:T(8,128)}, f32[16,128]{1,0:T(8,128)S(1)}, u32[]{:S(2)}, u32[]{:S(2)}) collective-permute-start(f32[16,128]{1,0:T(8,128)} %get-tuple-element.40), channel_id=1, source_target_pairs={{0,24},{8,16},{16,8},{24,0},{32,56},{40,48},{48,40},{56,32},{1,25}... | collective-permute-start | bytes 24584 | tf_op jit(solution)/shard_map/ppermute | solution.py:221
  50.5 6.1 %collective-permute-start.5 = (f32[16,128]{1,0:T(8,128)}, f32[16,128]{1,0:T(8,128)S(1)}, u32[]{:S(2)}, u32[]{:S(2)}) collective-permute-start(f32[16,128]{1,0:T(8,128)} %get-tuple-element.41), channel_id=1, source_target_pairs={{0,32},{8,40},{16,48},{24,56},{32,0},{40,8},{48,16},{56,24},{1,33}... | collective-permute-start | bytes 24584 | tf_op jit(solution)/shard_map/ppermute | solution.py:221
  56.6 3.1 %collective-permute-start.6 = (f32[16,128]{1,0:T(8,128)}, f32[16,128]{1,0:T(8,128)S(1)}, u32[]{:S(2)}, u32[]{:S(2)}) collective-permute-start(f32[16,128]{1,0:T(8,128)} %get-tuple-element.42), channel_id=1, source_target_pairs={{0,40},{8,32},{16,56},{24,48},{32,8},{40,0},{48,24},{56,16},{1,41}... | collective-permute-start | bytes 24584 | tf_op jit(solution)/shard_map/ppermute | solution.py:221
  59.7 7.5 %collective-permute-start.7 = (f32[16,128]{1,0:T(8,128)}, f32[16,128]{1,0:T(8,128)S(1)}, u32[]{:S(2)}, u32[]{:S(2)}) collective-permute-start(f32[16,128]{1,0:T(8,128)} %get-tuple-element.43), channel_id=1, source_target_pairs={{0,48},{8,56},{16,32},{24,40},{32,16},{40,24},{48,0},{56,8},{1,49}... | collective-permute-start | bytes 24584 | tf_op jit(solution)/shard_map/ppermute | solution.py:221
  67.3 3.4 %collective-permute-start.8 = (f32[16,128]{1,0:T(8,128)S(1)}, f32[16,128]{1,0:T(8,128)S(1)}, u32[]{:S(2)}, u32[]{:S(2)}) collective-permute-start(f32[16,128]{1,0:T(8,128)S(1)} %copy-done.8), channel_id=1, source_target_pairs={{0,56},{8,48},{16,40},{24,32},{32,24},{40,16},{48,8},{56,0},{1,57}... | collective-permute-start | bytes 24584 | tf_op jit(solution)/shard_map/ppermute | solution.py:221
  70.8 7.5 %collective-permute-done.8.refs_7_ = f32[16,128]{1,0:T(8,128)S(1)} collective-permute-done((f32[16,128]{1,0:T(8,128)S(1)}, f32[16,128]{1,0:T(8,128)S(1)}, u32[]{:S(2)}, u32[]{:S(2)}) %collective-permute-start.8) | collective-permute-done | bytes 8224 | tf_op jit(solution)/shard_map/ppermute | solution.py:221
  79.0 10.9 %all-to-all-start.1 = ((f32[32,2,128]{2,1,0:T(2,128)}), f32[32,2,128]{2,1,0:T(2,128)S(1)}, u32[]{:S(2)}, u32[]{:S(2)}) async-start(f32[32,2,128]{2,1,0:T(2,128)} %broadcast_in_dim.4), calls=%async_computation.1 | async-start | bytes 65536 | tf_op jit(solution)/shard_map/all_to_all | solution.py:210
  89.9 7.2 %all-to-all-done.1.parts_ref = f32[32,2,128]{2,1,0:T(2,128)S(1)} async-done(((f32[32,2,128]{2,1,0:T(2,128)}), f32[32,2,128]{2,1,0:T(2,128)S(1)}, u32[]{:S(2)}, u32[]{:S(2)}) %all-to-all-start.1) | async-done | bytes 32800 | tf_op jit(solution)/shard_map/all_to_all | solution.py:210
  97.1 1.1 shard_map.75
  98.2 21.2 %all-to-all-start.2 = ((f32[32,2,128]{2,1,0:T(2,128)}), f32[32,2,128]{2,1,0:T(2,128)S(1)}, u32[]{:S(2)}, u32[]{:S(2)}) async-start(f32[32,2,128]{2,1,0:T(2,128)} %shard_map.75), calls=%async_computation.2 | async-start | bytes 65536 | tf_op jit(solution)/shard_map/all_to_all | solution.py:243
  119.4 11.9 %collective-permute-start.9 = (f32[2,18,1,128]{3,2,1,0:T(1,128)S(1)}, f32[2,18,1,128]{3,2,1,0:T(1,128)S(1)}, u32[]{:S(2)}, u32[]{:S(2)}) collective-permute-start(f32[2,18,1,128]{3,2,1,0:T(1,128)S(1)} %pad_maximum_fusion), channel_id=1, source_target_pairs={{0,1},{1,2},{2,3},{3,0},{4,5},{5,6},{6,7},{7,4},{8,9},{9,10},{10,1... | collective-permute-start | bytes 55304 | tf_op jit(solution)/shard_map/ppermute | solution.py:205
  131.3 2.1 %collective-permute-start.10 = (f32[2,18,1,128]{3,2,1,0:T(1,128)S(1)}, f32[2,18,1,128]{3,2,1,0:T(1,128)S(1)}, u32[]{:S(2)}, u32[]{:S(2)}) collective-permute-start(f32[2,18,1,128]{3,2,1,0:T(1,128)S(1)} %pad_maximum_fusion.1), channel_id=1, source_target_pairs={{1,0},{2,1},{3,2},{0,3},{5,4},{6,5},{7,6},{4,7},{9,8},{10,9},{11,1... | collective-permute-start | bytes 55304 | tf_op jit(solution)/shard_map/ppermute | solution.py:205
  133.6 11.0 %collective-permute-done.10.y_high_ref = f32[2,18,1,128]{3,2,1,0:T(1,128)S(1)} collective-permute-done((f32[2,18,1,128]{3,2,1,0:T(1,128)S(1)}, f32[2,18,1,128]{3,2,1,0:T(1,128)S(1)}, u32[]{:S(2)}, u32[]{:S(2)}) %collective-permute-start.10) | collective-permute-done | bytes 18464 | tf_op jit(solution)/shard_map/ppermute | solution.py:205
  144.6 5.2 %shard_map.76.local_ref = f32[2,16,32,128]{3,2,1,0:T(8,128)S(1)} custom-call(f32[2,16,32,128]{3,2,1,0:T(8,128)S(1)} %copy-done.1, f32[2,1,32,128]{3,2,1,0:T(8,128)S(1)} %collective-permute-done.x_low_ref, f32[2,1,32,128]{3,2,1,0:T(8,128)S(1)} %collective-permute-done.1.x_high_ref, f32[2,18,1,128]{3,2,1,0:T(1,128)S(1)} %collective-permute-done.9.y_low_ref, ...), custom_call_target="tpu_custom_call" | custom-call | tf_op jit(solution)/shard_map/pallas_call | solution.py:191
  149.8 12.7 %all_to_all.20.coarse_ref = f32[32,2,128]{2,1,0:T(2,128)S(1)} all-to-all(f32[32,2,128]{2,1,0:T(2,128)S(1)} %broadcast_in_dim.5), channel_id=1, replica_groups=mesh['y'=4,'x'=4,'low'=8,'core'=2,'high'=4] {'y','x','core'}, dimensions={0} | all-to-all | bytes 65536 | tf_op jit(solution)/shard_map/all_to_all | solution.py:210
  162.5 1.5 shard_map.77
  (39 shorter events, 1.7 us)
Async XLA Ops:
  0.0 0.8 copy-start.4
  0.8 1.0 copy-start
  1.8 88.0 %copy-start.1 = (f32[2,16,32,128]{3,2,1,0:T(8,128)S(1)}, f32[2,16,32,128]{3,2,1,0:T(8,128)}, u32[]{:S(2)}) copy-start(f32[2,16,32,128]{3,2,1,0:T(8,128)} %residual_ref.3) | copy-start | bytes 1572868
  3.2 75.2 %all-to-all-start = ((f32[32,2,128]{2,1,0:T(2,128)}), f32[32,2,128]{2,1,0:T(2,128)S(1)}, u32[]{:S(2)}, u32[]{:S(2)}) async-start(f32[32,2,128]{2,1,0:T(2,128)} %shard_map.73), calls=%async_computation | async-start | bytes 65536 | tf_op jit(solution)/shard_map/all_to_all | solution.py:235
  32.5 45.9 %collective-permute-start = (f32[2,1,32,128]{3,2,1,0:T(8,128)S(1)}, f32[2,1,32,128]{3,2,1,0:T(8,128)S(1)}, u32[]{:S(2)}, u32[]{:S(2)}) collective-permute-start(f32[2,1,32,128]{3,2,1,0:T(8,128)S(1)} %get-tuple-element.34), channel_id=1, source_target_pairs={{0,4},{4,8},{8,12},{12,16},{16,20},{20,24},{24,28},{28,32},{32,36}... | collective-permute-start | bytes 98312 | tf_op jit(solution)/shard_map/ppermute | solution.py:205
  36.7 41.6 %collective-permute-start.1 = (f32[2,1,32,128]{3,2,1,0:T(8,128)S(1)}, f32[2,1,32,128]{3,2,1,0:T(8,128)S(1)}, u32[]{:S(2)}, u32[]{:S(2)}) collective-permute-start(f32[2,1,32,128]{3,2,1,0:T(8,128)S(1)} %get-tuple-element.35), channel_id=1, source_target_pairs={{4,0},{8,4},{12,8},{16,12},{20,16},{24,20},{28,24},{32,28},{36,32}... | collective-permute-start | bytes 98312 | tf_op jit(solution)/shard_map/ppermute | solution.py:205
  40.1 27.2 %copy-start.8 = (f32[16,128]{1,0:T(8,128)S(1)}, f32[16,128]{1,0:T(8,128)}, u32[]{:S(2)}) copy-start(f32[16,128]{1,0:T(8,128)} %get-tuple-element.44) | copy-start | bytes 24580
  40.1 10.4 %collective-permute-start.2 = (f32[16,128]{1,0:T(8,128)}, f32[16,128]{1,0:T(8,128)S(1)}, u32[]{:S(2)}, u32[]{:S(2)}) collective-permute-start(f32[16,128]{1,0:T(8,128)} %get-tuple-element.38), channel_id=1, source_target_pairs={{0,8},{8,0},{16,24},{24,16},{32,40},{40,32},{48,56},{56,48},{1,9},... | collective-permute-start | bytes 24584 | tf_op jit(solution)/shard_map/ppermute | solution.py:221
  43.4 13.2 %collective-permute-start.3 = (f32[16,128]{1,0:T(8,128)}, f32[16,128]{1,0:T(8,128)S(1)}, u32[]{:S(2)}, u32[]{:S(2)}) collective-permute-start(f32[16,128]{1,0:T(8,128)} %get-tuple-element.39), channel_id=1, source_target_pairs={{0,16},{8,24},{16,0},{24,8},{32,48},{40,56},{48,32},{56,40},{1,17}... | collective-permute-start | bytes 24584 | tf_op jit(solution)/shard_map/ppermute | solution.py:221
  48.6 11.2 %collective-permute-start.4 = (f32[16,128]{1,0:T(8,128)}, f32[16,128]{1,0:T(8,128)S(1)}, u32[]{:S(2)}, u32[]{:S(2)}) collective-permute-start(f32[16,128]{1,0:T(8,128)} %get-tuple-element.40), channel_id=1, source_target_pairs={{0,24},{8,16},{16,8},{24,0},{32,56},{40,48},{48,40},{56,32},{1,25}... | collective-permute-start | bytes 24584 | tf_op jit(solution)/shard_map/ppermute | solution.py:221
  50.5 16.8 %collective-permute-start.5 = (f32[16,128]{1,0:T(8,128)}, f32[16,128]{1,0:T(8,128)S(1)}, u32[]{:S(2)}, u32[]{:S(2)}) collective-permute-start(f32[16,128]{1,0:T(8,128)} %get-tuple-element.41), channel_id=1, source_target_pairs={{0,32},{8,40},{16,48},{24,56},{32,0},{40,8},{48,16},{56,24},{1,33}... | collective-permute-start | bytes 24584 | tf_op jit(solution)/shard_map/ppermute | solution.py:221
  56.6 14.2 %collective-permute-start.6 = (f32[16,128]{1,0:T(8,128)}, f32[16,128]{1,0:T(8,128)S(1)}, u32[]{:S(2)}, u32[]{:S(2)}) collective-permute-start(f32[16,128]{1,0:T(8,128)} %get-tuple-element.42), channel_id=1, source_target_pairs={{0,40},{8,32},{16,56},{24,48},{32,8},{40,0},{48,24},{56,16},{1,41}... | collective-permute-start | bytes 24584 | tf_op jit(solution)/shard_map/ppermute | solution.py:221
  59.7 11.0 %collective-permute-start.7 = (f32[16,128]{1,0:T(8,128)}, f32[16,128]{1,0:T(8,128)S(1)}, u32[]{:S(2)}, u32[]{:S(2)}) collective-permute-start(f32[16,128]{1,0:T(8,128)} %get-tuple-element.43), channel_id=1, source_target_pairs={{0,48},{8,56},{16,32},{24,40},{32,16},{40,24},{48,0},{56,8},{1,49}... | collective-permute-start | bytes 24584 | tf_op jit(solution)/shard_map/ppermute | solution.py:221
  67.3 11.0 %collective-permute-start.8 = (f32[16,128]{1,0:T(8,128)S(1)}, f32[16,128]{1,0:T(8,128)S(1)}, u32[]{:S(2)}, u32[]{:S(2)}) collective-permute-start(f32[16,128]{1,0:T(8,128)S(1)} %copy-done.8), channel_id=1, source_target_pairs={{0,56},{8,48},{16,40},{24,32},{32,24},{40,16},{48,8},{56,0},{1,57}... | collective-permute-start | bytes 24584 | tf_op jit(solution)/shard_map/ppermute | solution.py:221
  79.0 18.1 %all-to-all-start.1 = ((f32[32,2,128]{2,1,0:T(2,128)}), f32[32,2,128]{2,1,0:T(2,128)S(1)}, u32[]{:S(2)}, u32[]{:S(2)}) async-start(f32[32,2,128]{2,1,0:T(2,128)} %broadcast_in_dim.4), calls=%async_computation.1 | async-start | bytes 65536 | tf_op jit(solution)/shard_map/all_to_all | solution.py:210
  89.9 7.2 %copy-start.2 = (f32[16,128]{1,0:T(8,128)S(1)}, f32[16,128]{1,0:T(8,128)}, u32[]{:S(2)}) copy-start(f32[16,128]{1,0:T(8,128)} %get-tuple-element.49.refs_0_) | copy-start | bytes 24580
  98.2 51.6 %all-to-all-start.2 = ((f32[32,2,128]{2,1,0:T(2,128)}), f32[32,2,128]{2,1,0:T(2,128)S(1)}, u32[]{:S(2)}, u32[]{:S(2)}) async-start(f32[32,2,128]{2,1,0:T(2,128)} %shard_map.75), calls=%async_computation.2 | async-start | bytes 65536 | tf_op jit(solution)/shard_map/all_to_all | solution.py:243
  119.4 14.1 %copy-start.6 = (f32[8,18,18]{2,0,1:T(8,128)S(1)}, f32[8,18,18]{2,0,1:T(8,128)}, u32[]{:S(2)}) copy-start(f32[8,18,18]{2,0,1:T(8,128)} %param.10) | copy-start | bytes 31108
  119.4 14.1 %collective-permute-start.9 = (f32[2,18,1,128]{3,2,1,0:T(1,128)S(1)}, f32[2,18,1,128]{3,2,1,0:T(1,128)S(1)}, u32[]{:S(2)}, u32[]{:S(2)}) collective-permute-start(f32[2,18,1,128]{3,2,1,0:T(1,128)S(1)} %pad_maximum_fusion), channel_id=1, source_target_pairs={{0,1},{1,2},{2,3},{3,0},{4,5},{5,6},{6,7},{7,4},{8,9},{9,10},{10,1... | collective-permute-start | bytes 55304 | tf_op jit(solution)/shard_map/ppermute | solution.py:205
  131.3 2.2 %copy-start.7 = (f32[2,18,18]{2,0,1:T(2,128)S(1)}, f32[2,18,18]{2,0,1:T(2,128)}, u32[]{:S(2)}) copy-start(f32[2,18,18]{2,0,1:T(2,128)} %param.8) | copy-start | bytes 7780
  131.3 13.2 %collective-permute-start.10 = (f32[2,18,1,128]{3,2,1,0:T(1,128)S(1)}, f32[2,18,1,128]{3,2,1,0:T(1,128)S(1)}, u32[]{:S(2)}, u32[]{:S(2)}) collective-permute-start(f32[2,18,1,128]{3,2,1,0:T(1,128)S(1)} %pad_maximum_fusion.1), channel_id=1, source_target_pairs={{1,0},{2,1},{3,2},{0,3},{5,4},{6,5},{7,6},{4,7},{9,8},{10,9},{11,1... | collective-permute-start | bytes 55304 | tf_op jit(solution)/shard_map/ppermute | solution.py:205
  133.5 11.0 %copy-start.3 = (f32[8,18]{1,0:T(8,128)S(1)}, f32[8,18]{1,0:T(8,128)}, u32[]{:S(2)}) copy-start(f32[8,18]{1,0:T(8,128)} %upward_values_ref.1) | copy-start | bytes 1732
  133.5 11.0 %copy-start.5 = (f32[2,18]{1,0:T(2,128)S(1)}, f32[2,18]{1,0:T(2,128)}, u32[]{:S(2)}) copy-start(f32[2,18]{1,0:T(2,128)} %horiz_values_ref.1) | copy-start | bytes 436

commit v3 on v1

--- a/solution.py
+++ b/solution.py
@@ -60,26 +60,64 @@
     return first, pair - EXTENT * first
 
 
-def contributions_kernel(labels_ref, residual_ref, out_ref):
-    out_ref[...] = jnp.zeros_like(out_ref)
-    lane = iota((2, 128), 1)
+def message_kernel(labels_ref, residual_ref, out_ref):
+    lane = iota((1, 128), 1)
+    wide = iota((2, 128), 1)
+    message = jnp.zeros((1, 128), jnp.float32)
     for j in range(2):
+        ys = slice(j * SPAN, (j + 1) * SPAN)
         sums = jnp.concatenate(
             [
-                jnp.sum(
-                    jnp.sum(residual_ref[v, :, j * SPAN : (j + 1) * SPAN, :], axis=0),
-                    axis=0,
-                    keepdims=True,
-                )
+                jnp.sum(jnp.sum(residual_ref[v, :, ys, :], axis=0), axis=0, keepdims=True)
                 for v in range(2)
             ],
             axis=0,
         )
         for k in range(8):
-            total = jnp.sum(jnp.where((lane >> 4) == k, sums, 0.0), axis=1, keepdims=True)
-            label = labels_ref[j * 8 + k]
-            block = label >> 7
-            out_ref[block] += jnp.where(lane == (label & 127), total * WEIGHT, 0.0)
+            total = jnp.sum(jnp.where((wide >> 4) == k, sums, 0.0), axis=1, keepdims=True)
+            slot = j * 8 + k
+            label = labels_ref[0, j, k].astype(jnp.float32)
+            message = jnp.where(lane == slot, total[0:1] * WEIGHT, message)
+            message = jnp.where(lane == slot + 16, total[1:2] * WEIGHT, message)
+            message = jnp.where(lane == slot + 32, label, message)
+    out_ref[...] = jnp.broadcast_to(message[None], out_ref.shape)
+
+
+def scatter_kernel(slab_ref, parts_ref, out_ref):
+    parts = parts_ref[...].reshape(LINE_SIZE, 128)
+    lane = iota((LINE_SIZE, 128), 1)
+    base = slab_ref[0] * 1024
+    first, second, label = (
+        [jnp.broadcast_to(parts[:, begin + e : begin + e + 1], parts.shape) for e in range(16)]
+        for begin in (0, 16, 32)
+    )
+    label = [value.astype(jnp.int32) for value in label]
+    rows = []
+    for values in (first, second):
+        for block in range(8):
+            column = lane + (base + block * 128)
+            total = jnp.zeros_like(parts)
+            for e in range(16):
+                total = total + jnp.where(label[e] == column, values[e], 0.0)
+            rows.append(jnp.sum(total, axis=0, keepdims=True))
+    rows = jnp.concatenate(rows, axis=0)
+    out_ref[...] = jnp.broadcast_to(rows[None], out_ref.shape)
+
+
+def terms_kernel(place_ref, parts_ref, matrix_ref, out_ref):
+    rhs = jnp.sum(parts_ref[...], axis=0)
+    lane = iota((SPAN, 128), 1) - iota((SPAN, 128), 0)
+    here = lane == place_ref[0] * SPAN
+    terms = []
+    for v in range(2):
+        total = jnp.zeros((SPAN, 128), jnp.float32)
+        for block in range(8):
+            row = v * 8 + block
+            total = total + matrix_ref[:, block * 128 : (block + 1) * 128] * rhs[row : row + 1]
+        column = jnp.sum(total, axis=1, keepdims=True)
+        terms.append(jnp.sum(jnp.where(here, column, 0.0), axis=0, keepdims=True))
+    terms = jnp.concatenate(terms, axis=0)
+    out_ref[...] = jnp.broadcast_to(terms[None], out_ref.shape)
 
 
 def local_kernel(
@@ -153,7 +191,7 @@
     for j in range(2):
         update = jnp.zeros((2, 128), jnp.float32)
         for k in range(8):
-            label = labels_ref[j * 8 + k]
+            label = labels_ref[0, j, k]
             block = ((label >> 8) << 1) | ((label >> 4) & 1)
             place = (((label >> 5) & 7) << 4) | (label & 15)
             value = jnp.sum(
@@ -177,12 +215,6 @@
     )(*scalars, *arrays)
 
 
-def neighbours(axis, size, low_side, high_side):
-    up = [(i, (i + 1) % size) for i in range(size)]
-    down = [(j, i) for i, j in up]
-    return lax.ppermute(high_side, axis, up), lax.ppermute(low_side, axis, down)
-
-
 def to_all(value, axes, size):
     copies = jnp.broadcast_to(value[None], (size,) + value.shape)
     return lax.all_to_all(copies, axes, 0, 0)
@@ -192,25 +224,37 @@
     residual, horiz_vectors, horiz_values, upward_eigen_tables, upward_eigen_values,
     aggregate_map, coarse_inverse,
 ):
-    labels = aggregate_map.reshape(16)
-
-    x_low, x_high = neighbours(GROUP, 256, residual[:, :1], residual[:, -1:])
+    labels = aggregate_map
+    place = lax.axis_index("low").reshape(1)
+    slab = lax.axis_index("high").reshape(1)
+    even = lax.axis_index("core") == 0
+    barrier = lax.optimization_barrier
+
+    parts = call(message_kernel, (LINE_SIZE, 1, 128), [labels], [residual])
+    first, last = residual[:, :1], residual[:, -1:]
+    parts, inner, outer = barrier(
+        (parts, jnp.where(even, last, first), jnp.where(even, first, last))
+    )
+    line_parts = lax.all_to_all(parts, LINE, 0, 0)
+    inner = lax.ppermute(inner, GROUP, [(i, i ^ 1) for i in range(256)])
+    outer = lax.ppermute(outer, GROUP, [(i, (i + i % 2 * 2 - 1) % 256) for i in range(256)])
+    line_parts, inner, outer = barrier((line_parts, inner, outer))
+    x_low, x_high = jnp.where(even, outer, inner), jnp.where(even, inner, outer)
     low_side = jnp.concatenate([x_low[:, :, :1], residual[:, :, :1], x_high[:, :, :1]], axis=1)
     high_side = jnp.concatenate([x_low[:, :, -1:], residual[:, :, -1:], x_high[:, :, -1:]], axis=1)
-    y_low, y_high = neighbours("high", 4, low_side, high_side)
-
-    tiles = jnp.swapaxes(coarse_inverse.reshape(16, 8, 128), 0, 1)
-    tile = lax.all_to_all(tiles, "low", 0, 0).reshape(128, 128)
-
-    parts = call(contributions_kernel, (LINE_SIZE, 2, 128), [labels], [residual])
-    line_sum = lax.all_to_all(parts, LINE, 0, 0).sum(axis=0)
-    rhs = to_all(line_sum, PLANE, PLANE_SIZE).sum(axis=0)
-    terms = lax.dot_general(
-        rhs, tile, (((1,), (1,)), ((), ())),
-        precision=lax.Precision.HIGHEST, preferred_element_type=jnp.float32,
-    )
-    rows = to_all(terms, LINE, LINE_SIZE).sum(axis=0)
-    coarse = to_all(rows, PLANE, PLANE_SIZE)
+
+    dense = call(scatter_kernel, (PLANE_SIZE, 16, 128), [slab], [line_parts])
+    dense, low_side, high_side = barrier((dense, low_side, high_side))
+    plane_parts = lax.all_to_all(dense, PLANE, 0, 0)
+    y_low = lax.ppermute(high_side, "high", [(i, (i + 1) % 4) for i in range(4)])
+    plane_parts, y_low, low_side = barrier((plane_parts, y_low, low_side))
+
+    terms = call(terms_kernel, (LINE_SIZE, 2, 128), [place], [plane_parts, coarse_inverse])
+    terms, low_side = barrier((terms, low_side))
+    row_parts = lax.all_to_all(terms, LINE, 0, 0)
+    y_high = lax.ppermute(low_side, "high", [(i, (i - 1) % 4) for i in range(4)])
+    row_parts, y_high = barrier((row_parts, y_high))
+    coarse = to_all(row_parts.sum(axis=0), PLANE, PLANE_SIZE)
 
     local = call(
         local_kernel, residual.shape, [],

time: 150 us -> 139 us (0.927)
  blocking collectives: 51 us -> 0 us
  starting transfers between devices: 52.1 us -> 83.2 us
  Pallas kernels: 7.38 us -> 14.2 us
  waiting for transfers between devices: 33.2 us -> 37.9 us
    all_to_all x1 -> x0, blocking collectives: 51 us -> none  [on_device(): line_sum = lax.all_to_all(parts, LINE, 0, 0).sum(axis=0)]
    all_to_all x1 -> x3, starting transfers between devices: 3.35 us -> 50.4 us  [the longest x1 29.3 us: on_device(): line_parts = lax.all_to_all(parts, LINE, 0, 0)]
    all_to_all x3 -> x1, starting transfers between devices: 29 us -> 10.1 us  [to_all(): return lax.all_to_all(copies, axes, 0, 0)]
    all_to_all x1 -> x3, waiting for transfers between devices: 3.91 us -> 21.1 us  [the longest x1 12.7 us: on_device(): line_parts = lax.all_to_all(parts, LINE, 0, 0)]
    all_to_all x3 -> x1, waiting for transfers between devices: 17.2 us -> 1.34 us  [to_all(): return lax.all_to_all(copies, axes, 0, 0)]
    pallas_call x3 -> x5, Pallas kernels: 7.38 us -> 14.2 us  [call(): pl.pallas_call(kernel, out_shape=jax.ShapeDtypeStruct(out_shape, jnp.floa...]
    ppermute x4, waiting for transfers between devices: 12.1 us -> 15.4 us  [the longest x1 11.5 us: on_device(): lax.ppermute(high_side, 'high', [(i, (i + 1) % 4) for i in range(4)])]
    ppermute x4, starting transfers between devices: 19.8 us -> 22.7 us  [the longest x1 11.9 us: on_device(): lax.ppermute(low_side, 'high', [(i, (i - 1) % 4) for i in range(4)])]
  transfers between devices with their start and end apart: 8 -> 8, of which waited for: 4 -> 6; matrix products, arithmetic and copies ran while one was open for 2% -> 0% of each run, Pallas kernels for 3% -> 4%
where the time goes in v3:
time: 139 us
  starting transfers between devices  83.2 us (60%)
  waiting for transfers between devices  37.9 us (27%)
  Pallas kernels  14.2 us (10%)
  local copies, waits for them, and re-layouts  3.07 us (2%)
    all_to_all x1, starting transfers between devices, on_device(): line_parts = lax.all_to_all(parts, LINE, 0, 0)  29.3 us
    pallas_call x5, Pallas kernels, call(): pl.pallas_call(kernel, out_shape=jax.ShapeDtypeStruct(out_shape, jnp.floa...  14.2 us
    all_to_all x1, waiting for transfers between devices, on_device(): line_parts = lax.all_to_all(parts, LINE, 0, 0)  12.7 us
    ppermute x1, starting transfers between devices, on_device(): lax.ppermute(low_side, 'high', [(i, (i - 1) % 4) for i in range(4)])  11.9 us
    all_to_all x1, starting transfers between devices, on_device(): row_parts = lax.all_to_all(terms, LINE, 0, 0)  11.8 us
    ppermute x1, waiting for transfers between devices, on_device(): lax.ppermute(high_side, 'high', [(i, (i + 1) % 4) for i in range(4)])  11.5 us
    all_to_all x1, starting transfers between devices, to_all(): return lax.all_to_all(copies, axes, 0, 0)  10.1 us
    all_to_all x1, starting transfers between devices, on_device(): plane_parts = lax.all_to_all(dense, PLANE, 0, 0)  9.3 us
  transfers between devices with their start and end apart: 8, of which 6 were waited for; matrix products, arithmetic and copies ran while one was open for 0% of the time, Pallas kernels for 4%

profile of v3, /device:TPU:1, one launch (start us, length us, event | category | flops | bytes accessed | tf_op | source)
XLA Modules:
  0.0 138.7 jit_solution(12165284389963773233)
XLA Ops:
  0.0 0.7 copy-done.4
  0.7 1.0 copy-done
  1.7 1.3 shard_map.73
  3.1 29.3 %all-to-all-start = ((f32[32,1,128]{2,1,0:T(1,128)}), f32[32,1,128]{2,1,0:T(1,128)S(1)}, u32[]{:S(2)}, u32[]{:S(2)}) async-start(f32[32,1,128]{2,1,0:T(1,128)} %shard_map.73), calls=%async_computation | async-start | bytes 32768 | tf_op jit(solution)/shard_map/all_to_all | solution.py:238
  32.4 2.9 %collective-permute-start = (f32[2,1,32,128]{3,2,1,0:T(8,128)S(1)}, f32[2,1,32,128]{3,2,1,0:T(8,128)S(1)}, u32[]{:S(2)}, u32[]{:S(2)}) collective-permute-start(f32[2,1,32,128]{3,2,1,0:T(8,128)S(1)} %get-tuple-element.22), channel_id=1, source_target_pairs={{0,4},{4,0},{8,12},{12,8},{16,20},{20,16},{24,28},{28,24},{32,36},... | collective-permute-start | bytes 98312 | tf_op jit(solution)/shard_map/ppermute | solution.py:239
  35.2 3.3 %collective-permute-start.1 = (f32[2,1,32,128]{3,2,1,0:T(8,128)S(1)}, f32[2,1,32,128]{3,2,1,0:T(8,128)S(1)}, u32[]{:S(2)}, u32[]{:S(2)}) collective-permute-start(f32[2,1,32,128]{3,2,1,0:T(8,128)S(1)} %get-tuple-element.23), channel_id=1, source_target_pairs={{0,1020},{4,8},{8,4},{12,16},{16,12},{20,24},{24,20},{28,32},{32,2... | collective-permute-start | bytes 98312 | tf_op jit(solution)/shard_map/ppermute | solution.py:240
  38.6 2.2 %collective-permute-done.1 = f32[2,1,32,128]{3,2,1,0:T(8,128)S(1)} collective-permute-done((f32[2,1,32,128]{3,2,1,0:T(8,128)S(1)}, f32[2,1,32,128]{3,2,1,0:T(8,128)S(1)}, u32[]{:S(2)}, u32[]{:S(2)}) %collective-permute-start.1) | collective-permute-done | bytes 32800 | tf_op jit(solution)/shard_map/ppermute | solution.py:240
  40.8 12.7 %all-to-all-done.parts_ref = f32[32,1,128]{2,1,0:T(1,128)S(1)} async-done(((f32[32,1,128]{2,1,0:T(1,128)}), f32[32,1,128]{2,1,0:T(1,128)S(1)}, u32[]{:S(2)}, u32[]{:S(2)}) %all-to-all-start) | async-done | bytes 16416 | tf_op jit(solution)/shard_map/all_to_all | solution.py:238
  53.6 5.5 %shard_map.74 = f32[32,16,128]{2,1,0:T(8,128)} custom-call(s32[1]{0:T(128)} %bitcast.slab_ref, f32[32,1,128]{2,1,0:T(1,128)S(1)} %all-to-all-done.parts_ref), custom_call_target="tpu_custom_call" | custom-call | tf_op jit(solution)/shard_map/pallas_call | solution.py:207
  59.1 9.3 %all-to-all-start.1 = ((f32[32,16,128]{2,1,0:T(8,128)}), f32[32,16,128]{2,1,0:T(8,128)S(1)}, u32[]{:S(2)}, u32[]{:S(2)}) async-start(f32[32,16,128]{2,1,0:T(8,128)} %shard_map.74), calls=%async_computation.1 | async-start | bytes 524288 | tf_op jit(solution)/shard_map/all_to_all | solution.py:248
  68.4 4.6 %collective-permute-start.2 = (f32[2,18,1,128]{3,2,1,0:T(1,128)S(1)}, f32[2,18,1,128]{3,2,1,0:T(1,128)S(1)}, u32[]{:S(2)}, u32[]{:S(2)}) collective-permute-start(f32[2,18,1,128]{3,2,1,0:T(1,128)S(1)} %pad_maximum_fusion.1), channel_id=1, source_target_pairs={{0,1},{1,2},{2,3},{3,0},{4,5},{5,6},{6,7},{7,4},{8,9},{9,10},{10,1... | collective-permute-start | bytes 55304 | tf_op jit(solution)/shard_map/ppermute | solution.py:249
  73.1 11.5 %collective-permute-done.2.y_low_ref = f32[2,18,1,128]{3,2,1,0:T(1,128)S(1)} collective-permute-done((f32[2,18,1,128]{3,2,1,0:T(1,128)S(1)}, f32[2,18,1,128]{3,2,1,0:T(1,128)S(1)}, u32[]{:S(2)}, u32[]{:S(2)}) %collective-permute-start.2) | collective-permute-done | bytes 18464 | tf_op jit(solution)/shard_map/ppermute | solution.py:249
  84.5 0.8 shard_map.75
  85.3 11.8 %all-to-all-start.2 = ((f32[32,2,128]{2,1,0:T(2,128)}), f32[32,2,128]{2,1,0:T(2,128)S(1)}, u32[]{:S(2)}, u32[]{:S(2)}) async-start(f32[32,2,128]{2,1,0:T(2,128)} %shard_map.75), calls=%async_computation.2 | async-start | bytes 65536 | tf_op jit(solution)/shard_map/all_to_all | solution.py:254
  97.2 11.9 %collective-permute-start.3 = (f32[2,18,1,128]{3,2,1,0:T(1,128)S(1)}, f32[2,18,1,128]{3,2,1,0:T(1,128)S(1)}, u32[]{:S(2)}, u32[]{:S(2)}) collective-permute-start(f32[2,18,1,128]{3,2,1,0:T(1,128)S(1)} %pad_maximum_fusion), channel_id=1, source_target_pairs={{0,3},{1,0},{2,1},{3,2},{4,7},{5,4},{6,5},{7,6},{8,11},{9,8},{10,9... | collective-permute-start | bytes 55304 | tf_op jit(solution)/shard_map/ppermute | solution.py:255
  109.1 1.7 %collective-permute-done.3.y_high_ref = f32[2,18,1,128]{3,2,1,0:T(1,128)S(1)} collective-permute-done((f32[2,18,1,128]{3,2,1,0:T(1,128)S(1)}, f32[2,18,1,128]{3,2,1,0:T(1,128)S(1)}, u32[]{:S(2)}, u32[]{:S(2)}) %collective-permute-start.3) | collective-permute-done | bytes 18464 | tf_op jit(solution)/shard_map/ppermute | solution.py:255
  110.8 8.4 %all-to-all-done.2 = f32[32,2,128]{2,1,0:T(2,128)S(1)} async-done(((f32[32,2,128]{2,1,0:T(2,128)}), f32[32,2,128]{2,1,0:T(2,128)S(1)}, u32[]{:S(2)}, u32[]{:S(2)}) %all-to-all-start.2) | async-done | bytes 32800 | tf_op jit(solution)/shard_map/all_to_all | solution.py:254
  119.2 0.6 broadcast_in_dim.2
  119.8 10.1 %all-to-all-start.3 = ((f32[32,2,128]{2,1,0:T(2,128)}), f32[32,2,128]{2,1,0:T(2,128)S(1)}, u32[]{:S(2)}, u32[]{:S(2)}) async-start(f32[32,2,128]{2,1,0:T(2,128)} %broadcast_in_dim.2), calls=%async_computation.3 | async-start | bytes 65536 | tf_op jit(solution)/shard_map/all_to_all | solution.py:220
  130.0 0.6 copy-done.3
  130.7 0.0 copy-done.5
  130.7 5.2 %shard_map.76.local_ref = f32[2,16,32,128]{3,2,1,0:T(8,128)S(1)} custom-call(f32[2,16,32,128]{3,2,1,0:T(8,128)S(1)} %copy-done.1, f32[2,1,32,128]{3,2,1,0:T(8,128)S(1)} %get-tuple-element.42.x_low_ref, f32[2,1,32,128]{3,2,1,0:T(8,128)S(1)} %get-tuple-element.41.x_high_ref, f32[2,18,1,128]{3,2,1,0:T(1,128)S(1)} %collective-permute-done.2.y_low_ref, ...), custom_call_target="tpu_custom_call" | custom-call | tf_op jit(solution)/shard_map/pallas_call | solution.py:207
  135.8 1.3 all-to-all-done.3.coarse_ref
  137.2 1.5 %shard_map.77 = f32[2,16,32,128]{3,2,1,0:T(8,128)} custom-call(s32[1,2,8]{2,1,0:T(2,128)S(1)} %copy-done.4, f32[2,16,32,128]{3,2,1,0:T(8,128)S(1)} %shard_map.76.local_ref, f32[32,2,128]{2,1,0:T(2,128)S(1)} %all-to-all-done.3.coarse_ref), custom_call_target="tpu_custom_call" | custom-call | tf_op jit(solution)/shard_map/pallas_call | solution.py:207
  (23 shorter events, 0.2 us)
Async XLA Ops:
  0.0 0.7 copy-start.4
  0.7 1.0 copy-start
  1.7 36.8 %copy-start.1 = (f32[2,16,32,128]{3,2,1,0:T(8,128)S(1)}, f32[2,16,32,128]{3,2,1,0:T(8,128)}, u32[]{:S(2)}) copy-start(f32[2,16,32,128]{3,2,1,0:T(8,128)} %residual_ref.3) | copy-start | bytes 1572868
  3.1 50.5 %all-to-all-start = ((f32[32,1,128]{2,1,0:T(1,128)}), f32[32,1,128]{2,1,0:T(1,128)S(1)}, u32[]{:S(2)}, u32[]{:S(2)}) async-start(f32[32,1,128]{2,1,0:T(1,128)} %shard_map.73), calls=%async_computation | async-start | bytes 32768 | tf_op jit(solution)/shard_map/all_to_all | solution.py:238
  32.4 6.2 %collective-permute-start = (f32[2,1,32,128]{3,2,1,0:T(8,128)S(1)}, f32[2,1,32,128]{3,2,1,0:T(8,128)S(1)}, u32[]{:S(2)}, u32[]{:S(2)}) collective-permute-start(f32[2,1,32,128]{3,2,1,0:T(8,128)S(1)} %get-tuple-element.22), channel_id=1, source_target_pairs={{0,4},{4,0},{8,12},{12,8},{16,20},{20,16},{24,28},{28,24},{32,36},... | collective-permute-start | bytes 98312 | tf_op jit(solution)/shard_map/ppermute | solution.py:239
  35.2 5.6 %collective-permute-start.1 = (f32[2,1,32,128]{3,2,1,0:T(8,128)S(1)}, f32[2,1,32,128]{3,2,1,0:T(8,128)S(1)}, u32[]{:S(2)}, u32[]{:S(2)}) collective-permute-start(f32[2,1,32,128]{3,2,1,0:T(8,128)S(1)} %get-tuple-element.23), channel_id=1, source_target_pairs={{0,1020},{4,8},{8,4},{12,16},{16,12},{20,24},{24,20},{28,32},{32,2... | collective-permute-start | bytes 98312 | tf_op jit(solution)/shard_map/ppermute | solution.py:240
  59.1 25.4 %copy-start.2 = (f32[16,1024]{1,0:T(8,128)S(1)}, f32[16,1024]{1,0:T(8,128)}, u32[]{:S(2)}) copy-start(f32[16,1024]{1,0:T(8,128)} %matrix_ref.1) | copy-start | bytes 196612
  59.1 25.4 %all-to-all-start.1 = ((f32[32,16,128]{2,1,0:T(8,128)}), f32[32,16,128]{2,1,0:T(8,128)S(1)}, u32[]{:S(2)}, u32[]{:S(2)}) async-start(f32[32,16,128]{2,1,0:T(8,128)} %shard_map.74), calls=%async_computation.1 | async-start | bytes 524288 | tf_op jit(solution)/shard_map/all_to_all | solution.py:248
  68.4 16.1 %collective-permute-start.2 = (f32[2,18,1,128]{3,2,1,0:T(1,128)S(1)}, f32[2,18,1,128]{3,2,1,0:T(1,128)S(1)}, u32[]{:S(2)}, u32[]{:S(2)}) collective-permute-start(f32[2,18,1,128]{3,2,1,0:T(1,128)S(1)} %pad_maximum_fusion.1), channel_id=1, source_target_pairs={{0,1},{1,2},{2,3},{3,0},{4,5},{5,6},{6,7},{7,4},{8,9},{9,10},{10,1... | collective-permute-start | bytes 55304 | tf_op jit(solution)/shard_map/ppermute | solution.py:249
  85.3 33.9 %all-to-all-start.2 = ((f32[32,2,128]{2,1,0:T(2,128)}), f32[32,2,128]{2,1,0:T(2,128)S(1)}, u32[]{:S(2)}, u32[]{:S(2)}) async-start(f32[32,2,128]{2,1,0:T(2,128)} %shard_map.75), calls=%async_computation.2 | async-start | bytes 65536 | tf_op jit(solution)/shard_map/all_to_all | solution.py:254
  97.2 13.7 %collective-permute-start.3 = (f32[2,18,1,128]{3,2,1,0:T(1,128)S(1)}, f32[2,18,1,128]{3,2,1,0:T(1,128)S(1)}, u32[]{:S(2)}, u32[]{:S(2)}) collective-permute-start(f32[2,18,1,128]{3,2,1,0:T(1,128)S(1)} %pad_maximum_fusion), channel_id=1, source_target_pairs={{0,3},{1,0},{2,1},{3,2},{4,7},{5,4},{6,5},{7,6},{8,11},{9,8},{10,9... | collective-permute-start | bytes 55304 | tf_op jit(solution)/shard_map/ppermute | solution.py:255
  119.2 10.7 %copy-start.6 = (f32[8,18,18]{2,0,1:T(8,128)S(1)}, f32[8,18,18]{2,0,1:T(8,128)}, u32[]{:S(2)}) copy-start(f32[8,18,18]{2,0,1:T(8,128)} %param.10) | copy-start | bytes 31108
  119.8 10.1 %copy-start.7 = (f32[2,18,18]{2,0,1:T(2,128)S(1)}, f32[2,18,18]{2,0,1:T(2,128)}, u32[]{:S(2)}) copy-start(f32[2,18,18]{2,0,1:T(2,128)} %param.8) | copy-start | bytes 7780
  119.8 17.3 %all-to-all-start.3 = ((f32[32,2,128]{2,1,0:T(2,128)}), f32[32,2,128]{2,1,0:T(2,128)S(1)}, u32[]{:S(2)}, u32[]{:S(2)}) async-start(f32[32,2,128]{2,1,0:T(2,128)} %broadcast_in_dim.2), calls=%async_computation.3 | async-start | bytes 65536 | tf_op jit(solution)/shard_map/all_to_all | solution.py:220
  130.0 0.7 copy-start.3
  130.0 0.7 copy-start.5

commit v4 on v3

--- a/solution.py
+++ b/solution.py
@@ -14,6 +14,7 @@
 PLANE = ("y", "x", "core")
 LINE = ("high", "low")
 LINE_SIZE = 32
+LOCAL_FLOPS = 30000000000
 PLANE_SIZE = 32
 
 
@@ -86,21 +87,19 @@
 def scatter_kernel(slab_ref, parts_ref, out_ref):
     parts = parts_ref[...].reshape(LINE_SIZE, 128)
     lane = iota((LINE_SIZE, 128), 1)
-    base = slab_ref[0] * 1024
-    first, second, label = (
-        [jnp.broadcast_to(parts[:, begin + e : begin + e + 1], parts.shape) for e in range(16)]
-        for begin in (0, 16, 32)
-    )
-    label = [value.astype(jnp.int32) for value in label]
-    rows = []
-    for values in (first, second):
-        for block in range(8):
-            column = lane + (base + block * 128)
-            total = jnp.zeros_like(parts)
-            for e in range(16):
-                total = total + jnp.where(label[e] == column, values[e], 0.0)
-            rows.append(jnp.sum(total, axis=0, keepdims=True))
-    rows = jnp.concatenate(rows, axis=0)
+    block = (lane & 7) + slab_ref[0] * 8
+    values, places = [], []
+    for e in range(16):
+        first, second, label = (
+            jnp.broadcast_to(parts[:, slot : slot + 1], parts.shape) for slot in (e, e + 16, e + 32)
+        )
+        label = label.astype(jnp.int32)
+        here = ((label >> 7) == block) & (lane < 16)
+        values.append(jnp.where(here, jnp.where(lane < 8, first, second), 0.0))
+        places.append(jnp.where((label & 127) == lane, 1.0, 0.0))
+    values = jnp.concatenate(values, axis=0)
+    places = jnp.concatenate(places, axis=0)
+    rows = exact(values, places, ((0,), (0,)))[:16]
     out_ref[...] = jnp.broadcast_to(rows[None], out_ref.shape)
 
 
@@ -203,7 +202,7 @@
             out_ref[v, :, ys, :] = local_ref[v, :, ys, :] + update[v : v + 1][None]
 
 
-def call(kernel, out_shape, scalars, arrays, scratch=()):
+def call(kernel, out_shape, scalars, arrays, scratch=(), cost=None):
     return pl.pallas_call(
         kernel,
         out_shape=jax.ShapeDtypeStruct(out_shape, jnp.float32),
@@ -212,6 +211,7 @@
         out_specs=pl.BlockSpec(memory_space=pltpu.VMEM),
         scratch_shapes=list(scratch),
         compiler_params=pltpu.CompilerParams(vmem_limit_bytes=40 << 20),
+        cost_estimate=cost,
     )(*scalars, *arrays)
 
 
@@ -246,23 +246,22 @@
     dense = call(scatter_kernel, (PLANE_SIZE, 16, 128), [slab], [line_parts])
     dense, low_side, high_side = barrier((dense, low_side, high_side))
     plane_parts = lax.all_to_all(dense, PLANE, 0, 0)
+    plane_parts, low_side, high_side = barrier((plane_parts, low_side, high_side))
+
+    terms = call(terms_kernel, (LINE_SIZE, 2, 128), [place], [plane_parts, coarse_inverse])
+    row_parts = lax.all_to_all(terms, LINE, 0, 0)
     y_low = lax.ppermute(high_side, "high", [(i, (i + 1) % 4) for i in range(4)])
-    plane_parts, y_low, low_side = barrier((plane_parts, y_low, low_side))
-
-    terms = call(terms_kernel, (LINE_SIZE, 2, 128), [place], [plane_parts, coarse_inverse])
-    terms, low_side = barrier((terms, low_side))
-    row_parts = lax.all_to_all(terms, LINE, 0, 0)
     y_high = lax.ppermute(low_side, "high", [(i, (i - 1) % 4) for i in range(4)])
-    row_parts, y_high = barrier((row_parts, y_high))
-    coarse = to_all(row_parts.sum(axis=0), PLANE, PLANE_SIZE)
-
     local = call(
         local_kernel, residual.shape, [],
         [residual, x_low, x_high, y_low, y_high, horiz_vectors, horiz_values,
          upward_eigen_tables, upward_eigen_values],
         [pltpu.VMEM((POINTS, 512), jnp.float32), pltpu.VMEM((PAIRS, 512), jnp.float32),
          pltpu.VMEM((128, 144), jnp.float32), pltpu.VMEM((1, 144), jnp.float32)],
-    )
+        pl.CostEstimate(flops=LOCAL_FLOPS, transcendentals=0, bytes_accessed=1 << 20),
+    )
+    row_parts, local = barrier((row_parts, local))
+    coarse = to_all(row_parts.sum(axis=0), PLANE, PLANE_SIZE)
     return call(merge_kernel, residual.shape, [labels], [local, coarse])
 
 

time: 139 us -> 141 us (1.014)
  blocking collectives: 0 us -> 30.8 us
  starting transfers between devices: 83.2 us -> 64.3 us
  waiting for transfers between devices: 37.9 us -> 31.7 us
  Pallas kernels: 14.2 us -> 11 us
    all_to_all x0 -> x2, blocking collectives: none -> 30.8 us  [the longest x1 18 us: on_device(): plane_parts = lax.all_to_all(dense, PLANE, 0, 0)]
    all_to_all x2 -> x0, starting transfers between devices: 19.4 us -> none  [the longest x1 10.1 us: to_all(): return lax.all_to_all(copies, axes, 0, 0)]
    ppermute x1, waiting for transfers between devices: 11.5 us -> 0.01 us  [on_device(): lax.ppermute(high_side, 'high', [(i, (i + 1) % 4) for i in range(4)])]
    all_to_all x1, waiting for transfers between devices: 8.35 us -> 16.8 us  [on_device(): row_parts = lax.all_to_all(terms, LINE, 0, 0)]
    pallas_call x5, Pallas kernels: 14.2 us -> 11 us  [call(): pl.pallas_call(kernel, out_shape=jax.ShapeDtypeStruct(out_shape, jnp.floa...]
    all_to_all x1, starting transfers between devices: 11.8 us -> 14.9 us  [on_device(): row_parts = lax.all_to_all(terms, LINE, 0, 0)]
    ppermute x1, starting transfers between devices: 11.9 us -> 9.4 us  [on_device(): lax.ppermute(low_side, 'high', [(i, (i - 1) % 4) for i in range(4)])]
    ppermute x1, waiting for transfers between devices: 1.75 us -> 0.01 us  [on_device(): lax.ppermute(low_side, 'high', [(i, (i - 1) % 4) for i in range(4)])]
  transfers between devices with their start and end apart: 8 -> 6, of which waited for: 6 -> 3; matrix products, arithmetic and copies ran while one was open for 0% -> 0% of each run, Pallas kernels for 4% -> 4%
where the time goes in v4:
time: 141 us
  starting transfers between devices  64.3 us (46%)
  waiting for transfers between devices  31.7 us (22%)
  blocking collectives  30.8 us (22%)
  Pallas kernels  11 us (8%)
  local copies, waits for them, and re-layouts  2.62 us (2%)
    all_to_all x1, starting transfers between devices, on_device(): line_parts = lax.all_to_all(parts, LINE, 0, 0)  29.3 us
    all_to_all x1, blocking collectives, on_device(): plane_parts = lax.all_to_all(dense, PLANE, 0, 0)  18 us
    all_to_all x1, waiting for transfers between devices, on_device(): row_parts = lax.all_to_all(terms, LINE, 0, 0)  16.8 us
    all_to_all x1, starting transfers between devices, on_device(): row_parts = lax.all_to_all(terms, LINE, 0, 0)  14.9 us
    all_to_all x1, blocking collectives, to_all(): return lax.all_to_all(copies, axes, 0, 0)  12.8 us
    all_to_all x1, waiting for transfers between devices, on_device(): line_parts = lax.all_to_all(parts, LINE, 0, 0)  12.7 us
    pallas_call x5, Pallas kernels, call(): pl.pallas_call(kernel, out_shape=jax.ShapeDtypeStruct(out_shape, jnp.floa...  11 us
    ppermute x1, starting transfers between devices, on_device(): lax.ppermute(low_side, 'high', [(i, (i - 1) % 4) for i in range(4)])  9.4 us
  transfers between devices with their start and end apart: 6, of which 3 were waited for; matrix products, arithmetic and copies ran while one was open for 0% of the time, Pallas kernels for 4%

profile of v4, /device:TPU:1, one launch (start us, length us, event | category | flops | bytes accessed | tf_op | source)
XLA Modules:
  0.0 140.8 jit_solution(4010680586987679802)
XLA Ops:
  0.0 0.7 copy-done.3
  0.7 1.0 copy-done
  1.7 1.3 shard_map.73
  3.1 29.3 %all-to-all-start = ((f32[32,1,128]{2,1,0:T(1,128)}), f32[32,1,128]{2,1,0:T(1,128)S(1)}, u32[]{:S(2)}, u32[]{:S(2)}) async-start(f32[32,1,128]{2,1,0:T(1,128)} %shard_map.73), calls=%async_computation | async-start | bytes 32768 | tf_op jit(solution)/shard_map/all_to_all | solution.py:238
  32.4 2.9 %collective-permute-start = (f32[2,1,32,128]{3,2,1,0:T(8,128)S(1)}, f32[2,1,32,128]{3,2,1,0:T(8,128)S(1)}, u32[]{:S(2)}, u32[]{:S(2)}) collective-permute-start(f32[2,1,32,128]{3,2,1,0:T(8,128)S(1)} %get-tuple-element.20), channel_id=1, source_target_pairs={{0,4},{4,0},{8,12},{12,8},{16,20},{20,16},{24,28},{28,24},{32,36},... | collective-permute-start | bytes 98312 | tf_op jit(solution)/shard_map/ppermute | solution.py:239
  35.2 3.3 %collective-permute-start.1 = (f32[2,1,32,128]{3,2,1,0:T(8,128)S(1)}, f32[2,1,32,128]{3,2,1,0:T(8,128)S(1)}, u32[]{:S(2)}, u32[]{:S(2)}) collective-permute-start(f32[2,1,32,128]{3,2,1,0:T(8,128)S(1)} %get-tuple-element.21), channel_id=1, source_target_pairs={{0,1020},{4,8},{8,4},{12,16},{16,12},{20,24},{24,20},{28,32},{32,2... | collective-permute-start | bytes 98312 | tf_op jit(solution)/shard_map/ppermute | solution.py:240
  38.6 0.0 collective-permute-done
  38.6 2.2 %collective-permute-done.1 = f32[2,1,32,128]{3,2,1,0:T(8,128)S(1)} collective-permute-done((f32[2,1,32,128]{3,2,1,0:T(8,128)S(1)}, f32[2,1,32,128]{3,2,1,0:T(8,128)S(1)}, u32[]{:S(2)}, u32[]{:S(2)}) %collective-permute-start.1) | collective-permute-done | bytes 32800 | tf_op jit(solution)/shard_map/ppermute | solution.py:240
  40.8 12.7 %all-to-all-done.parts_ref = f32[32,1,128]{2,1,0:T(1,128)S(1)} async-done(((f32[32,1,128]{2,1,0:T(1,128)}), f32[32,1,128]{2,1,0:T(1,128)S(1)}, u32[]{:S(2)}, u32[]{:S(2)}) %all-to-all-start) | async-done | bytes 16416 | tf_op jit(solution)/shard_map/all_to_all | solution.py:238
  53.6 2.2 %shard_map.74 = f32[32,16,128]{2,1,0:T(8,128)S(1)} custom-call(s32[1]{0:T(128)} %bitcast.1.slab_ref, f32[32,1,128]{2,1,0:T(1,128)S(1)} %all-to-all-done.parts_ref), custom_call_target="tpu_custom_call" | custom-call | tf_op jit(solution)/shard_map/pallas_call | solution.py:206
  55.9 0.0 copy-start.7
  55.9 0.0 copy-start.6
  55.9 18.0 %all_to_all.20.parts_ref = f32[32,16,128]{2,1,0:T(8,128)S(1)} all-to-all(f32[32,16,128]{2,1,0:T(8,128)S(1)} %shard_map.74), channel_id=1, replica_groups=mesh['y'=4,'x'=4,'low'=8,'core'=2,'high'=4] {'y','x','core'}, dimensions={0} | all-to-all | bytes 524288 | tf_op jit(solution)/shard_map/all_to_all | solution.py:248
  73.9 4.6 %collective-permute-start.2 = (f32[2,18,1,128]{3,2,1,0:T(1,128)S(1)}, f32[2,18,1,128]{3,2,1,0:T(1,128)S(1)}, u32[]{:S(2)}, u32[]{:S(2)}) collective-permute-start(f32[2,18,1,128]{3,2,1,0:T(1,128)S(1)} %pad_maximum_fusion.1), channel_id=1, source_target_pairs={{0,1},{1,2},{2,3},{3,0},{4,5},{5,6},{6,7},{7,4},{8,9},{9,10},{10,1... | collective-permute-start | bytes 55304 | tf_op jit(solution)/shard_map/ppermute | solution.py:253
  78.5 9.4 %collective-permute-start.3 = (f32[2,18,1,128]{3,2,1,0:T(1,128)S(1)}, f32[2,18,1,128]{3,2,1,0:T(1,128)S(1)}, u32[]{:S(2)}, u32[]{:S(2)}) collective-permute-start(f32[2,18,1,128]{3,2,1,0:T(1,128)S(1)} %pad_maximum_fusion), channel_id=1, source_target_pairs={{0,3},{1,0},{2,1},{3,2},{4,7},{5,4},{6,5},{7,6},{8,11},{9,8},{10,9... | collective-permute-start | bytes 55304 | tf_op jit(solution)/shard_map/ppermute | solution.py:254
  87.9 0.0 copy-start.2
  88.0 0.8 copy-done.2
  88.8 0.8 shard_map.75
  89.5 14.9 %all-to-all-start.2 = ((f32[32,2,128]{2,1,0:T(2,128)}), f32[32,2,128]{2,1,0:T(2,128)S(1)}, u32[]{:S(2)}, u32[]{:S(2)}) async-start(f32[32,2,128]{2,1,0:T(2,128)} %shard_map.75), calls=%async_computation.2 | async-start | bytes 65536 | tf_op jit(solution)/shard_map/all_to_all | solution.py:252
  104.4 0.0 collective-permute-done.2.y_low_ref
  104.5 5.2 %shard_map.76.local_ref = f32[2,16,32,128]{3,2,1,0:T(8,128)S(1)} custom-call(f32[2,16,32,128]{3,2,1,0:T(8,128)S(1)} %copy-done.1, f32[2,1,32,128]{3,2,1,0:T(8,128)S(1)} %get-tuple-element.37.x_low_ref, f32[2,1,32,128]{3,2,1,0:T(8,128)S(1)} %get-tuple-element.38.x_high_ref, f32[2,18,1,128]{3,2,1,0:T(1,128)S(1)} %collective-permute-done.2.y_low_ref, ...), custom_call_target="tpu_custom_call" | custom-call | flops 30000001024 | bytes 1048576 | tf_op jit(solution)/shard_map/pallas_call | solution.py:206
  109.6 16.8 %all-to-all-done.2 = f32[32,2,128]{2,1,0:T(2,128)S(1)} async-done(((f32[32,2,128]{2,1,0:T(2,128)}), f32[32,2,128]{2,1,0:T(2,128)S(1)}, u32[]{:S(2)}, u32[]{:S(2)}) %all-to-all-start.2) | async-done | bytes 32800 | tf_op jit(solution)/shard_map/all_to_all | solution.py:252
  126.5 12.8 %all_to_all.21.coarse_ref = f32[32,2,128]{2,1,0:T(2,128)S(1)} all-to-all(f32[32,2,128]{2,1,0:T(2,128)S(1)} %broadcast_in_dim.2), channel_id=1, replica_groups=mesh['y'=4,'x'=4,'low'=8,'core'=2,'high'=4] {'y','x','core'}, dimensions={0} | all-to-all | bytes 65536 | tf_op jit(solution)/shard_map/all_to_all | solution.py:220
  139.3 1.5 %shard_map.77 = f32[2,16,32,128]{3,2,1,0:T(8,128)} custom-call(s32[1,2,8]{2,1,0:T(2,128)S(1)} %copy-done.3, f32[2,16,32,128]{3,2,1,0:T(8,128)S(1)} %shard_map.76.local_ref, f32[32,2,128]{2,1,0:T(2,128)S(1)} %all_to_all.21.coarse_ref), custom_call_target="tpu_custom_call" | custom-call | tf_op jit(solution)/shard_map/pallas_call | solution.py:206
  (21 shorter events, 0.2 us)
Async XLA Ops:
  0.0 0.7 copy-start.3
  0.7 1.0 copy-start
  1.7 36.8 %copy-start.1 = (f32[2,16,32,128]{3,2,1,0:T(8,128)S(1)}, f32[2,16,32,128]{3,2,1,0:T(8,128)}, u32[]{:S(2)}) copy-start(f32[2,16,32,128]{3,2,1,0:T(8,128)} %residual_ref.3) | copy-start | bytes 1572868
  3.1 50.5 %all-to-all-start = ((f32[32,1,128]{2,1,0:T(1,128)}), f32[32,1,128]{2,1,0:T(1,128)S(1)}, u32[]{:S(2)}, u32[]{:S(2)}) async-start(f32[32,1,128]{2,1,0:T(1,128)} %shard_map.73), calls=%async_computation | async-start | bytes 32768 | tf_op jit(solution)/shard_map/all_to_all | solution.py:238
  32.4 6.2 %collective-permute-start = (f32[2,1,32,128]{3,2,1,0:T(8,128)S(1)}, f32[2,1,32,128]{3,2,1,0:T(8,128)S(1)}, u32[]{:S(2)}, u32[]{:S(2)}) collective-permute-start(f32[2,1,32,128]{3,2,1,0:T(8,128)S(1)} %get-tuple-element.20), channel_id=1, source_target_pairs={{0,4},{4,0},{8,12},{12,8},{16,20},{20,16},{24,28},{28,24},{32,36},... | collective-permute-start | bytes 98312 | tf_op jit(solution)/shard_map/ppermute | solution.py:239
  35.2 5.6 %collective-permute-start.1 = (f32[2,1,32,128]{3,2,1,0:T(8,128)S(1)}, f32[2,1,32,128]{3,2,1,0:T(8,128)S(1)}, u32[]{:S(2)}, u32[]{:S(2)}) collective-permute-start(f32[2,1,32,128]{3,2,1,0:T(8,128)S(1)} %get-tuple-element.21), channel_id=1, source_target_pairs={{0,1020},{4,8},{8,4},{12,16},{16,12},{20,24},{24,20},{28,32},{32,2... | collective-permute-start | bytes 98312 | tf_op jit(solution)/shard_map/ppermute | solution.py:240
  55.9 32.0 %copy-start.7 = (f32[2,18,18]{2,0,1:T(2,128)S(1)}, f32[2,18,18]{2,0,1:T(2,128)}, u32[]{:S(2)}) copy-start(f32[2,18,18]{2,0,1:T(2,128)} %param.8) | copy-start | bytes 7780
  55.9 32.0 %copy-start.6 = (f32[8,18,18]{2,0,1:T(8,128)S(1)}, f32[8,18,18]{2,0,1:T(8,128)}, u32[]{:S(2)}) copy-start(f32[8,18,18]{2,0,1:T(8,128)} %param.10) | copy-start | bytes 31108
  73.9 30.5 %collective-permute-start.2 = (f32[2,18,1,128]{3,2,1,0:T(1,128)S(1)}, f32[2,18,1,128]{3,2,1,0:T(1,128)S(1)}, u32[]{:S(2)}, u32[]{:S(2)}) collective-permute-start(f32[2,18,1,128]{3,2,1,0:T(1,128)S(1)} %pad_maximum_fusion.1), channel_id=1, source_target_pairs={{0,1},{1,2},{2,3},{3,0},{4,5},{5,6},{6,7},{7,4},{8,9},{9,10},{10,1... | collective-permute-start | bytes 55304 | tf_op jit(solution)/shard_map/ppermute | solution.py:253
  78.5 25.9 %collective-permute-start.3 = (f32[2,18,1,128]{3,2,1,0:T(1,128)S(1)}, f32[2,18,1,128]{3,2,1,0:T(1,128)S(1)}, u32[]{:S(2)}, u32[]{:S(2)}) collective-permute-start(f32[2,18,1,128]{3,2,1,0:T(1,128)S(1)} %pad_maximum_fusion), channel_id=1, source_target_pairs={{0,3},{1,0},{2,1},{3,2},{4,7},{5,4},{6,5},{7,6},{8,11},{9,8},{10,9... | collective-permute-start | bytes 55304 | tf_op jit(solution)/shard_map/ppermute | solution.py:254
  87.9 0.8 copy-start.2
  89.5 14.9 %copy-start.4 = (f32[8,18]{1,0:T(8,128)S(1)}, f32[8,18]{1,0:T(8,128)}, u32[]{:S(2)}) copy-start(f32[8,18]{1,0:T(8,128)} %upward_values_ref.1) | copy-start | bytes 1732
  89.5 14.9 %copy-start.5 = (f32[2,18]{1,0:T(2,128)S(1)}, f32[2,18]{1,0:T(2,128)}, u32[]{:S(2)}) copy-start(f32[2,18]{1,0:T(2,128)} %horiz_values_ref.1) | copy-start | bytes 436
  89.5 36.9 %all-to-all-start.2 = ((f32[32,2,128]{2,1,0:T(2,128)}), f32[32,2,128]{2,1,0:T(2,128)S(1)}, u32[]{:S(2)}, u32[]{:S(2)}) async-start(f32[32,2,128]{2,1,0:T(2,128)} %shard_map.75), calls=%async_computation.2 | async-start | bytes 65536 | tf_op jit(solution)/shard_map/all_to_all | solution.py:252

commit v5 on v4

--- a/solution.py
+++ b/solution.py
@@ -14,7 +14,6 @@
 PLANE = ("y", "x", "core")
 LINE = ("high", "low")
 LINE_SIZE = 32
-LOCAL_FLOPS = 30000000000
 PLANE_SIZE = 32
 
 
@@ -81,13 +80,15 @@
             message = jnp.where(lane == slot, total[0:1] * WEIGHT, message)
             message = jnp.where(lane == slot + 16, total[1:2] * WEIGHT, message)
             message = jnp.where(lane == slot + 32, label, message)
-    out_ref[...] = jnp.broadcast_to(message[None], out_ref.shape)
-
-
-def scatter_kernel(slab_ref, parts_ref, out_ref):
-    parts = parts_ref[...].reshape(LINE_SIZE, 128)
+    out_ref[:, 0:1, :] = jnp.broadcast_to(message[None], (LINE_SIZE, 1, 128))
+    out_ref[:, 1, :] = residual_ref[:, :, 2 * SPAN - 1, :].reshape(LINE_SIZE, 128)
+    out_ref[:, 2, :] = residual_ref[:, :, 0, :].reshape(LINE_SIZE, 128)
+
+
+def scatter_kernel(spots_ref, parts_ref, out_ref):
+    parts = parts_ref[:, 0, :]
     lane = iota((LINE_SIZE, 128), 1)
-    block = (lane & 7) + slab_ref[0] * 8
+    block = (lane & 7) + (spots_ref[0] >> 3) * 8
     values, places = [], []
     for e in range(16):
         first, second, label = (
@@ -103,24 +104,32 @@
     out_ref[...] = jnp.broadcast_to(rows[None], out_ref.shape)
 
 
-def terms_kernel(place_ref, parts_ref, matrix_ref, out_ref):
+def terms_kernel(spots_ref, parts_ref, line_ref, x_low_ref, x_high_ref, matrix_ref, out_ref):
     rhs = jnp.sum(parts_ref[...], axis=0)
     lane = iota((SPAN, 128), 1) - iota((SPAN, 128), 0)
-    here = lane == place_ref[0] * SPAN
-    terms = []
+    here = lane == (spots_ref[0] & 7) * SPAN
     for v in range(2):
         total = jnp.zeros((SPAN, 128), jnp.float32)
         for block in range(8):
             row = v * 8 + block
             total = total + matrix_ref[:, block * 128 : (block + 1) * 128] * rhs[row : row + 1]
         column = jnp.sum(total, axis=1, keepdims=True)
-        terms.append(jnp.sum(jnp.where(here, column, 0.0), axis=0, keepdims=True))
-    terms = jnp.concatenate(terms, axis=0)
-    out_ref[...] = jnp.broadcast_to(terms[None], out_ref.shape)
+        terms = jnp.sum(jnp.where(here, column, 0.0), axis=0, keepdims=True)
+        out_ref[:, v, :] = jnp.broadcast_to(terms, (LINE_SIZE, 128))
+    out_ref[0:8, 2, :] = line_ref[24:32, 1, :]
+    out_ref[8:32, 2, :] = line_ref[0:24, 1, :]
+    out_ref[0:24, 3, :] = line_ref[8:32, 2, :]
+    out_ref[24:32, 3, :] = line_ref[0:8, 2, :]
+    out_ref[:, 4:8, :] = jnp.zeros((LINE_SIZE, 4, 128), jnp.float32)
+    for spot, edge in ((1, 0), (2, 2 * SPAN - 1)):
+        corners = [
+            side_ref[v, 0, edge : edge + 1, :] for v in range(2) for side_ref in (x_low_ref, x_high_ref)
+        ]
+        out_ref[spots_ref[spot], 4:8, :] = jnp.concatenate(corners, axis=0)
 
 
 def local_kernel(
-    residual_ref, x_low_ref, x_high_ref, y_low_ref, y_high_ref,
+    spots_ref, residual_ref, x_low_ref, x_high_ref, line_parts_ref,
     horiz_ref, horiz_values_ref, upward_ref, upward_values_ref,
     out_ref, box_ref, hat_ref, line_ref, line_values_ref,
 ):
@@ -167,9 +176,12 @@
             box_ref[272:288, lanes] = x_high_ref[v, 0, ys, :]
             box_ref[304:312, lanes] = jnp.zeros((8, 128), jnp.float32)
             box_ref[328:336, lanes] = jnp.zeros((8, 128), jnp.float32)
-            for begin, edge, outer in ((288, 15, y_low_ref), (312, 16, y_high_ref)):
+            for begin, edge, spot in ((288, 15, 1), (312, 16, 2)):
                 if (edge == 15) == (j == 0):
-                    box_ref[begin : begin + 18, lanes] = outer[v, :, 0, :]
+                    corner, rows = line_parts_ref[spots_ref[spot]], slice(SPAN * v, SPAN * v + SPAN)
+                    box_ref[begin : begin + 1, lanes] = corner[4 + 2 * v : 5 + 2 * v]
+                    box_ref[begin + 1 : begin + 17, lanes] = line_parts_ref[rows, spot + 1, :]
+                    box_ref[begin + 17 : begin + 18, lanes] = corner[5 + 2 * v : 6 + 2 * v]
                 else:
                     box_ref[begin : begin + 1, lanes] = x_low_ref[v, 0, edge : edge + 1, :]
                     box_ref[begin + 1 : begin + 17, lanes] = residual_ref[v, :, edge, :]
@@ -202,7 +214,7 @@
             out_ref[v, :, ys, :] = local_ref[v, :, ys, :] + update[v : v + 1][None]
 
 
-def call(kernel, out_shape, scalars, arrays, scratch=(), cost=None):
+def call(kernel, out_shape, scalars, arrays, scratch=()):
     return pl.pallas_call(
         kernel,
         out_shape=jax.ShapeDtypeStruct(out_shape, jnp.float32),
@@ -211,7 +223,6 @@
         out_specs=pl.BlockSpec(memory_space=pltpu.VMEM),
         scratch_shapes=list(scratch),
         compiler_params=pltpu.CompilerParams(vmem_limit_bytes=40 << 20),
-        cost_estimate=cost,
     )(*scalars, *arrays)
 
 
@@ -225,12 +236,12 @@
     aggregate_map, coarse_inverse,
 ):
     labels = aggregate_map
-    place = lax.axis_index("low").reshape(1)
-    slab = lax.axis_index("high").reshape(1)
     even = lax.axis_index("core") == 0
+    spot = lax.axis_index("high") * 8 + lax.axis_index("low")
+    spots = (spot + jnp.array([0, 24, 8], jnp.int32)) % LINE_SIZE
     barrier = lax.optimization_barrier
 
-    parts = call(message_kernel, (LINE_SIZE, 1, 128), [labels], [residual])
+    parts = call(message_kernel, (LINE_SIZE, 3, 128), [labels], [residual])
     first, last = residual[:, :1], residual[:, -1:]
     parts, inner, outer = barrier(
         (parts, jnp.where(even, last, first), jnp.where(even, first, last))
@@ -240,28 +251,23 @@
     outer = lax.ppermute(outer, GROUP, [(i, (i + i % 2 * 2 - 1) % 256) for i in range(256)])
     line_parts, inner, outer = barrier((line_parts, inner, outer))
     x_low, x_high = jnp.where(even, outer, inner), jnp.where(even, inner, outer)
-    low_side = jnp.concatenate([x_low[:, :, :1], residual[:, :, :1], x_high[:, :, :1]], axis=1)
-    high_side = jnp.concatenate([x_low[:, :, -1:], residual[:, :, -1:], x_high[:, :, -1:]], axis=1)
-
-    dense = call(scatter_kernel, (PLANE_SIZE, 16, 128), [slab], [line_parts])
-    dense, low_side, high_side = barrier((dense, low_side, high_side))
+
+    dense = call(scatter_kernel, (PLANE_SIZE, 16, 128), [spots], [line_parts])
+    dense, x_low, x_high = barrier((dense, x_low, x_high))
     plane_parts = lax.all_to_all(dense, PLANE, 0, 0)
-    plane_parts, low_side, high_side = barrier((plane_parts, low_side, high_side))
-
-    terms = call(terms_kernel, (LINE_SIZE, 2, 128), [place], [plane_parts, coarse_inverse])
+    terms = call(
+        terms_kernel, (LINE_SIZE, 8, 128), [spots],
+        [plane_parts, line_parts, x_low, x_high, coarse_inverse],
+    )
     row_parts = lax.all_to_all(terms, LINE, 0, 0)
-    y_low = lax.ppermute(high_side, "high", [(i, (i + 1) % 4) for i in range(4)])
-    y_high = lax.ppermute(low_side, "high", [(i, (i - 1) % 4) for i in range(4)])
+    coarse = to_all(row_parts[:, :2].sum(axis=0), PLANE, PLANE_SIZE)
     local = call(
-        local_kernel, residual.shape, [],
-        [residual, x_low, x_high, y_low, y_high, horiz_vectors, horiz_values,
+        local_kernel, residual.shape, [spots],
+        [residual, x_low, x_high, row_parts, horiz_vectors, horiz_values,
          upward_eigen_tables, upward_eigen_values],
         [pltpu.VMEM((POINTS, 512), jnp.float32), pltpu.VMEM((PAIRS, 512), jnp.float32),
          pltpu.VMEM((128, 144), jnp.float32), pltpu.VMEM((1, 144), jnp.float32)],
-        pl.CostEstimate(flops=LOCAL_FLOPS, transcendentals=0, bytes_accessed=1 << 20),
-    )
-    row_parts, local = barrier((row_parts, local))
-    coarse = to_all(row_parts.sum(axis=0), PLANE, PLANE_SIZE)
+    )
     return call(merge_kernel, residual.shape, [labels], [local, coarse])
 
 

time: 141 us -> 136 us (0.965)
  blocking collectives: 30.8 us -> 59.5 us
  starting transfers between devices: 64.3 us -> 41.6 us
  waiting for transfers between devices: 31.7 us -> 18.2 us
    all_to_all x1, blocking collectives: 12.8 us -> 40.7 us  [on_device(): row_parts = lax.all_to_all(terms, LINE, 0, 0)]
    all_to_all x1, waiting for transfers between devices: 16.8 us -> 0.91 us  [to_all(): return lax.all_to_all(copies, axes, 0, 0)]
    ppermute x2 -> x0, starting transfers between devices: 14 us -> none  [the longest x1 9.4 us: on_device(): lax.ppermute(low_side, 'high', [(i, (i - 1) % 4) for i in range(4)])]
    all_to_all x1, starting transfers between devices: 14.9 us -> 6.16 us  [to_all(): return lax.all_to_all(copies, axes, 0, 0)]
    all_to_all x1, waiting for transfers between devices: 12.7 us -> 15.4 us  [on_device(): line_parts = lax.all_to_all(parts, LINE, 0, 0)]
    unnamed x18 -> x20, local copies, waits for them, and re-layouts: 2.57 us -> 3.05 us
  transfers between devices with their start and end apart: 6 -> 4, of which waited for: 3 -> 3; matrix products, arithmetic and copies ran while one was open for 0% -> 0% of each run, Pallas kernels for 4% -> 4%
where the time goes in v5:
time: 136 us; the launch traced here: 135 us
  blocking collectives  59.5 us (44%)
  starting transfers between devices  41.6 us (31%)
  waiting for transfers between devices  18.2 us (13%)
  Pallas kernels  12 us (9%)
  local copies, waits for them, and re-layouts  3.68 us (3%)
    all_to_all x1, blocking collectives, on_device(): row_parts = lax.all_to_all(terms, LINE, 0, 0)  40.7 us
    all_to_all x1, starting transfers between devices, on_device(): line_parts = lax.all_to_all(parts, LINE, 0, 0)  29.3 us
    all_to_all x1, blocking collectives, on_device(): plane_parts = lax.all_to_all(dense, PLANE, 0, 0)  18.7 us
    all_to_all x1, waiting for transfers between devices, on_device(): line_parts = lax.all_to_all(parts, LINE, 0, 0)  15.4 us
    pallas_call x5, Pallas kernels, call(): pl.pallas_call(kernel, out_shape=jax.ShapeDtypeStruct(out_shape, jnp.floa...  12 us
    all_to_all x1, starting transfers between devices, to_all(): return lax.all_to_all(copies, axes, 0, 0)  6.16 us
    ppermute x1, starting transfers between devices, on_device(): lax.ppermute(outer, GROUP, [(i, (i + i % 2 * 2 - 1) % 256) for i in range...  3.32 us
    unnamed x20, local copies, waits for them, and re-layouts  3.05 us
  transfers between devices with their start and end apart: 4, of which 3 were waited for; matrix products, arithmetic and copies ran while one was open for 0% of the time, Pallas kernels for 4%

profile of v5, /device:TPU:1, one launch (start us, length us, event | category | flops | bytes accessed | tf_op | source)
XLA Modules:
  0.0 135.2 jit_solution(16586936900505872805)
XLA Ops:
  0.0 0.7 copy-done.4
  0.7 1.0 copy-done
  1.7 1.3 shard_map.82
  3.1 29.3 %all-to-all-start = ((f32[32,3,128]{2,1,0:T(4,128)}), f32[32,3,128]{2,1,0:T(4,128)S(1)}, u32[]{:S(2)}, u32[]{:S(2)}) async-start(f32[32,3,128]{2,1,0:T(4,128)} %shard_map.82), calls=%async_computation | async-start | bytes 131072 | tf_op jit(solution)/shard_map/all_to_all | solution.py:249
  32.4 2.9 %collective-permute-start = (f32[2,1,32,128]{3,2,1,0:T(8,128)S(1)}, f32[2,1,32,128]{3,2,1,0:T(8,128)S(1)}, u32[]{:S(2)}, u32[]{:S(2)}) collective-permute-start(f32[2,1,32,128]{3,2,1,0:T(8,128)S(1)} %get-tuple-element.15), channel_id=1, source_target_pairs={{0,4},{4,0},{8,12},{12,8},{16,20},{20,16},{24,28},{28,24},{32,36},... | collective-permute-start | bytes 98312 | tf_op jit(solution)/shard_map/ppermute | solution.py:250
  35.3 3.3 %collective-permute-start.1 = (f32[2,1,32,128]{3,2,1,0:T(8,128)S(1)}, f32[2,1,32,128]{3,2,1,0:T(8,128)S(1)}, u32[]{:S(2)}, u32[]{:S(2)}) collective-permute-start(f32[2,1,32,128]{3,2,1,0:T(8,128)S(1)} %get-tuple-element.16), channel_id=1, source_target_pairs={{0,1020},{4,8},{8,4},{12,16},{16,12},{20,24},{24,20},{28,32},{32,2... | collective-permute-start | bytes 98312 | tf_op jit(solution)/shard_map/ppermute | solution.py:251
  38.6 0.0 copy-start.8
  38.6 0.6 copy-done.8
  39.3 1.9 %collective-permute-done.1 = f32[2,1,32,128]{3,2,1,0:T(8,128)S(1)} collective-permute-done((f32[2,1,32,128]{3,2,1,0:T(8,128)S(1)}, f32[2,1,32,128]{3,2,1,0:T(8,128)S(1)}, u32[]{:S(2)}, u32[]{:S(2)}) %collective-permute-start.1) | collective-permute-done | bytes 32800 | tf_op jit(solution)/shard_map/ppermute | solution.py:251
  41.2 15.4 %all-to-all-done.parts_ref.line_ref = f32[32,3,128]{2,1,0:T(4,128)S(1)} async-done(((f32[32,3,128]{2,1,0:T(4,128)}), f32[32,3,128]{2,1,0:T(4,128)S(1)}, u32[]{:S(2)}, u32[]{:S(2)}) %all-to-all-start) | async-done | bytes 49184 | tf_op jit(solution)/shard_map/all_to_all | solution.py:249
  56.5 2.8 %shard_map.83 = f32[32,16,128]{2,1,0:T(8,128)S(1)} custom-call(s32[3]{0:T(128)S(1)} %and_select_fusion.spots_ref, f32[32,3,128]{2,1,0:T(4,128)S(1)} %all-to-all-done.parts_ref.line_ref), custom_call_target="tpu_custom_call" | custom-call | tf_op jit(solution)/shard_map/pallas_call | solution.py:218
  59.3 0.0 copy-start.2
  59.3 18.7 %all_to_all.20.parts_ref = f32[32,16,128]{2,1,0:T(8,128)S(1)} all-to-all(f32[32,16,128]{2,1,0:T(8,128)S(1)} %shard_map.83), channel_id=1, replica_groups=mesh['y'=4,'x'=4,'low'=8,'core'=2,'high'=4] {'y','x','core'}, dimensions={0} | all-to-all | bytes 524288 | tf_op jit(solution)/shard_map/all_to_all | solution.py:257
  78.1 0.7 shard_map.84
  78.8 40.7 %all_to_all.21.line_parts_ref = f32[32,8,128]{2,1,0:T(8,128)S(1)} all-to-all(f32[32,8,128]{2,1,0:T(8,128)S(1)} %shard_map.84), channel_id=1, replica_groups=mesh['y'=4,'x'=4,'low'=8,'core'=2,'high'=4] {'high','low'}, dimensions={0} | all-to-all | bytes 262144 | tf_op jit(solution)/shard_map/all_to_all | solution.py:262
  119.5 0.6 broadcast_in_dim.2
  120.2 6.2 %all-to-all-start.3 = ((f32[32,2,128]{2,1,0:T(2,128)}), f32[32,2,128]{2,1,0:T(2,128)S(1)}, u32[]{:S(2)}, u32[]{:S(2)}) async-start(f32[32,2,128]{2,1,0:T(2,128)} %broadcast_in_dim.2), calls=%async_computation.3 | async-start | bytes 65536 | tf_op jit(solution)/shard_map/all_to_all | solution.py:231
  126.4 0.0 copy-start.3
  126.4 0.0 copy-start.5
  126.4 0.6 copy-done.3
  127.1 0.0 copy-done.5
  127.1 5.7 %shard_map.85.local_ref = f32[2,16,32,128]{3,2,1,0:T(8,128)S(1)} custom-call(s32[3]{0:T(128)S(1)} %and_select_fusion.spots_ref, f32[2,16,32,128]{3,2,1,0:T(8,128)S(1)} %copy-done.1, f32[2,1,32,128]{3,2,1,0:T(8,128)S(1)} %get-tuple-element.20.x_low_ref, f32[2,1,32,128]{3,2,1,0:T(8,128)S(1)} %get-tuple-element.21.x_high_ref, ...), custom_call_target="tpu_custom_call" | custom-call | tf_op jit(solution)/shard_map/pallas_call | solution.py:218
  132.8 0.9 all-to-all-done.3.coarse_ref
  133.7 1.5 %shard_map.86 = f32[2,16,32,128]{3,2,1,0:T(8,128)} custom-call(s32[1,2,8]{2,1,0:T(2,128)S(1)} %copy-done.4, f32[2,16,32,128]{3,2,1,0:T(8,128)S(1)} %shard_map.85.local_ref, f32[32,2,128]{2,1,0:T(2,128)S(1)} %all-to-all-done.3.coarse_ref), custom_call_target="tpu_custom_call" | custom-call | tf_op jit(solution)/shard_map/pallas_call | solution.py:218
  (16 shorter events, 0.1 us)
Async XLA Ops:
  0.0 0.7 copy-start.4
  0.7 1.0 copy-start
  3.1 53.4 %all-to-all-start = ((f32[32,3,128]{2,1,0:T(4,128)}), f32[32,3,128]{2,1,0:T(4,128)S(1)}, u32[]{:S(2)}, u32[]{:S(2)}) async-start(f32[32,3,128]{2,1,0:T(4,128)} %shard_map.82), calls=%async_computation | async-start | bytes 131072 | tf_op jit(solution)/shard_map/all_to_all | solution.py:249
  32.4 6.9 %collective-permute-start = (f32[2,1,32,128]{3,2,1,0:T(8,128)S(1)}, f32[2,1,32,128]{3,2,1,0:T(8,128)S(1)}, u32[]{:S(2)}, u32[]{:S(2)}) collective-permute-start(f32[2,1,32,128]{3,2,1,0:T(8,128)S(1)} %get-tuple-element.15), channel_id=1, source_target_pairs={{0,4},{4,0},{8,12},{12,8},{16,20},{20,16},{24,28},{28,24},{32,36},... | collective-permute-start | bytes 98312 | tf_op jit(solution)/shard_map/ppermute | solution.py:250
  35.3 5.9 %collective-permute-start.1 = (f32[2,1,32,128]{3,2,1,0:T(8,128)S(1)}, f32[2,1,32,128]{3,2,1,0:T(8,128)S(1)}, u32[]{:S(2)}, u32[]{:S(2)}) collective-permute-start(f32[2,1,32,128]{3,2,1,0:T(8,128)S(1)} %get-tuple-element.16), channel_id=1, source_target_pairs={{0,1020},{4,8},{8,4},{12,16},{16,12},{20,24},{24,20},{28,32},{32,2... | collective-permute-start | bytes 98312 | tf_op jit(solution)/shard_map/ppermute | solution.py:251
  38.6 0.7 copy-start.8
  59.3 18.8 %copy-start.2 = (f32[16,1024]{1,0:T(8,128)S(1)}, f32[16,1024]{1,0:T(8,128)}, u32[]{:S(2)}) copy-start(f32[16,1024]{1,0:T(8,128)} %matrix_ref.1) | copy-start | bytes 196612
  78.1 48.3 %copy-start.1 = (f32[2,16,32,128]{3,2,1,0:T(8,128)S(1)}, f32[2,16,32,128]{3,2,1,0:T(8,128)}, u32[]{:S(2)}) copy-start(f32[2,16,32,128]{3,2,1,0:T(8,128)} %residual_ref.3) | copy-start | bytes 1572868
  119.5 6.8 %copy-start.6 = (f32[8,18,18]{2,0,1:T(8,128)S(1)}, f32[8,18,18]{2,0,1:T(8,128)}, u32[]{:S(2)}) copy-start(f32[8,18,18]{2,0,1:T(8,128)} %param.11) | copy-start | bytes 31108
  120.2 6.2 %copy-start.7 = (f32[2,18,18]{2,0,1:T(2,128)S(1)}, f32[2,18,18]{2,0,1:T(2,128)}, u32[]{:S(2)}) copy-start(f32[2,18,18]{2,0,1:T(2,128)} %param.9) | copy-start | bytes 7780
  120.2 13.5 %all-to-all-start.3 = ((f32[32,2,128]{2,1,0:T(2,128)}), f32[32,2,128]{2,1,0:T(2,128)S(1)}, u32[]{:S(2)}, u32[]{:S(2)}) async-start(f32[32,2,128]{2,1,0:T(2,128)} %broadcast_in_dim.2), calls=%async_computation.3 | async-start | bytes 65536 | tf_op jit(solution)/shard_map/all_to_all | solution.py:231
  126.4 0.7 copy-start.3
  126.4 0.7 copy-start.5

commit v6 on v5

--- a/solution.py
+++ b/solution.py
@@ -14,6 +14,7 @@
 PLANE = ("y", "x", "core")
 LINE = ("high", "low")
 LINE_SIZE = 32
+WINDOW_FLOPS = 1000000000
 PLANE_SIZE = 32
 
 
@@ -128,10 +129,34 @@
         out_ref[spots_ref[spot], 4:8, :] = jnp.concatenate(corners, axis=0)
 
 
-def local_kernel(
-    spots_ref, residual_ref, x_low_ref, x_high_ref, line_parts_ref,
-    horiz_ref, horiz_values_ref, upward_ref, upward_values_ref,
-    out_ref, box_ref, hat_ref, line_ref, line_values_ref,
+def prepare_kernel(
+    residual_ref, x_low_ref, x_high_ref, horiz_ref, high_ref, low_ref, hat_ref, box_ref
+):
+    x_of, y_of = point_index((POINTS, EXTENT), 0)
+    mode = iota((POINTS, EXTENT), 1)
+    pair_a, pair_b = pair_index((EXTENT, PAIRS), 1)
+    table = iota((EXTENT, PAIRS), 0)
+    pick_a = jnp.where(pair_a == table, 1.0, 0.0)
+    pick_b = jnp.where((pair_b == table) & (pair_a < EXTENT), 1.0, 0.0)
+    rows_x = exact(jnp.where(x_of == mode, 1.0, 0.0), exact(horiz_ref[0], pick_a))
+    rows_y = exact(jnp.where(y_of == mode, 1.0, 0.0), exact(horiz_ref[1], pick_b))
+    high, low = split(rows_x * rows_y)
+    high_ref[...] = high
+    low_ref[...] = low
+    for v in range(2):
+        for j in range(2):
+            lanes = slice(128 * (2 * v + j), 128 * (2 * v + j + 1))
+            ys = slice(j * SPAN, (j + 1) * SPAN)
+            box_ref[0:256, lanes] = residual_ref[v, :, ys, :].reshape(256, 128)
+            box_ref[256:272, lanes] = x_low_ref[v, 0, ys, :]
+            box_ref[272:288, lanes] = x_high_ref[v, 0, ys, :]
+    hat_ref[...] = dot3((high[:288], low[:288]), split(box_ref[...]), ((0,), (0,)))
+
+
+def finish_kernel(
+    spots_ref, residual_ref, x_low_ref, x_high_ref, line_parts_ref, high_ref, low_ref, hat_ref,
+    horiz_values_ref, upward_ref, upward_values_ref,
+    out_ref, box_ref, line_ref, line_values_ref,
 ):
     line_ref[...] = jnp.zeros_like(line_ref)
     for k in range(8):
@@ -146,17 +171,6 @@
     line_own = split(jnp.where((z >> 4) == layer, line, 0.0))
     line = split(line)
 
-    x_of, y_of = point_index((POINTS, EXTENT), 0)
-    mode = iota((POINTS, EXTENT), 1)
-    pair_a, pair_b = pair_index((EXTENT, PAIRS), 1)
-    table = iota((EXTENT, PAIRS), 0)
-    pick_a = jnp.where(pair_a == table, 1.0, 0.0)
-    pick_b = jnp.where((pair_b == table) & (pair_a < EXTENT), 1.0, 0.0)
-    rows_x = exact(jnp.where(x_of == mode, 1.0, 0.0), exact(horiz_ref[0], pick_a))
-    rows_y = exact(jnp.where(y_of == mode, 1.0, 0.0), exact(horiz_ref[1], pick_b))
-    plane = split(rows_x * rows_y)
-    plane_own = (plane[0][:256], plane[1][:256])
-
     pair_first, pair_second = pair_index((PAIRS, EXTENT), 0)
     table = iota((PAIRS, EXTENT), 1)
     values = jnp.sum(
@@ -168,17 +182,13 @@
     inverse = 1.0 / (values + line_values_ref[...])
 
     for v in range(2):
+        rows = slice(SPAN * v, SPAN * v + SPAN)
         for j in range(2):
             lanes = slice(128 * (2 * v + j), 128 * (2 * v + j + 1))
-            ys = slice(j * SPAN, (j + 1) * SPAN)
-            box_ref[0:256, lanes] = residual_ref[v, :, ys, :].reshape(256, 128)
-            box_ref[256:272, lanes] = x_low_ref[v, 0, ys, :]
-            box_ref[272:288, lanes] = x_high_ref[v, 0, ys, :]
-            box_ref[304:312, lanes] = jnp.zeros((8, 128), jnp.float32)
-            box_ref[328:336, lanes] = jnp.zeros((8, 128), jnp.float32)
-            for begin, edge, spot in ((288, 15, 1), (312, 16, 2)):
+            for begin, edge, spot in ((0, 15, 1), (24, 16, 2)):
+                box_ref[begin + 16 : begin + 24, lanes] = jnp.zeros((8, 128), jnp.float32)
                 if (edge == 15) == (j == 0):
-                    corner, rows = line_parts_ref[spots_ref[spot]], slice(SPAN * v, SPAN * v + SPAN)
+                    corner = line_parts_ref[spots_ref[spot]]
                     box_ref[begin : begin + 1, lanes] = corner[4 + 2 * v : 5 + 2 * v]
                     box_ref[begin + 1 : begin + 17, lanes] = line_parts_ref[rows, spot + 1, :]
                     box_ref[begin + 17 : begin + 18, lanes] = corner[5 + 2 * v : 6 + 2 * v]
@@ -186,13 +196,14 @@
                     box_ref[begin : begin + 1, lanes] = x_low_ref[v, 0, edge : edge + 1, :]
                     box_ref[begin + 1 : begin + 17, lanes] = residual_ref[v, :, edge, :]
                     box_ref[begin + 17 : begin + 18, lanes] = x_high_ref[v, 0, edge : edge + 1, :]
-
-    hat_ref[...] = dot3(plane, split(box_ref[...]), ((0,), (0,)))
+    sides = (high_ref[288:336, :], low_ref[288:336, :])
+    own = (high_ref[0:256, :], low_ref[0:256, :])
+    all_hat = hat_ref[...] + dot3(sides, split(box_ref[...]), ((0,), (0,)))
+
     for part in range(4):
-        lanes = slice(128 * part, 128 * (part + 1))
-        hat = dot3(split(hat_ref[:, lanes]), line, ((1,), (0,)))
+        hat = dot3(split(all_hat[:, 128 * part : 128 * (part + 1)]), line, ((1,), (0,)))
         back = dot3(split(hat * inverse), line_own, ((1,), (1,)))
-        solved = dot3(plane_own, split(back), ((1,), (0,)))
+        solved = dot3(own, split(back), ((1,), (0,)))
         v, j = divmod(part, 2)
         out_ref[v, :, j * SPAN : (j + 1) * SPAN, :] = solved.reshape(SPAN, SPAN, 128)
 
@@ -214,15 +225,18 @@
             out_ref[v, :, ys, :] = local_ref[v, :, ys, :] + update[v : v + 1][None]
 
 
-def call(kernel, out_shape, scalars, arrays, scratch=()):
+def call(kernel, out_shape, scalars, arrays, scratch=(), cost=None):
+    if not isinstance(out_shape, list):
+        out_shape = jax.ShapeDtypeStruct(out_shape, jnp.float32)
     return pl.pallas_call(
         kernel,
-        out_shape=jax.ShapeDtypeStruct(out_shape, jnp.float32),
+        out_shape=out_shape,
         in_specs=[pl.BlockSpec(memory_space=pltpu.SMEM)] * len(scalars)
         + [pl.BlockSpec(memory_space=pltpu.VMEM)] * len(arrays),
-        out_specs=pl.BlockSpec(memory_space=pltpu.VMEM),
+        out_specs=jax.tree.map(lambda _: pl.BlockSpec(memory_space=pltpu.VMEM), out_shape),
         scratch_shapes=list(scratch),
         compiler_params=pltpu.CompilerParams(vmem_limit_bytes=40 << 20),
+        cost_estimate=cost,
     )(*scalars, *arrays)
 
 
@@ -249,12 +263,19 @@
     line_parts = lax.all_to_all(parts, LINE, 0, 0)
     inner = lax.ppermute(inner, GROUP, [(i, i ^ 1) for i in range(256)])
     outer = lax.ppermute(outer, GROUP, [(i, (i + i % 2 * 2 - 1) % 256) for i in range(256)])
-    line_parts, inner, outer = barrier((line_parts, inner, outer))
     x_low, x_high = jnp.where(even, outer, inner), jnp.where(even, inner, outer)
 
     dense = call(scatter_kernel, (PLANE_SIZE, 16, 128), [spots], [line_parts])
-    dense, x_low, x_high = barrier((dense, x_low, x_high))
     plane_parts = lax.all_to_all(dense, PLANE, 0, 0)
+    table = jax.ShapeDtypeStruct((POINTS, PAIRS), jnp.bfloat16)
+    prepared = call(
+        prepare_kernel,
+        [table, table, jax.ShapeDtypeStruct((PAIRS, 512), jnp.float32)],
+        [], [residual, x_low, x_high, horiz_vectors],
+        [pltpu.VMEM((288, 512), jnp.float32)],
+        pl.CostEstimate(flops=WINDOW_FLOPS, transcendentals=0, bytes_accessed=1 << 20),
+    )
+    plane_parts, prepared, x_low, x_high = barrier((plane_parts, prepared, x_low, x_high))
     terms = call(
         terms_kernel, (LINE_SIZE, 8, 128), [spots],
         [plane_parts, line_parts, x_low, x_high, coarse_inverse],
@@ -262,11 +283,11 @@
     row_parts = lax.all_to_all(terms, LINE, 0, 0)
     coarse = to_all(row_parts[:, :2].sum(axis=0), PLANE, PLANE_SIZE)
     local = call(
-        local_kernel, residual.shape, [spots],
-        [residual, x_low, x_high, row_parts, horiz_vectors, horiz_values,
+        finish_kernel, residual.shape, [spots],
+        [residual, x_low, x_high, row_parts, *prepared, horiz_values,
          upward_eigen_tables, upward_eigen_values],
-        [pltpu.VMEM((POINTS, 512), jnp.float32), pltpu.VMEM((PAIRS, 512), jnp.float32),
-         pltpu.VMEM((128, 144), jnp.float32), pltpu.VMEM((1, 144), jnp.float32)],
+        [pltpu.VMEM((48, 512), jnp.float32), pltpu.VMEM((128, 144), jnp.float32),
+         pltpu.VMEM((1, 144), jnp.float32)],
     )
     return call(merge_kernel, residual.shape, [labels], [local, coarse])
 

time: 136 us -> 129 us (0.949)
  blocking collectives: 59.5 us -> 34 us
  starting transfers between devices: 41.6 us -> 61.2 us
  waiting for transfers between devices: 18.2 us -> 16.4 us
    all_to_all x1 -> x0, blocking collectives: 18.7 us -> none  [on_device(): plane_parts = lax.all_to_all(dense, PLANE, 0, 0)]
    all_to_all x0 -> x1, starting transfers between devices: none -> 10.1 us  [on_device(): plane_parts = lax.all_to_all(dense, PLANE, 0, 0)]
    ppermute x1, starting transfers between devices: 2.86 us -> 12.4 us  [on_device(): inner = lax.ppermute(inner, GROUP, [(i, i ^ 1) for i in range(256)])]
    all_to_all x1, waiting for transfers between devices: 15.4 us -> 7.19 us  [on_device(): line_parts = lax.all_to_all(parts, LINE, 0, 0)]
    all_to_all x0 -> x1, waiting for transfers between devices: none -> 6.91 us  [on_device(): plane_parts = lax.all_to_all(dense, PLANE, 0, 0)]
    all_to_all x1, blocking collectives: 40.7 us -> 34 us  [on_device(): row_parts = lax.all_to_all(terms, LINE, 0, 0)]
    ppermute x1, waiting for transfers between devices: 1.9 us -> 0.01 us  [on_device(): lax.ppermute(outer, GROUP, [(i, (i + i % 2 * 2 - 1) % 256) for i in range...]
    all_to_all x1, waiting for transfers between devices: 0.91 us -> 2.28 us  [to_all(): return lax.all_to_all(copies, axes, 0, 0)]
  transfers between devices with their start and end apart: 4 -> 5, of which waited for: 3 -> 3; matrix products, arithmetic and copies ran while one was open for 0% -> 0% of each run, Pallas kernels for 4% -> 8%
where the time goes in v6:
time: 129 us; the launch traced here: 128 us
  starting transfers between devices  61.2 us (47%)
  blocking collectives  34 us (26%)
  waiting for transfers between devices  16.4 us (13%)
  Pallas kernels  13.3 us (10%)
  local copies, waits for them, and re-layouts  3.05 us (2%)
    all_to_all x1, blocking collectives, on_device(): row_parts = lax.all_to_all(terms, LINE, 0, 0)  34 us
    all_to_all x1, starting transfers between devices, on_device(): line_parts = lax.all_to_all(parts, LINE, 0, 0)  29.3 us
    pallas_call x6, Pallas kernels, call(): pl.pallas_call(kernel, out_shape=out_shape, in_specs=[pl.BlockSpec(memory...  13.3 us
    ppermute x1, starting transfers between devices, on_device(): inner = lax.ppermute(inner, GROUP, [(i, i ^ 1) for i in range(256)])  12.4 us
    all_to_all x1, starting transfers between devices, on_device(): plane_parts = lax.all_to_all(dense, PLANE, 0, 0)  10.1 us
    all_to_all x1, waiting for transfers between devices, on_device(): line_parts = lax.all_to_all(parts, LINE, 0, 0)  7.19 us
    all_to_all x1, waiting for transfers between devices, on_device(): plane_parts = lax.all_to_all(dense, PLANE, 0, 0)  6.91 us
    all_to_all x1, starting transfers between devices, to_all(): return lax.all_to_all(copies, axes, 0, 0)  5.01 us
  transfers between devices with their start and end apart: 5, of which 3 were waited for; matrix products, arithmetic and copies ran while one was open for 0% of the time, Pallas kernels for 8%

profile of v6, /device:TPU:1, one launch (start us, length us, event | category | flops | bytes accessed | tf_op | source)
XLA Modules:
  0.0 128.2 jit_solution(11406778985201316385)
XLA Ops:
  0.0 0.7 copy-done.3
  0.7 1.0 copy-done
  1.7 1.3 %shard_map.82 = f32[32,3,128]{2,1,0:T(4,128)} custom-call(s32[1,2,8]{2,1,0:T(2,128)S(1)} %copy-done.3, f32[2,16,32,128]{3,2,1,0:T(8,128)S(1)} %copy-done), custom_call_target="tpu_custom_call" | custom-call | tf_op jit(solution)/shard_map/pallas_call | solution.py:231
  3.1 0.0 copy-start.8
  3.1 0.0 copy-start.7
  3.1 29.3 %all-to-all-start = ((f32[32,3,128]{2,1,0:T(4,128)}), f32[32,3,128]{2,1,0:T(4,128)S(1)}, u32[]{:S(2)}, u32[]{:S(2)}) async-start(f32[32,3,128]{2,1,0:T(4,128)} %shard_map.82), calls=%async_computation | async-start | bytes 131072 | tf_op jit(solution)/shard_map/all_to_all | solution.py:263
  32.4 4.4 %collective-permute-start = (f32[2,1,32,128]{3,2,1,0:T(8,128)S(1)}, f32[2,1,32,128]{3,2,1,0:T(8,128)S(1)}, u32[]{:S(2)}, u32[]{:S(2)}) collective-permute-start(f32[2,1,32,128]{3,2,1,0:T(8,128)S(1)} %get-tuple-element.18), channel_id=1, source_target_pairs={{0,1020},{4,8},{8,4},{12,16},{16,12},{20,24},{24,20},{28,32},{32,2... | collective-permute-start | bytes 98312 | tf_op jit(solution)/shard_map/ppermute | solution.py:265
  36.8 12.4 %collective-permute-start.1 = (f32[2,1,32,128]{3,2,1,0:T(8,128)S(1)}, f32[2,1,32,128]{3,2,1,0:T(8,128)S(1)}, u32[]{:S(2)}, u32[]{:S(2)}) collective-permute-start(f32[2,1,32,128]{3,2,1,0:T(8,128)S(1)} %get-tuple-element.19), channel_id=1, source_target_pairs={{0,4},{4,0},{8,12},{12,8},{16,20},{20,16},{24,28},{28,24},{32,36},... | collective-permute-start | bytes 98312 | tf_op jit(solution)/shard_map/ppermute | solution.py:264
  49.3 7.2 %all-to-all-done.parts_ref.line_ref = f32[32,3,128]{2,1,0:T(4,128)S(1)} async-done(((f32[32,3,128]{2,1,0:T(4,128)}), f32[32,3,128]{2,1,0:T(4,128)S(1)}, u32[]{:S(2)}, u32[]{:S(2)}) %all-to-all-start) | async-done | bytes 49184 | tf_op jit(solution)/shard_map/all_to_all | solution.py:263
  56.5 3.5 %shard_map.83 = f32[32,16,128]{2,1,0:T(8,128)} custom-call(s32[3]{0:T(128)S(1)} %and_select_fusion.spots_ref, f32[32,3,128]{2,1,0:T(4,128)S(1)} %all-to-all-done.parts_ref.line_ref), custom_call_target="tpu_custom_call" | custom-call | tf_op jit(solution)/shard_map/pallas_call | solution.py:231
  60.0 10.1 %all-to-all-start.1 = ((f32[32,16,128]{2,1,0:T(8,128)}), f32[32,16,128]{2,1,0:T(8,128)S(1)}, u32[]{:S(2)}, u32[]{:S(2)}) async-start(f32[32,16,128]{2,1,0:T(8,128)} %shard_map.83), calls=%async_computation.1 | async-start | bytes 524288 | tf_op jit(solution)/shard_map/all_to_all | solution.py:269
  70.2 0.0 copy-start.2
  70.2 1.9 %shard_map.84 = (bf16[336,336]{1,0:T(8,128)(2,1)S(1)}, bf16[336,336]{1,0:T(8,128)(2,1)S(1)}, f32[336,512]{1,0:T(8,128)S(1)}) custom-call(f32[2,16,32,128]{3,2,1,0:T(8,128)S(1)} %copy-done.1, f32[2,1,32,128]{3,2,1,0:T(8,128)S(1)} %get-tuple-element.23.x_low_ref, f32[2,1,32,128]{3,2,1,0:T(8,128)S(1)} %get-tuple-element.24.x_high_ref, ...), custom_call_target="tpu_custom_call" | custom-call | flops 1000000000 | bytes 1048576 | tf_op jit(solution)/shard_map/pallas_call | solution.py:231
  72.1 6.9 %all-to-all-done.1.parts_ref = f32[32,16,128]{2,1,0:T(8,128)S(1)} async-done(((f32[32,16,128]{2,1,0:T(8,128)}), f32[32,16,128]{2,1,0:T(8,128)S(1)}, u32[]{:S(2)}, u32[]{:S(2)}) %all-to-all-start.1) | async-done | bytes 262176 | tf_op jit(solution)/shard_map/all_to_all | solution.py:269
  79.0 0.7 shard_map.85
  79.7 34.0 %all_to_all.20.line_parts_ref = f32[32,8,128]{2,1,0:T(8,128)S(1)} all-to-all(f32[32,8,128]{2,1,0:T(8,128)S(1)} %shard_map.85), channel_id=1, replica_groups=mesh['y'=4,'x'=4,'low'=8,'core'=2,'high'=4] {'high','low'}, dimensions={0} | all-to-all | bytes 262144 | tf_op jit(solution)/shard_map/all_to_all | solution.py:283
  113.7 0.6 broadcast_in_dim.2
  114.4 5.0 %all-to-all-start.3 = ((f32[32,2,128]{2,1,0:T(2,128)}), f32[32,2,128]{2,1,0:T(2,128)S(1)}, u32[]{:S(2)}, u32[]{:S(2)}) async-start(f32[32,2,128]{2,1,0:T(2,128)} %broadcast_in_dim.2), calls=%async_computation.3 | async-start | bytes 65536 | tf_op jit(solution)/shard_map/all_to_all | solution.py:245
  119.4 0.0 copy-start.5
  119.4 0.6 copy-done.4
  120.1 0.0 copy-done.5
  120.1 4.4 %shard_map.86.local_ref = f32[2,16,32,128]{3,2,1,0:T(8,128)S(1)} custom-call(s32[3]{0:T(128)S(1)} %and_select_fusion.spots_ref, f32[2,16,32,128]{3,2,1,0:T(8,128)S(1)} %copy-done.1, f32[2,1,32,128]{3,2,1,0:T(8,128)S(1)} %get-tuple-element.23.x_low_ref, f32[2,1,32,128]{3,2,1,0:T(8,128)S(1)} %get-tuple-element.24.x_high_ref, ...), custom_call_target="tpu_custom_call" | custom-call | tf_op jit(solution)/shard_map/pallas_call | solution.py:231
  124.5 2.3 %all-to-all-done.3.coarse_ref = f32[32,2,128]{2,1,0:T(2,128)S(1)} async-done(((f32[32,2,128]{2,1,0:T(2,128)}), f32[32,2,128]{2,1,0:T(2,128)S(1)}, u32[]{:S(2)}, u32[]{:S(2)}) %all-to-all-start.3) | async-done | bytes 32800 | tf_op jit(solution)/shard_map/all_to_all | solution.py:245
  126.7 1.5 %shard_map.87 = f32[2,16,32,128]{3,2,1,0:T(8,128)} custom-call(s32[1,2,8]{2,1,0:T(2,128)S(1)} %copy-done.3, f32[2,16,32,128]{3,2,1,0:T(8,128)S(1)} %shard_map.86.local_ref, f32[32,2,128]{2,1,0:T(2,128)S(1)} %all-to-all-done.3.coarse_ref), custom_call_target="tpu_custom_call" | custom-call | tf_op jit(solution)/shard_map/pallas_call | solution.py:231
  (18 shorter events, 0.1 us)
Async XLA Ops:
  0.0 0.7 copy-start.3
  0.7 1.0 copy-start
  3.1 46.2 %copy-start.8 = (s32[3]{0:T(128)S(1)}, s32[3]{0:T(128)}, u32[]{:S(2)}) copy-start(s32[3]{0:T(128)} %constant.35.clone) | copy-start | bytes 40
  3.1 46.2 %copy-start.7 = (f32[2,18,18]{2,0,1:T(2,128)S(1)}, f32[2,18,18]{2,0,1:T(2,128)}, u32[]{:S(2)}) copy-start(f32[2,18,18]{2,0,1:T(2,128)} %param.9) | copy-start | bytes 7780
  3.1 53.4 %all-to-all-start = ((f32[32,3,128]{2,1,0:T(4,128)}), f32[32,3,128]{2,1,0:T(4,128)S(1)}, u32[]{:S(2)}, u32[]{:S(2)}) async-start(f32[32,3,128]{2,1,0:T(4,128)} %shard_map.82), calls=%async_computation | async-start | bytes 131072 | tf_op jit(solution)/shard_map/all_to_all | solution.py:263
  32.4 37.8 %copy-start.1 = (f32[2,16,32,128]{3,2,1,0:T(8,128)S(1)}, f32[2,16,32,128]{3,2,1,0:T(8,128)}, u32[]{:S(2)}) copy-start(f32[2,16,32,128]{3,2,1,0:T(8,128)} %residual_ref.5) | copy-start | bytes 1572868
  32.4 37.7 %collective-permute-start = (f32[2,1,32,128]{3,2,1,0:T(8,128)S(1)}, f32[2,1,32,128]{3,2,1,0:T(8,128)S(1)}, u32[]{:S(2)}, u32[]{:S(2)}) collective-permute-start(f32[2,1,32,128]{3,2,1,0:T(8,128)S(1)} %get-tuple-element.18), channel_id=1, source_target_pairs={{0,1020},{4,8},{8,4},{12,16},{16,12},{20,24},{24,20},{28,32},{32,2... | collective-permute-start | bytes 98312 | tf_op jit(solution)/shard_map/ppermute | solution.py:265
  36.8 33.3 %collective-permute-start.1 = (f32[2,1,32,128]{3,2,1,0:T(8,128)S(1)}, f32[2,1,32,128]{3,2,1,0:T(8,128)S(1)}, u32[]{:S(2)}, u32[]{:S(2)}) collective-permute-start(f32[2,1,32,128]{3,2,1,0:T(8,128)S(1)} %get-tuple-element.19), channel_id=1, source_target_pairs={{0,4},{4,0},{8,12},{12,8},{16,20},{20,16},{24,28},{28,24},{32,36},... | collective-permute-start | bytes 98312 | tf_op jit(solution)/shard_map/ppermute | solution.py:264
  60.0 19.0 %all-to-all-start.1 = ((f32[32,16,128]{2,1,0:T(8,128)}), f32[32,16,128]{2,1,0:T(8,128)S(1)}, u32[]{:S(2)}, u32[]{:S(2)}) async-start(f32[32,16,128]{2,1,0:T(8,128)} %shard_map.83), calls=%async_computation.1 | async-start | bytes 524288 | tf_op jit(solution)/shard_map/all_to_all | solution.py:269
  70.2 8.9 %copy-start.2 = (f32[16,1024]{1,0:T(8,128)S(1)}, f32[16,1024]{1,0:T(8,128)}, u32[]{:S(2)}) copy-start(f32[16,1024]{1,0:T(8,128)} %matrix_ref.1) | copy-start | bytes 196612
  113.7 5.7 %copy-start.6 = (f32[8,18,18]{2,0,1:T(8,128)S(1)}, f32[8,18,18]{2,0,1:T(8,128)}, u32[]{:S(2)}) copy-start(f32[8,18,18]{2,0,1:T(8,128)} %param.11) | copy-start | bytes 31108
  114.4 12.4 %all-to-all-start.3 = ((f32[32,2,128]{2,1,0:T(2,128)}), f32[32,2,128]{2,1,0:T(2,128)S(1)}, u32[]{:S(2)}, u32[]{:S(2)}) async-start(f32[32,2,128]{2,1,0:T(2,128)} %broadcast_in_dim.2), calls=%async_computation.3 | async-start | bytes 65536 | tf_op jit(solution)/shard_map/all_to_all | solution.py:245
  119.4 0.7 copy-start.4
  119.4 0.7 copy-start.5

commit v7 on v6

--- a/solution.py
+++ b/solution.py
@@ -61,48 +61,90 @@
     return first, pair - EXTENT * first
 
 
-def message_kernel(labels_ref, residual_ref, out_ref):
+def message_kernel(
+    even_ref, labels_hbm, residual_hbm, out_ref, inner_ref, outer_ref, labels_ref, residual_ref, sems
+):
+    copies = [pltpu.make_async_copy(residual_hbm.at[v], residual_ref.at[v], sems.at[v]) for v in range(2)]
+    copies.append(pltpu.make_async_copy(labels_hbm, labels_ref, sems.at[2]))
+    for copy in copies:
+        copy.start()
+    copies[2].wait()
     lane = iota((1, 128), 1)
-    wide = iota((2, 128), 1)
     message = jnp.zeros((1, 128), jnp.float32)
-    for j in range(2):
-        ys = slice(j * SPAN, (j + 1) * SPAN)
+    for slot in range(16):
+        j, k = divmod(slot, 8)
+        label = labels_ref[0, j : j + 1, k : k + 1].astype(jnp.float32)
+        message = jnp.where(lane == slot + 32, label, message)
+    even = even_ref[0] != 0
+    for v in range(2):
+        copies[v].wait()
         sums = jnp.concatenate(
             [
-                jnp.sum(jnp.sum(residual_ref[v, :, ys, :], axis=0), axis=0, keepdims=True)
-                for v in range(2)
+                jnp.sum(
+                    jnp.sum(residual_ref[v, :, j * SPAN : (j + 1) * SPAN, :], axis=0),
+                    axis=0,
+                    keepdims=True,
+                )
+                for j in range(2)
             ],
             axis=0,
         )
+        wide = iota((2, 128), 1) >> 4
         for k in range(8):
-            total = jnp.sum(jnp.where((wide >> 4) == k, sums, 0.0), axis=1, keepdims=True)
-            slot = j * 8 + k
-            label = labels_ref[0, j, k].astype(jnp.float32)
-            message = jnp.where(lane == slot, total[0:1] * WEIGHT, message)
-            message = jnp.where(lane == slot + 16, total[1:2] * WEIGHT, message)
-            message = jnp.where(lane == slot + 32, label, message)
+            total = jnp.sum(jnp.where(wide == k, sums, 0.0), axis=1, keepdims=True)
+            for j in range(2):
+                slot = v * 16 + j * 8 + k
+                message = jnp.where(lane == slot, total[j : j + 1] * WEIGHT, message)
+        rows = slice(v * SPAN, (v + 1) * SPAN)
+        out_ref[rows, 1, :] = residual_ref[v, :, 2 * SPAN - 1, :]
+        out_ref[rows, 2, :] = residual_ref[v, :, 0, :]
+        first, last = residual_ref[v, 0], residual_ref[v, SPAN - 1]
+        inner_ref[v, 0] = jnp.where(even, last, first)
+        outer_ref[v, 0] = jnp.where(even, first, last)
     out_ref[:, 0:1, :] = jnp.broadcast_to(message[None], (LINE_SIZE, 1, 128))
-    out_ref[:, 1, :] = residual_ref[:, :, 2 * SPAN - 1, :].reshape(LINE_SIZE, 128)
-    out_ref[:, 2, :] = residual_ref[:, :, 0, :].reshape(LINE_SIZE, 128)
+
+
+def send_messages(even, labels, residual):
+    vectors, _, span_y, span_z = residual.shape
+    side = jax.ShapeDtypeStruct((vectors, 1, span_y, span_z), jnp.float32)
+    return pl.pallas_call(
+        message_kernel,
+        out_shape=[jax.ShapeDtypeStruct((LINE_SIZE, 3, 128), jnp.float32), side, side],
+        in_specs=[pl.BlockSpec(memory_space=pltpu.SMEM)] + [pl.BlockSpec(memory_space=pl.ANY)] * 2,
+        out_specs=[pl.BlockSpec(memory_space=pltpu.VMEM)] * 3,
+        scratch_shapes=[
+            pltpu.VMEM(labels.shape, jnp.int32),
+            pltpu.VMEM(residual.shape, jnp.float32),
+            pltpu.SemaphoreType.DMA((3,)),
+        ],
+    )(even, labels, residual)
 
 
 def scatter_kernel(spots_ref, parts_ref, out_ref):
-    parts = parts_ref[:, 0, :]
-    lane = iota((LINE_SIZE, 128), 1)
-    block = (lane & 7) + (spots_ref[0] >> 3) * 8
-    values, places = [], []
-    for e in range(16):
-        first, second, label = (
-            jnp.broadcast_to(parts[:, slot : slot + 1], parts.shape) for slot in (e, e + 16, e + 32)
-        )
-        label = label.astype(jnp.int32)
-        here = ((label >> 7) == block) & (lane < 16)
-        values.append(jnp.where(here, jnp.where(lane < 8, first, second), 0.0))
-        places.append(jnp.where((label & 127) == lane, 1.0, 0.0))
-    values = jnp.concatenate(values, axis=0)
-    places = jnp.concatenate(places, axis=0)
-    rows = exact(values, places, ((0,), (0,)))[:16]
-    out_ref[...] = jnp.broadcast_to(rows[None], out_ref.shape)
+    slots = jnp.transpose(parts_ref[:, 0, :])
+    slots = jnp.concatenate([slots, jnp.zeros((128, 96), jnp.float32)], axis=1)
+    quarter = iota((4, 128), 1) >> 5
+
+    def along_lanes(begin):
+        total = slots[begin : begin + 4]
+        for q in range(1, 4):
+            part = pltpu.roll(slots[begin + 4 * q : begin + 4 * q + 4], 32 * q, 1)
+            total = jnp.where(quarter == q, part, total)
+        return total
+
+    first, second, label = (along_lanes(begin) for begin in (0, 16, 32))
+    label = label.astype(jnp.int32)
+    row = iota((SPAN, 128), 0)
+    block = (row & 7) + (spots_ref[0] >> 3) * 8
+    column = iota((128, 128), 0)
+    total = jnp.zeros((SPAN, 128), jnp.float32)
+    for g in range(4):
+        here = (label[g : g + 1] >> 7) == block
+        values = jnp.where(row < 8, first[g : g + 1], second[g : g + 1])
+        values = jnp.where(here, values, 0.0)
+        places = jnp.where((label[g : g + 1] & 127) == column, 1.0, 0.0)
+        total = total + exact(values, places, ((1,), (1,)))
+    out_ref[...] = jnp.broadcast_to(total[None], out_ref.shape)
 
 
 def terms_kernel(spots_ref, parts_ref, line_ref, x_low_ref, x_high_ref, matrix_ref, out_ref):
@@ -255,11 +297,8 @@
     spots = (spot + jnp.array([0, 24, 8], jnp.int32)) % LINE_SIZE
     barrier = lax.optimization_barrier
 
-    parts = call(message_kernel, (LINE_SIZE, 3, 128), [labels], [residual])
-    first, last = residual[:, :1], residual[:, -1:]
-    parts, inner, outer = barrier(
-        (parts, jnp.where(even, last, first), jnp.where(even, first, last))
-    )
+    parts, inner, outer = send_messages(even.astype(jnp.int32).reshape(1), labels, residual)
+    parts, inner, outer = barrier((parts, inner, outer))
     line_parts = lax.all_to_all(parts, LINE, 0, 0)
     inner = lax.ppermute(inner, GROUP, [(i, i ^ 1) for i in range(256)])
     outer = lax.ppermute(outer, GROUP, [(i, (i + i % 2 * 2 - 1) % 256) for i in range(256)])

time: 129 us -> 126 us (0.977)
  local copies, waits for them, and re-layouts: 3.05 us -> 1.35 us
    pallas_call x6 -> x5, Pallas kernels: 13.3 us -> 10.4 us  [call(): pl.pallas_call(kernel, out_shape=out_shape, in_specs=[pl.BlockSpec(memory...]
    pallas_call x0 -> x1, Pallas kernels: none -> 1.88 us  [send_messages(): pl.pallas_call(message_kernel, out_shape=[jax.ShapeDtypeStruct((LINE_SIZE...]
    unnamed x20 -> x22, local copies, waits for them, and re-layouts: 2.43 us -> 0.72 us
  transfers between devices with their start and end apart: 5 -> 5, of which waited for: 3 -> 3; matrix products, arithmetic and copies ran while one was open for 0% -> 0% of each run, Pallas kernels for 8% -> 7%
where the time goes in v7:
time: 126 us
  starting transfers between devices  61.4 us (49%)
  blocking collectives  34 us (27%)
  waiting for transfers between devices  16.3 us (13%)
  Pallas kernels  12.3 us (10%)
  local copies, waits for them, and re-layouts  1.35 us (1%)
    all_to_all x1, blocking collectives, on_device(): row_parts = lax.all_to_all(terms, LINE, 0, 0)  34 us
    all_to_all x1, starting transfers between devices, on_device(): line_parts = lax.all_to_all(parts, LINE, 0, 0)  29.4 us
    ppermute x1, starting transfers between devices, on_device(): inner = lax.ppermute(inner, GROUP, [(i, i ^ 1) for i in range(256)])  12.4 us
    pallas_call x5, Pallas kernels, call(): pl.pallas_call(kernel, out_shape=out_shape, in_specs=[pl.BlockSpec(memory...  10.4 us
    all_to_all x1, starting transfers between devices, on_device(): plane_parts = lax.all_to_all(dense, PLANE, 0, 0)  10.1 us
    all_to_all x1, waiting for transfers between devices, on_device(): line_parts = lax.all_to_all(parts, LINE, 0, 0)  7.15 us
    all_to_all x1, waiting for transfers between devices, on_device(): plane_parts = lax.all_to_all(dense, PLANE, 0, 0)  6.9 us
    all_to_all x1, starting transfers between devices, to_all(): return lax.all_to_all(copies, axes, 0, 0)  5.01 us
  transfers between devices with their start and end apart: 5, of which 3 were waited for; matrix products, arithmetic and copies ran while one was open for 0% of the time, Pallas kernels for 7%

profile of v7, /device:TPU:1, one launch (start us, length us, event | category | flops | bytes accessed | tf_op | source)
XLA Modules:
  0.0 125.7 jit_solution(3909772733191561985)
XLA Ops:
  0.0 1.9 %shard_map.82 = (f32[32,3,128]{2,1,0:T(4,128)}, f32[2,1,32,128]{3,2,1,0:T(8,128)}, f32[2,1,32,128]{3,2,1,0:T(8,128)}) custom-call(s32[1]{0:T(128)} %bitcast.even_ref, s32[1,2,8]{2,1,0:T(2,128)} %labels_ref.1, f32[2,16,32,128]{3,2,1,0:T(8,128)} %residual_ref.3), custom_call_target="tpu_custom_call" | custom-call | tf_op jit(solution)/shard_map/pallas_call | solution.py:110
  1.9 0.0 copy-start.9
  1.9 29.4 %all-to-all-start = ((f32[32,3,128]{2,1,0:T(4,128)}), f32[32,3,128]{2,1,0:T(4,128)S(1)}, u32[]{:S(2)}, u32[]{:S(2)}) async-start(f32[32,3,128]{2,1,0:T(4,128)} %get-tuple-element.17), calls=%async_computation | async-start | bytes 131072 | tf_op jit(solution)/shard_map/all_to_all | solution.py:302
  31.4 0.0 copy-start.6
  31.4 0.0 copy-start
  31.4 4.4 %collective-permute-start = (f32[2,1,32,128]{3,2,1,0:T(8,128)S(1)}, f32[2,1,32,128]{3,2,1,0:T(8,128)S(1)}, u32[]{:S(2)}, u32[]{:S(2)}) collective-permute-start(f32[2,1,32,128]{3,2,1,0:T(8,128)S(1)} %copy-done.8), channel_id=1, source_target_pairs={{0,1020},{4,8},{8,4},{12,16},{16,12},{20,24},{24,20},{28,32},{32,2... | collective-permute-start | bytes 98312 | tf_op jit(solution)/shard_map/ppermute | solution.py:304
  35.8 12.4 %collective-permute-start.1 = (f32[2,1,32,128]{3,2,1,0:T(8,128)S(1)}, f32[2,1,32,128]{3,2,1,0:T(8,128)S(1)}, u32[]{:S(2)}, u32[]{:S(2)}) collective-permute-start(f32[2,1,32,128]{3,2,1,0:T(8,128)S(1)} %copy-done.7), channel_id=1, source_target_pairs={{0,4},{4,0},{8,12},{12,8},{16,20},{20,16},{24,28},{28,24},{32,36},... | collective-permute-start | bytes 98312 | tf_op jit(solution)/shard_map/ppermute | solution.py:303
  48.3 7.2 %all-to-all-done.parts_ref.line_ref = f32[32,3,128]{2,1,0:T(4,128)S(1)} async-done(((f32[32,3,128]{2,1,0:T(4,128)}), f32[32,3,128]{2,1,0:T(4,128)S(1)}, u32[]{:S(2)}, u32[]{:S(2)}) %all-to-all-start) | async-done | bytes 49184 | tf_op jit(solution)/shard_map/all_to_all | solution.py:302
  55.5 1.9 %shard_map.83 = f32[32,16,128]{2,1,0:T(8,128)} custom-call(s32[3]{0:T(128)S(1)} %and_select_fusion.spots_ref, f32[32,3,128]{2,1,0:T(4,128)S(1)} %all-to-all-done.parts_ref.line_ref), custom_call_target="tpu_custom_call" | custom-call | tf_op jit(solution)/shard_map/pallas_call | solution.py:273
  57.4 10.1 %all-to-all-start.1 = ((f32[32,16,128]{2,1,0:T(8,128)}), f32[32,16,128]{2,1,0:T(8,128)S(1)}, u32[]{:S(2)}, u32[]{:S(2)}) async-start(f32[32,16,128]{2,1,0:T(8,128)} %shard_map.83), calls=%async_computation.1 | async-start | bytes 524288 | tf_op jit(solution)/shard_map/all_to_all | solution.py:308
  67.6 0.0 copy-start.1
  67.6 1.9 %shard_map.84 = (bf16[336,336]{1,0:T(8,128)(2,1)S(1)}, bf16[336,336]{1,0:T(8,128)(2,1)S(1)}, f32[336,512]{1,0:T(8,128)S(1)}) custom-call(f32[2,16,32,128]{3,2,1,0:T(8,128)S(1)} %copy-done, f32[2,1,32,128]{3,2,1,0:T(8,128)S(1)} %get-tuple-element.23.x_low_ref, f32[2,1,32,128]{3,2,1,0:T(8,128)S(1)} %get-tuple-element.24.x_high_ref, f32[2,18,18]{2,1,0:T(8,128)S(1)} %copy.9.horiz_ref), custom_call_target="tpu_custom_call" | custom-call | flops 1000000000 | bytes 1048576 | tf_op jit(solution)/shard_map/pallas_call | solution.py:273
  69.5 6.9 %all-to-all-done.1.parts_ref = f32[32,16,128]{2,1,0:T(8,128)S(1)} async-done(((f32[32,16,128]{2,1,0:T(8,128)}), f32[32,16,128]{2,1,0:T(8,128)S(1)}, u32[]{:S(2)}, u32[]{:S(2)}) %all-to-all-start.1) | async-done | bytes 262176 | tf_op jit(solution)/shard_map/all_to_all | solution.py:308
  76.4 0.7 shard_map.85
  77.1 34.0 %all_to_all.20.line_parts_ref = f32[32,8,128]{2,1,0:T(8,128)S(1)} all-to-all(f32[32,8,128]{2,1,0:T(8,128)S(1)} %shard_map.85), channel_id=1, replica_groups=mesh['y'=4,'x'=4,'low'=8,'core'=2,'high'=4] {'high','low'}, dimensions={0} | all-to-all | bytes 262144 | tf_op jit(solution)/shard_map/all_to_all | solution.py:322
  111.1 0.6 broadcast_in_dim.2
  111.8 5.0 %all-to-all-start.3 = ((f32[32,2,128]{2,1,0:T(2,128)}), f32[32,2,128]{2,1,0:T(2,128)S(1)}, u32[]{:S(2)}, u32[]{:S(2)}) async-start(f32[32,2,128]{2,1,0:T(2,128)} %broadcast_in_dim.2), calls=%async_computation.3 | async-start | bytes 65536 | tf_op jit(solution)/shard_map/all_to_all | solution.py:287
  116.8 0.0 copy-start.3
  116.8 0.0 copy-start.4
  116.8 0.6 copy-done.3
  117.5 0.0 copy-done.4
  117.5 4.4 %shard_map.86.local_ref = f32[2,16,32,128]{3,2,1,0:T(8,128)S(1)} custom-call(s32[3]{0:T(128)S(1)} %and_select_fusion.spots_ref, f32[2,16,32,128]{3,2,1,0:T(8,128)S(1)} %copy-done, f32[2,1,32,128]{3,2,1,0:T(8,128)S(1)} %get-tuple-element.23.x_low_ref, f32[2,1,32,128]{3,2,1,0:T(8,128)S(1)} %get-tuple-element.24.x_high_ref, ...), custom_call_target="tpu_custom_call" | custom-call | tf_op jit(solution)/shard_map/pallas_call | solution.py:273
  121.9 2.3 %all-to-all-done.3.coarse_ref = f32[32,2,128]{2,1,0:T(2,128)S(1)} async-done(((f32[32,2,128]{2,1,0:T(2,128)}), f32[32,2,128]{2,1,0:T(2,128)S(1)}, u32[]{:S(2)}, u32[]{:S(2)}) %all-to-all-start.3) | async-done | bytes 32800 | tf_op jit(solution)/shard_map/all_to_all | solution.py:287
  124.1 1.5 %shard_map.87 = f32[2,16,32,128]{3,2,1,0:T(8,128)} custom-call(s32[1,2,8]{2,1,0:T(2,128)S(1)} %copy-done.2, f32[2,16,32,128]{3,2,1,0:T(8,128)S(1)} %shard_map.86.local_ref, f32[32,2,128]{2,1,0:T(2,128)S(1)} %all-to-all-done.3.coarse_ref), custom_call_target="tpu_custom_call" | custom-call | tf_op jit(solution)/shard_map/pallas_call | solution.py:273
  (19 shorter events, 0.1 us)
Async XLA Ops:
  1.9 29.5 %copy-start.8 = (f32[2,1,32,128]{3,2,1,0:T(8,128)S(1)}, f32[2,1,32,128]{3,2,1,0:T(8,128)}, u32[]{:S(2)}) copy-start(f32[2,1,32,128]{3,2,1,0:T(8,128)} %get-tuple-element.18) | copy-start | bytes 98308
  1.9 33.9 %copy-start.7 = (f32[2,1,32,128]{3,2,1,0:T(8,128)S(1)}, f32[2,1,32,128]{3,2,1,0:T(8,128)}, u32[]{:S(2)}) copy-start(f32[2,1,32,128]{3,2,1,0:T(8,128)} %get-tuple-element.19) | copy-start | bytes 98308
  1.9 46.3 %copy-start.9 = (s32[3]{0:T(128)S(1)}, s32[3]{0:T(128)}, u32[]{:S(2)}) copy-start(s32[3]{0:T(128)} %constant.35.clone) | copy-start | bytes 40
  1.9 53.5 %all-to-all-start = ((f32[32,3,128]{2,1,0:T(4,128)}), f32[32,3,128]{2,1,0:T(4,128)S(1)}, u32[]{:S(2)}, u32[]{:S(2)}) async-start(f32[32,3,128]{2,1,0:T(4,128)} %get-tuple-element.17), calls=%async_computation | async-start | bytes 131072 | tf_op jit(solution)/shard_map/all_to_all | solution.py:302
  31.4 16.9 %copy-start.6 = (f32[2,18,18]{2,0,1:T(2,128)S(1)}, f32[2,18,18]{2,0,1:T(2,128)}, u32[]{:S(2)}) copy-start(f32[2,18,18]{2,0,1:T(2,128)} %param.9) | copy-start | bytes 7780
  31.4 36.2 %copy-start = (f32[2,16,32,128]{3,2,1,0:T(8,128)S(1)}, f32[2,16,32,128]{3,2,1,0:T(8,128)}, u32[]{:S(2)}) copy-start(f32[2,16,32,128]{3,2,1,0:T(8,128)} %residual_ref.3) | copy-start | bytes 1572868
  31.4 36.1 %collective-permute-start = (f32[2,1,32,128]{3,2,1,0:T(8,128)S(1)}, f32[2,1,32,128]{3,2,1,0:T(8,128)S(1)}, u32[]{:S(2)}, u32[]{:S(2)}) collective-permute-start(f32[2,1,32,128]{3,2,1,0:T(8,128)S(1)} %copy-done.8), channel_id=1, source_target_pairs={{0,1020},{4,8},{8,4},{12,16},{16,12},{20,24},{24,20},{28,32},{32,2... | collective-permute-start | bytes 98312 | tf_op jit(solution)/shard_map/ppermute | solution.py:304
  35.8 31.7 %collective-permute-start.1 = (f32[2,1,32,128]{3,2,1,0:T(8,128)S(1)}, f32[2,1,32,128]{3,2,1,0:T(8,128)S(1)}, u32[]{:S(2)}, u32[]{:S(2)}) collective-permute-start(f32[2,1,32,128]{3,2,1,0:T(8,128)S(1)} %copy-done.7), channel_id=1, source_target_pairs={{0,4},{4,0},{8,12},{12,8},{16,20},{20,16},{24,28},{28,24},{32,36},... | collective-permute-start | bytes 98312 | tf_op jit(solution)/shard_map/ppermute | solution.py:303
  57.4 19.0 %all-to-all-start.1 = ((f32[32,16,128]{2,1,0:T(8,128)}), f32[32,16,128]{2,1,0:T(8,128)S(1)}, u32[]{:S(2)}, u32[]{:S(2)}) async-start(f32[32,16,128]{2,1,0:T(8,128)} %shard_map.83), calls=%async_computation.1 | async-start | bytes 524288 | tf_op jit(solution)/shard_map/all_to_all | solution.py:308
  67.6 8.9 %copy-start.1 = (f32[16,1024]{1,0:T(8,128)S(1)}, f32[16,1024]{1,0:T(8,128)}, u32[]{:S(2)}) copy-start(f32[16,1024]{1,0:T(8,128)} %matrix_ref.1) | copy-start | bytes 196612
  111.1 5.7 %copy-start.5 = (f32[8,18,18]{2,0,1:T(8,128)S(1)}, f32[8,18,18]{2,0,1:T(8,128)}, u32[]{:S(2)}) copy-start(f32[8,18,18]{2,0,1:T(8,128)} %param.11) | copy-start | bytes 31108
  111.8 12.4 %all-to-all-start.3 = ((f32[32,2,128]{2,1,0:T(2,128)}), f32[32,2,128]{2,1,0:T(2,128)S(1)}, u32[]{:S(2)}, u32[]{:S(2)}) async-start(f32[32,2,128]{2,1,0:T(2,128)} %broadcast_in_dim.2), calls=%async_computation.3 | async-start | bytes 65536 | tf_op jit(solution)/shard_map/all_to_all | solution.py:287
  116.8 0.7 copy-start.3
  116.8 0.7 copy-start.4
  117.5 6.7 %copy-start.2 = (s32[1,2,8]{2,1,0:T(2,128)S(1)}, s32[1,2,8]{2,1,0:T(2,128)}, u32[]{:S(2)}) copy-start(s32[1,2,8]{2,1,0:T(2,128)} %labels_ref.1) | copy-start | bytes 196

commit v8 on v7

--- a/solution.py
+++ b/solution.py
@@ -96,12 +96,12 @@
                 slot = v * 16 + j * 8 + k
                 message = jnp.where(lane == slot, total[j : j + 1] * WEIGHT, message)
         rows = slice(v * SPAN, (v + 1) * SPAN)
-        out_ref[rows, 1, :] = residual_ref[v, :, 2 * SPAN - 1, :]
-        out_ref[rows, 2, :] = residual_ref[v, :, 0, :]
+        out_ref[rows, 0, 128:256] = residual_ref[v, :, 2 * SPAN - 1, :]
+        out_ref[rows, 0, 256:384] = residual_ref[v, :, 0, :]
         first, last = residual_ref[v, 0], residual_ref[v, SPAN - 1]
         inner_ref[v, 0] = jnp.where(even, last, first)
         outer_ref[v, 0] = jnp.where(even, first, last)
-    out_ref[:, 0:1, :] = jnp.broadcast_to(message[None], (LINE_SIZE, 1, 128))
+    out_ref[:, 0, 0:128] = jnp.broadcast_to(message, (LINE_SIZE, 128))
 
 
 def send_messages(even, labels, residual):
@@ -109,7 +109,7 @@
     side = jax.ShapeDtypeStruct((vectors, 1, span_y, span_z), jnp.float32)
     return pl.pallas_call(
         message_kernel,
-        out_shape=[jax.ShapeDtypeStruct((LINE_SIZE, 3, 128), jnp.float32), side, side],
+        out_shape=[jax.ShapeDtypeStruct((LINE_SIZE, 1, 384), jnp.float32), side, side],
         in_specs=[pl.BlockSpec(memory_space=pltpu.SMEM)] + [pl.BlockSpec(memory_space=pl.ANY)] * 2,
         out_specs=[pl.BlockSpec(memory_space=pltpu.VMEM)] * 3,
         scratch_shapes=[
@@ -121,7 +121,7 @@
 
 
 def scatter_kernel(spots_ref, parts_ref, out_ref):
-    slots = jnp.transpose(parts_ref[:, 0, :])
+    slots = jnp.transpose(parts_ref[:, 0, 0:128])
     slots = jnp.concatenate([slots, jnp.zeros((128, 96), jnp.float32)], axis=1)
     quarter = iota((4, 128), 1) >> 5
 
@@ -150,25 +150,27 @@
 def terms_kernel(spots_ref, parts_ref, line_ref, x_low_ref, x_high_ref, matrix_ref, out_ref):
     rhs = jnp.sum(parts_ref[...], axis=0)
     lane = iota((SPAN, 128), 1) - iota((SPAN, 128), 0)
-    here = lane == (spots_ref[0] & 7) * SPAN
+    place = (spots_ref[0] & 3) * 32
+    message = jnp.zeros((1, 128), jnp.float32)
     for v in range(2):
         total = jnp.zeros((SPAN, 128), jnp.float32)
         for block in range(8):
             row = v * 8 + block
             total = total + matrix_ref[:, block * 128 : (block + 1) * 128] * rhs[row : row + 1]
         column = jnp.sum(total, axis=1, keepdims=True)
-        terms = jnp.sum(jnp.where(here, column, 0.0), axis=0, keepdims=True)
-        out_ref[:, v, :] = jnp.broadcast_to(terms, (LINE_SIZE, 128))
-    out_ref[0:8, 2, :] = line_ref[24:32, 1, :]
-    out_ref[8:32, 2, :] = line_ref[0:24, 1, :]
-    out_ref[0:24, 3, :] = line_ref[8:32, 2, :]
-    out_ref[24:32, 3, :] = line_ref[0:8, 2, :]
-    out_ref[:, 4:8, :] = jnp.zeros((LINE_SIZE, 4, 128), jnp.float32)
+        here = lane == place + SPAN * v
+        message = message + jnp.sum(jnp.where(here, column, 0.0), axis=0, keepdims=True)
+    out_ref[:, 0, 0:128] = jnp.broadcast_to(message, (LINE_SIZE, 128))
+    out_ref[0:8, 0, 128:256] = line_ref[24:32, 0, 128:256]
+    out_ref[8:32, 0, 128:256] = line_ref[0:24, 0, 128:256]
+    out_ref[0:24, 0, 256:384] = line_ref[8:32, 0, 256:384]
+    out_ref[24:32, 0, 256:384] = line_ref[0:8, 0, 256:384]
+    out_ref[:, 0, 384:896] = jnp.zeros((LINE_SIZE, 512), jnp.float32)
     for spot, edge in ((1, 0), (2, 2 * SPAN - 1)):
         corners = [
             side_ref[v, 0, edge : edge + 1, :] for v in range(2) for side_ref in (x_low_ref, x_high_ref)
         ]
-        out_ref[spots_ref[spot], 4:8, :] = jnp.concatenate(corners, axis=0)
+        out_ref[spots_ref[spot], :, 384:896] = jnp.concatenate(corners, axis=1)
 
 
 def prepare_kernel(
@@ -231,9 +233,11 @@
                 box_ref[begin + 16 : begin + 24, lanes] = jnp.zeros((8, 128), jnp.float32)
                 if (edge == 15) == (j == 0):
                     corner = line_parts_ref[spots_ref[spot]]
-                    box_ref[begin : begin + 1, lanes] = corner[4 + 2 * v : 5 + 2 * v]
-                    box_ref[begin + 1 : begin + 17, lanes] = line_parts_ref[rows, spot + 1, :]
-                    box_ref[begin + 17 : begin + 18, lanes] = corner[5 + 2 * v : 6 + 2 * v]
+                    first = 128 * (3 + 2 * v)
+                    side = slice(128 * spot, 128 * (spot + 1))
+                    box_ref[begin : begin + 1, lanes] = corner[:, first : first + 128]
+                    box_ref[begin + 1 : begin + 17, lanes] = line_parts_ref[rows, 0, side]
+                    box_ref[begin + 17 : begin + 18, lanes] = corner[:, first + 128 : first + 256]
                 else:
                     box_ref[begin : begin + 1, lanes] = x_low_ref[v, 0, edge : edge + 1, :]
                     box_ref[begin + 1 : begin + 17, lanes] = residual_ref[v, :, edge, :]
@@ -251,20 +255,21 @@
 
 
 def merge_kernel(labels_ref, local_ref, coarse_ref, out_ref):
-    lane = iota((2, 128), 1)
+    lane = iota((1, 128), 1)
     for j in range(2):
-        update = jnp.zeros((2, 128), jnp.float32)
+        updates = [jnp.zeros((1, 128), jnp.float32)] * 2
         for k in range(8):
             label = labels_ref[0, j, k]
             block = ((label >> 8) << 1) | ((label >> 4) & 1)
-            place = (((label >> 5) & 7) << 4) | (label & 15)
-            value = jnp.sum(
-                jnp.where(lane == place, coarse_ref[block], 0.0), axis=1, keepdims=True
-            )
-            update = update + jnp.where((lane >> 4) == k, value * WEIGHT, 0.0)
+            place = (((label >> 5) & 3) << 5) | (label & 15)
+            row = coarse_ref[block, pl.ds((label >> 7) & 1, 1), :]
+            for v in range(2):
+                here = lane == place + SPAN * v
+                value = jnp.sum(jnp.where(here, row, 0.0), axis=1, keepdims=True)
+                updates[v] = jnp.where((lane >> 4) == k, value * WEIGHT, updates[v])
         ys = slice(j * SPAN, (j + 1) * SPAN)
         for v in range(2):
-            out_ref[v, :, ys, :] = local_ref[v, :, ys, :] + update[v : v + 1][None]
+            out_ref[v, :, ys, :] = local_ref[v, :, ys, :] + updates[v][None]
 
 
 def call(kernel, out_shape, scalars, arrays, scratch=(), cost=None):
@@ -316,11 +321,12 @@
     )
     plane_parts, prepared, x_low, x_high = barrier((plane_parts, prepared, x_low, x_high))
     terms = call(
-        terms_kernel, (LINE_SIZE, 8, 128), [spots],
+        terms_kernel, (LINE_SIZE, 1, 896), [spots],
         [plane_parts, line_parts, x_low, x_high, coarse_inverse],
     )
     row_parts = lax.all_to_all(terms, LINE, 0, 0)
-    coarse = to_all(row_parts[:, :2].sum(axis=0), PLANE, PLANE_SIZE)
+    rows = row_parts[:, 0, :128].reshape(4, 2, 4, 128).sum(axis=(0, 2))
+    coarse = to_all(rows, PLANE, PLANE_SIZE)
     local = call(
         finish_kernel, residual.shape, [spots],
         [residual, x_low, x_high, row_parts, *prepared, horiz_values,

time: 126 us -> 123 us (0.976)
  blocking collectives: 34 us -> 32.4 us
  waiting for transfers between devices: 16.3 us -> 14.9 us
    all_to_all x1, blocking collectives: 34 us -> 32.4 us  [on_device(): row_parts = lax.all_to_all(terms, LINE, 0, 0)]
    all_to_all x1, waiting for transfers between devices: 7.15 us -> 5.76 us  [on_device(): line_parts = lax.all_to_all(parts, LINE, 0, 0)]
where the time goes in v8:
time: 123 us
  starting transfers between devices  61.4 us (50%)
  blocking collectives  32.4 us (26%)
  waiting for transfers between devices  14.9 us (12%)
  Pallas kernels  12.3 us (10%)
  local copies, waits for them, and re-layouts  1.36 us (1%)
    all_to_all x1, blocking collectives, on_device(): row_parts = lax.all_to_all(terms, LINE, 0, 0)  32.4 us
    all_to_all x1, starting transfers between devices, on_device(): line_parts = lax.all_to_all(parts, LINE, 0, 0)  29.4 us
    ppermute x1, starting transfers between devices, on_device(): inner = lax.ppermute(inner, GROUP, [(i, i ^ 1) for i in range(256)])  12.4 us
    pallas_call x5, Pallas kernels, call(): pl.pallas_call(kernel, out_shape=out_shape, in_specs=[pl.BlockSpec(memory...  10.5 us
    all_to_all x1, starting transfers between devices, on_device(): plane_parts = lax.all_to_all(dense, PLANE, 0, 0)  9.97 us
    all_to_all x1, waiting for transfers between devices, on_device(): plane_parts = lax.all_to_all(dense, PLANE, 0, 0)  6.91 us
    all_to_all x1, waiting for transfers between devices, on_device(): line_parts = lax.all_to_all(parts, LINE, 0, 0)  5.76 us
    all_to_all x1, starting transfers between devices, to_all(): return lax.all_to_all(copies, axes, 0, 0)  5.18 us
  transfers between devices with their start and end apart: 5, of which 3 were waited for; matrix products, arithmetic and copies ran while one was open for 0% of the time, Pallas kernels for 7%

profile of v8, /device:TPU:1, one launch (start us, length us, event | category | flops | bytes accessed | tf_op | source)
XLA Modules:
  0.0 122.7 jit_solution(1546452517063679910)
XLA Ops:
  0.0 1.9 %shard_map.82 = (f32[32,1,384]{2,1,0:T(1,128)}, f32[2,1,32,128]{3,2,1,0:T(8,128)}, f32[2,1,32,128]{3,2,1,0:T(8,128)}) custom-call(s32[1]{0:T(128)} %bitcast.even_ref, s32[1,2,8]{2,1,0:T(2,128)} %labels_ref.1, f32[2,16,32,128]{3,2,1,0:T(8,128)} %residual_ref.3), custom_call_target="tpu_custom_call" | custom-call | tf_op jit(solution)/shard_map/pallas_call | solution.py:110
  1.9 0.0 copy-start.9
  1.9 0.0 copy-start.6
  1.9 29.4 %all-to-all-start = ((f32[32,1,384]{2,1,0:T(1,128)}), f32[32,1,384]{2,1,0:T(1,128)S(1)}, u32[]{:S(2)}, u32[]{:S(2)}) async-start(f32[32,1,384]{2,1,0:T(1,128)} %get-tuple-element.17), calls=%async_computation | async-start | bytes 98304 | tf_op jit(solution)/shard_map/all_to_all | solution.py:307
  31.4 0.0 copy-start
  31.4 4.4 %collective-permute-start = (f32[2,1,32,128]{3,2,1,0:T(8,128)S(1)}, f32[2,1,32,128]{3,2,1,0:T(8,128)S(1)}, u32[]{:S(2)}, u32[]{:S(2)}) collective-permute-start(f32[2,1,32,128]{3,2,1,0:T(8,128)S(1)} %copy-done.8), channel_id=1, source_target_pairs={{0,1020},{4,8},{8,4},{12,16},{16,12},{20,24},{24,20},{28,32},{32,2... | collective-permute-start | bytes 98312 | tf_op jit(solution)/shard_map/ppermute | solution.py:309
  35.8 12.4 %collective-permute-start.1 = (f32[2,1,32,128]{3,2,1,0:T(8,128)S(1)}, f32[2,1,32,128]{3,2,1,0:T(8,128)S(1)}, u32[]{:S(2)}, u32[]{:S(2)}) collective-permute-start(f32[2,1,32,128]{3,2,1,0:T(8,128)S(1)} %copy-done.7), channel_id=1, source_target_pairs={{0,4},{4,0},{8,12},{12,8},{16,20},{20,16},{24,28},{28,24},{32,36},... | collective-permute-start | bytes 98312 | tf_op jit(solution)/shard_map/ppermute | solution.py:308
  48.3 5.8 %all-to-all-done.parts_ref.line_ref = f32[32,1,384]{2,1,0:T(1,128)S(1)} async-done(((f32[32,1,384]{2,1,0:T(1,128)}), f32[32,1,384]{2,1,0:T(1,128)S(1)}, u32[]{:S(2)}, u32[]{:S(2)}) %all-to-all-start) | async-done | bytes 49184 | tf_op jit(solution)/shard_map/all_to_all | solution.py:307
  54.1 1.9 %shard_map.83 = f32[32,16,128]{2,1,0:T(8,128)} custom-call(s32[3]{0:T(128)S(1)} %and_select_fusion.spots_ref, f32[32,1,384]{2,1,0:T(1,128)S(1)} %all-to-all-done.parts_ref.line_ref), custom_call_target="tpu_custom_call" | custom-call | tf_op jit(solution)/shard_map/pallas_call | solution.py:278
  56.0 10.0 %all-to-all-start.1 = ((f32[32,16,128]{2,1,0:T(8,128)}), f32[32,16,128]{2,1,0:T(8,128)S(1)}, u32[]{:S(2)}, u32[]{:S(2)}) async-start(f32[32,16,128]{2,1,0:T(8,128)} %shard_map.83), calls=%async_computation.1 | async-start | bytes 524288 | tf_op jit(solution)/shard_map/all_to_all | solution.py:313
  66.0 0.0 copy-start.1
  66.0 1.9 %shard_map.84 = (bf16[336,336]{1,0:T(8,128)(2,1)S(1)}, bf16[336,336]{1,0:T(8,128)(2,1)S(1)}, f32[336,512]{1,0:T(8,128)S(1)}) custom-call(f32[2,16,32,128]{3,2,1,0:T(8,128)S(1)} %copy-done, f32[2,1,32,128]{3,2,1,0:T(8,128)S(1)} %get-tuple-element.23.x_low_ref, f32[2,1,32,128]{3,2,1,0:T(8,128)S(1)} %get-tuple-element.24.x_high_ref, f32[2,18,18]{2,1,0:T(8,128)S(1)} %copy.9.horiz_ref), custom_call_target="tpu_custom_call" | custom-call | flops 1000000000 | bytes 1048576 | tf_op jit(solution)/shard_map/pallas_call | solution.py:278
  68.0 6.9 %all-to-all-done.1.parts_ref = f32[32,16,128]{2,1,0:T(8,128)S(1)} async-done(((f32[32,16,128]{2,1,0:T(8,128)}), f32[32,16,128]{2,1,0:T(8,128)S(1)}, u32[]{:S(2)}, u32[]{:S(2)}) %all-to-all-start.1) | async-done | bytes 262176 | tf_op jit(solution)/shard_map/all_to_all | solution.py:313
  74.9 0.7 shard_map.85
  75.6 32.4 %all_to_all.20.line_parts_ref = f32[32,1,896]{2,1,0:T(1,128)S(1)} all-to-all(f32[32,1,896]{2,1,0:T(1,128)S(1)} %shard_map.85), channel_id=1, replica_groups=mesh['y'=4,'x'=4,'low'=8,'core'=2,'high'=4] {'high','low'}, dimensions={0} | all-to-all | bytes 229376 | tf_op jit(solution)/shard_map/all_to_all | solution.py:327
  108.0 0.6 broadcast_in_dim.2
  108.6 5.2 %all-to-all-start.3 = ((f32[32,2,128]{2,1,0:T(2,128)}), f32[32,2,128]{2,1,0:T(2,128)S(1)}, u32[]{:S(2)}, u32[]{:S(2)}) async-start(f32[32,2,128]{2,1,0:T(2,128)} %broadcast_in_dim.2), calls=%async_computation.3 | async-start | bytes 65536 | tf_op jit(solution)/shard_map/all_to_all | solution.py:292
  113.8 0.0 copy-start.2
  113.8 0.0 copy-start.4
  113.9 0.6 copy-done.2
  114.5 0.0 copy-done.4
  114.5 4.4 %shard_map.86.local_ref = f32[2,16,32,128]{3,2,1,0:T(8,128)S(1)} custom-call(s32[3]{0:T(128)S(1)} %and_select_fusion.spots_ref, f32[2,16,32,128]{3,2,1,0:T(8,128)S(1)} %copy-done, f32[2,1,32,128]{3,2,1,0:T(8,128)S(1)} %get-tuple-element.23.x_low_ref, f32[2,1,32,128]{3,2,1,0:T(8,128)S(1)} %get-tuple-element.24.x_high_ref, ...), custom_call_target="tpu_custom_call" | custom-call | tf_op jit(solution)/shard_map/pallas_call | solution.py:278
  118.9 2.3 %all-to-all-done.3.coarse_ref = f32[32,2,128]{2,1,0:T(2,128)S(1)} async-done(((f32[32,2,128]{2,1,0:T(2,128)}), f32[32,2,128]{2,1,0:T(2,128)S(1)}, u32[]{:S(2)}, u32[]{:S(2)}) %all-to-all-start.3) | async-done | bytes 32800 | tf_op jit(solution)/shard_map/all_to_all | solution.py:292
  121.2 1.5 %shard_map.87 = f32[2,16,32,128]{3,2,1,0:T(8,128)} custom-call(s32[1,2,8]{2,1,0:T(2,128)S(1)} %copy-done.3, f32[2,16,32,128]{3,2,1,0:T(8,128)S(1)} %shard_map.86.local_ref, f32[32,2,128]{2,1,0:T(2,128)S(1)} %all-to-all-done.3.coarse_ref), custom_call_target="tpu_custom_call" | custom-call | tf_op jit(solution)/shard_map/pallas_call | solution.py:278
  (20 shorter events, 0.1 us)
Async XLA Ops:
  1.9 29.5 %copy-start.8 = (f32[2,1,32,128]{3,2,1,0:T(8,128)S(1)}, f32[2,1,32,128]{3,2,1,0:T(8,128)}, u32[]{:S(2)}) copy-start(f32[2,1,32,128]{3,2,1,0:T(8,128)} %get-tuple-element.18) | copy-start | bytes 98308
  1.9 33.9 %copy-start.7 = (f32[2,1,32,128]{3,2,1,0:T(8,128)S(1)}, f32[2,1,32,128]{3,2,1,0:T(8,128)}, u32[]{:S(2)}) copy-start(f32[2,1,32,128]{3,2,1,0:T(8,128)} %get-tuple-element.19) | copy-start | bytes 98308
  1.9 46.3 %copy-start.9 = (s32[3]{0:T(128)S(1)}, s32[3]{0:T(128)}, u32[]{:S(2)}) copy-start(s32[3]{0:T(128)} %constant.35.clone) | copy-start | bytes 40
  1.9 46.4 %copy-start.6 = (f32[2,18,18]{2,0,1:T(2,128)S(1)}, f32[2,18,18]{2,0,1:T(2,128)}, u32[]{:S(2)}) copy-start(f32[2,18,18]{2,0,1:T(2,128)} %param.9) | copy-start | bytes 7780
  1.9 52.1 %all-to-all-start = ((f32[32,1,384]{2,1,0:T(1,128)}), f32[32,1,384]{2,1,0:T(1,128)S(1)}, u32[]{:S(2)}, u32[]{:S(2)}) async-start(f32[32,1,384]{2,1,0:T(1,128)} %get-tuple-element.17), calls=%async_computation | async-start | bytes 98304 | tf_op jit(solution)/shard_map/all_to_all | solution.py:307
  31.4 34.7 %copy-start = (f32[2,16,32,128]{3,2,1,0:T(8,128)S(1)}, f32[2,16,32,128]{3,2,1,0:T(8,128)}, u32[]{:S(2)}) copy-start(f32[2,16,32,128]{3,2,1,0:T(8,128)} %residual_ref.3) | copy-start | bytes 1572868
  31.4 34.6 %collective-permute-start = (f32[2,1,32,128]{3,2,1,0:T(8,128)S(1)}, f32[2,1,32,128]{3,2,1,0:T(8,128)S(1)}, u32[]{:S(2)}, u32[]{:S(2)}) collective-permute-start(f32[2,1,32,128]{3,2,1,0:T(8,128)S(1)} %copy-done.8), channel_id=1, source_target_pairs={{0,1020},{4,8},{8,4},{12,16},{16,12},{20,24},{24,20},{28,32},{32,2... | collective-permute-start | bytes 98312 | tf_op jit(solution)/shard_map/ppermute | solution.py:309
  35.8 30.2 %collective-permute-start.1 = (f32[2,1,32,128]{3,2,1,0:T(8,128)S(1)}, f32[2,1,32,128]{3,2,1,0:T(8,128)S(1)}, u32[]{:S(2)}, u32[]{:S(2)}) collective-permute-start(f32[2,1,32,128]{3,2,1,0:T(8,128)S(1)} %copy-done.7), channel_id=1, source_target_pairs={{0,4},{4,0},{8,12},{12,8},{16,20},{20,16},{24,28},{28,24},{32,36},... | collective-permute-start | bytes 98312 | tf_op jit(solution)/shard_map/ppermute | solution.py:308
  56.0 18.9 %all-to-all-start.1 = ((f32[32,16,128]{2,1,0:T(8,128)}), f32[32,16,128]{2,1,0:T(8,128)S(1)}, u32[]{:S(2)}, u32[]{:S(2)}) async-start(f32[32,16,128]{2,1,0:T(8,128)} %shard_map.83), calls=%async_computation.1 | async-start | bytes 524288 | tf_op jit(solution)/shard_map/all_to_all | solution.py:313
  66.0 8.9 %copy-start.1 = (f32[16,1024]{1,0:T(8,128)S(1)}, f32[16,1024]{1,0:T(8,128)}, u32[]{:S(2)}) copy-start(f32[16,1024]{1,0:T(8,128)} %matrix_ref.1) | copy-start | bytes 196612
  108.0 5.9 %copy-start.5 = (f32[8,18,18]{2,0,1:T(8,128)S(1)}, f32[8,18,18]{2,0,1:T(8,128)}, u32[]{:S(2)}) copy-start(f32[8,18,18]{2,0,1:T(8,128)} %param.11) | copy-start | bytes 31108
  108.6 12.6 %all-to-all-start.3 = ((f32[32,2,128]{2,1,0:T(2,128)}), f32[32,2,128]{2,1,0:T(2,128)S(1)}, u32[]{:S(2)}, u32[]{:S(2)}) async-start(f32[32,2,128]{2,1,0:T(2,128)} %broadcast_in_dim.2), calls=%async_computation.3 | async-start | bytes 65536 | tf_op jit(solution)/shard_map/all_to_all | solution.py:292
  113.8 0.7 copy-start.2
  113.8 0.7 copy-start.4
  114.5 6.7 %copy-start.3 = (s32[1,2,8]{2,1,0:T(2,128)S(1)}, s32[1,2,8]{2,1,0:T(2,128)}, u32[]{:S(2)}) copy-start(s32[1,2,8]{2,1,0:T(2,128)} %labels_ref.1) | copy-start | bytes 196

commit v9 on v8

--- a/solution.py
+++ b/solution.py
@@ -174,7 +174,9 @@
 
 
 def prepare_kernel(
-    residual_ref, x_low_ref, x_high_ref, horiz_ref, high_ref, low_ref, hat_ref, box_ref
+    residual_ref, x_low_ref, x_high_ref, horiz_ref, horiz_values_ref, upward_ref, upward_values_ref,
+    high_ref, low_ref, hat_ref, line_high_ref, line_low_ref, own_high_ref, own_low_ref, inverse_ref,
+    box_ref, line_ref, line_values_ref,
 ):
     x_of, y_of = point_index((POINTS, EXTENT), 0)
     mode = iota((POINTS, EXTENT), 1)
@@ -196,12 +198,6 @@
             box_ref[272:288, lanes] = x_high_ref[v, 0, ys, :]
     hat_ref[...] = dot3((high[:288], low[:288]), split(box_ref[...]), ((0,), (0,)))
 
-
-def finish_kernel(
-    spots_ref, residual_ref, x_low_ref, x_high_ref, line_parts_ref, high_ref, low_ref, hat_ref,
-    horiz_values_ref, upward_ref, upward_values_ref,
-    out_ref, box_ref, line_ref, line_values_ref,
-):
     line_ref[...] = jnp.zeros_like(line_ref)
     for k in range(8):
         begin = 16 * k - 1
@@ -212,8 +208,8 @@
     line = line_ref[...]
     z = iota((128, 144), 0)
     layer, _ = pair_index((128, 144), 1)
-    line_own = split(jnp.where((z >> 4) == layer, line, 0.0))
-    line = split(line)
+    line_high_ref[...], line_low_ref[...] = split(line)
+    own_high_ref[...], own_low_ref[...] = split(jnp.where((z >> 4) == layer, line, 0.0))
 
     pair_first, pair_second = pair_index((PAIRS, EXTENT), 0)
     table = iota((PAIRS, EXTENT), 1)
@@ -223,8 +219,13 @@
         axis=1,
         keepdims=True,
     )
-    inverse = 1.0 / (values + line_values_ref[...])
-
+    inverse_ref[...] = 1.0 / (values + line_values_ref[...])
+
+
+def finish_kernel(
+    spots_ref, residual_ref, x_low_ref, x_high_ref, line_parts_ref, high_ref, low_ref, hat_ref,
+    line_high_ref, line_low_ref, own_high_ref, own_low_ref, inverse_ref, out_ref, box_ref,
+):
     for v in range(2):
         rows = slice(SPAN * v, SPAN * v + SPAN)
         for j in range(2):
@@ -244,6 +245,9 @@
                     box_ref[begin + 17 : begin + 18, lanes] = x_high_ref[v, 0, edge : edge + 1, :]
     sides = (high_ref[288:336, :], low_ref[288:336, :])
     own = (high_ref[0:256, :], low_ref[0:256, :])
+    line = (line_high_ref[...], line_low_ref[...])
+    line_own = (own_high_ref[...], own_low_ref[...])
+    inverse = inverse_ref[...]
     all_hat = hat_ref[...] + dot3(sides, split(box_ref[...]), ((0,), (0,)))
 
     for part in range(4):
@@ -312,11 +316,15 @@
     dense = call(scatter_kernel, (PLANE_SIZE, 16, 128), [spots], [line_parts])
     plane_parts = lax.all_to_all(dense, PLANE, 0, 0)
     table = jax.ShapeDtypeStruct((POINTS, PAIRS), jnp.bfloat16)
+    line_table = jax.ShapeDtypeStruct((128, 144), jnp.bfloat16)
+    sums, reciprocals = (jax.ShapeDtypeStruct((PAIRS, n), jnp.float32) for n in (512, 144))
     prepared = call(
         prepare_kernel,
-        [table, table, jax.ShapeDtypeStruct((PAIRS, 512), jnp.float32)],
-        [], [residual, x_low, x_high, horiz_vectors],
-        [pltpu.VMEM((288, 512), jnp.float32)],
+        [table, table, sums, line_table, line_table, line_table, line_table, reciprocals],
+        [],
+        [residual, x_low, x_high, horiz_vectors, horiz_values, upward_eigen_tables, upward_eigen_values],
+        [pltpu.VMEM((288, 512), jnp.float32), pltpu.VMEM((128, 144), jnp.float32),
+         pltpu.VMEM((1, 144), jnp.float32)],
         pl.CostEstimate(flops=WINDOW_FLOPS, transcendentals=0, bytes_accessed=1 << 20),
     )
     plane_parts, prepared, x_low, x_high = barrier((plane_parts, prepared, x_low, x_high))
@@ -329,10 +337,8 @@
     coarse = to_all(rows, PLANE, PLANE_SIZE)
     local = call(
         finish_kernel, residual.shape, [spots],
-        [residual, x_low, x_high, row_parts, *prepared, horiz_values,
-         upward_eigen_tables, upward_eigen_values],
-        [pltpu.VMEM((48, 512), jnp.float32), pltpu.VMEM((128, 144), jnp.float32),
-         pltpu.VMEM((1, 144), jnp.float32)],
+        [residual, x_low, x_high, row_parts, *prepared],
+        [pltpu.VMEM((48, 512), jnp.float32)],
     )
     return call(merge_kernel, residual.shape, [labels], [local, coarse])
 

time: 123 us -> 123 us (level)
  no operation moved by 1% of the time
where the time goes in v9:
time: 123 us
  starting transfers between devices  61.3 us (50%)
  blocking collectives  32.4 us (26%)
  waiting for transfers between devices  15 us (12%)
  Pallas kernels  12.4 us (10%)
  local copies, waits for them, and re-layouts  1.36 us (1%)
    all_to_all x1, blocking collectives, on_device(): row_parts = lax.all_to_all(terms, LINE, 0, 0)  32.4 us
    all_to_all x1, starting transfers between devices, on_device(): line_parts = lax.all_to_all(parts, LINE, 0, 0)  29.4 us
    ppermute x1, starting transfers between devices, on_device(): inner = lax.ppermute(inner, GROUP, [(i, i ^ 1) for i in range(256)])  12.4 us
    pallas_call x5, Pallas kernels, call(): pl.pallas_call(kernel, out_shape=out_shape, in_specs=[pl.BlockSpec(memory...  10.5 us
    all_to_all x1, starting transfers between devices, on_device(): plane_parts = lax.all_to_all(dense, PLANE, 0, 0)  9.97 us
    all_to_all x1, waiting for transfers between devices, on_device(): plane_parts = lax.all_to_all(dense, PLANE, 0, 0)  6.19 us
    all_to_all x1, waiting for transfers between devices, on_device(): line_parts = lax.all_to_all(parts, LINE, 0, 0)  5.87 us
    all_to_all x1, starting transfers between devices, to_all(): return lax.all_to_all(copies, axes, 0, 0)  5.18 us
  transfers between devices with their start and end apart: 5, of which 3 were waited for; matrix products, arithmetic and copies ran while one was open for 0% of the time, Pallas kernels for 7%

profile of v9, /device:TPU:1, one launch (start us, length us, event | category | flops | bytes accessed | tf_op | source)
XLA Modules:
  0.0 122.7 jit_solution(6929399338350774574)
XLA Ops:
  0.0 1.9 %shard_map.82 = (f32[32,1,384]{2,1,0:T(1,128)}, f32[2,1,32,128]{3,2,1,0:T(8,128)}, f32[2,1,32,128]{3,2,1,0:T(8,128)}) custom-call(s32[1]{0:T(128)} %bitcast.even_ref, s32[1,2,8]{2,1,0:T(2,128)} %labels_ref.1, f32[2,16,32,128]{3,2,1,0:T(8,128)} %residual_ref.3), custom_call_target="tpu_custom_call" | custom-call | tf_op jit(solution)/shard_map/pallas_call | solution.py:110
  1.9 0.0 copy-start.7
  1.9 0.0 copy-start.5
  1.9 29.4 %all-to-all-start = ((f32[32,1,384]{2,1,0:T(1,128)}), f32[32,1,384]{2,1,0:T(1,128)S(1)}, u32[]{:S(2)}, u32[]{:S(2)}) async-start(f32[32,1,384]{2,1,0:T(1,128)} %get-tuple-element.27), calls=%async_computation | async-start | bytes 98304 | tf_op jit(solution)/shard_map/all_to_all | solution.py:311
  31.3 0.0 copy-start.6
  31.4 4.3 %collective-permute-start = (f32[2,1,32,128]{3,2,1,0:T(8,128)}, f32[2,1,32,128]{3,2,1,0:T(8,128)S(1)}, u32[]{:S(2)}, u32[]{:S(2)}) collective-permute-start(f32[2,1,32,128]{3,2,1,0:T(8,128)} %get-tuple-element.28), channel_id=1, source_target_pairs={{0,1020},{4,8},{8,4},{12,16},{16,12},{20,24},{24,20},{28,32},{32,2... | collective-permute-start | bytes 98312 | tf_op jit(solution)/shard_map/ppermute | solution.py:313
  35.6 12.4 %collective-permute-start.1 = (f32[2,1,32,128]{3,2,1,0:T(8,128)}, f32[2,1,32,128]{3,2,1,0:T(8,128)S(1)}, u32[]{:S(2)}, u32[]{:S(2)}) collective-permute-start(f32[2,1,32,128]{3,2,1,0:T(8,128)} %get-tuple-element.29), channel_id=1, source_target_pairs={{0,4},{4,0},{8,12},{12,8},{16,20},{20,16},{24,28},{28,24},{32,36},... | collective-permute-start | bytes 98312 | tf_op jit(solution)/shard_map/ppermute | solution.py:312
  48.2 0.0 copy-start
  48.2 5.9 %all-to-all-done.parts_ref.line_ref = f32[32,1,384]{2,1,0:T(1,128)S(1)} async-done(((f32[32,1,384]{2,1,0:T(1,128)}), f32[32,1,384]{2,1,0:T(1,128)S(1)}, u32[]{:S(2)}, u32[]{:S(2)}) %all-to-all-start) | async-done | bytes 49184 | tf_op jit(solution)/shard_map/all_to_all | solution.py:311
  54.0 1.9 %shard_map.83 = f32[32,16,128]{2,1,0:T(8,128)} custom-call(s32[3]{0:T(128)S(1)} %and_select_fusion.spots_ref, f32[32,1,384]{2,1,0:T(1,128)S(1)} %all-to-all-done.parts_ref.line_ref), custom_call_target="tpu_custom_call" | custom-call | tf_op jit(solution)/shard_map/pallas_call | solution.py:282
  56.0 10.0 %all-to-all-start.1 = ((f32[32,16,128]{2,1,0:T(8,128)}), f32[32,16,128]{2,1,0:T(8,128)S(1)}, u32[]{:S(2)}, u32[]{:S(2)}) async-start(f32[32,16,128]{2,1,0:T(8,128)} %shard_map.83), calls=%async_computation.1 | async-start | bytes 524288 | tf_op jit(solution)/shard_map/all_to_all | solution.py:317
  66.0 0.0 copy-start.4
  66.0 0.6 copy-done.3
  66.7 0.0 copy-done.4
  66.7 2.0 %shard_map.84 = (bf16[336,336]{1,0:T(8,128)(2,1)S(1)}, bf16[336,336]{1,0:T(8,128)(2,1)S(1)}, f32[336,512]{1,0:T(8,128)S(1)}, bf16[128,144]{1,0:T(8,128)(2,1)S(1)...) custom-call(f32[2,16,32,128]{3,2,1,0:T(8,128)S(1)} %copy-done, ...), custom_call_target="tpu_custom_call" | custom-call | flops 1000000000 | bytes 1048576 | tf_op jit(solution)/shard_map/pallas_call | solution.py:282
  68.7 6.2 %all-to-all-done.1.parts_ref = f32[32,16,128]{2,1,0:T(8,128)S(1)} async-done(((f32[32,16,128]{2,1,0:T(8,128)}), f32[32,16,128]{2,1,0:T(8,128)S(1)}, u32[]{:S(2)}, u32[]{:S(2)}) %all-to-all-start.1) | async-done | bytes 262176 | tf_op jit(solution)/shard_map/all_to_all | solution.py:317
  74.9 0.7 shard_map.85
  75.6 32.4 %all_to_all.20.line_parts_ref = f32[32,1,896]{2,1,0:T(1,128)S(1)} all-to-all(f32[32,1,896]{2,1,0:T(1,128)S(1)} %shard_map.85), channel_id=1, replica_groups=mesh['y'=4,'x'=4,'low'=8,'core'=2,'high'=4] {'high','low'}, dimensions={0} | all-to-all | bytes 229376 | tf_op jit(solution)/shard_map/all_to_all | solution.py:335
  108.0 0.6 broadcast_in_dim.2
  108.6 5.2 %all-to-all-start.3 = ((f32[32,2,128]{2,1,0:T(2,128)}), f32[32,2,128]{2,1,0:T(2,128)S(1)}, u32[]{:S(2)}, u32[]{:S(2)}) async-start(f32[32,2,128]{2,1,0:T(2,128)} %broadcast_in_dim.2), calls=%async_computation.3 | async-start | bytes 65536 | tf_op jit(solution)/shard_map/all_to_all | solution.py:296
  113.8 0.0 copy-start.2
  113.8 4.4 %shard_map.86.local_ref = f32[2,16,32,128]{3,2,1,0:T(8,128)S(1)} custom-call(s32[3]{0:T(128)S(1)} %and_select_fusion.spots_ref, f32[2,16,32,128]{3,2,1,0:T(8,128)S(1)} %copy-done, f32[2,1,32,128]{3,2,1,0:T(8,128)S(1)} %get-tuple-element.38.x_low_ref, f32[2,1,32,128]{3,2,1,0:T(8,128)S(1)} %get-tuple-element.39.x_high_ref, ...), custom_call_target="tpu_custom_call" | custom-call | tf_op jit(solution)/shard_map/pallas_call | solution.py:282
  118.2 3.0 %all-to-all-done.3.coarse_ref = f32[32,2,128]{2,1,0:T(2,128)S(1)} async-done(((f32[32,2,128]{2,1,0:T(2,128)}), f32[32,2,128]{2,1,0:T(2,128)S(1)}, u32[]{:S(2)}, u32[]{:S(2)}) %all-to-all-start.3) | async-done | bytes 32800 | tf_op jit(solution)/shard_map/all_to_all | solution.py:296
  121.2 1.5 %shard_map.87 = f32[2,16,32,128]{3,2,1,0:T(8,128)} custom-call(s32[1,2,8]{2,1,0:T(2,128)S(1)} %copy-done.2, f32[2,16,32,128]{3,2,1,0:T(8,128)S(1)} %shard_map.86.local_ref, f32[32,2,128]{2,1,0:T(2,128)S(1)} %all-to-all-done.3.coarse_ref), custom_call_target="tpu_custom_call" | custom-call | tf_op jit(solution)/shard_map/pallas_call | solution.py:282
  (16 shorter events, 0.1 us)
Async XLA Ops:
  1.9 46.2 %copy-start.7 = (s32[3]{0:T(128)S(1)}, s32[3]{0:T(128)}, u32[]{:S(2)}) copy-start(s32[3]{0:T(128)} %constant.35.clone) | copy-start | bytes 40
  1.9 46.2 %copy-start.5 = (f32[8,18,18]{2,0,1:T(8,128)S(1)}, f32[8,18,18]{2,0,1:T(8,128)}, u32[]{:S(2)}) copy-start(f32[8,18,18]{2,0,1:T(8,128)} %param.11) | copy-start | bytes 31108
  1.9 52.1 %all-to-all-start = ((f32[32,1,384]{2,1,0:T(1,128)}), f32[32,1,384]{2,1,0:T(1,128)S(1)}, u32[]{:S(2)}, u32[]{:S(2)}) async-start(f32[32,1,384]{2,1,0:T(1,128)} %get-tuple-element.27), calls=%async_computation | async-start | bytes 98304 | tf_op jit(solution)/shard_map/all_to_all | solution.py:311
  31.3 16.8 %copy-start.6 = (f32[2,18,18]{2,0,1:T(2,128)S(1)}, f32[2,18,18]{2,0,1:T(2,128)}, u32[]{:S(2)}) copy-start(f32[2,18,18]{2,0,1:T(2,128)} %param.9) | copy-start | bytes 7780
  31.4 34.6 %collective-permute-start = (f32[2,1,32,128]{3,2,1,0:T(8,128)}, f32[2,1,32,128]{3,2,1,0:T(8,128)S(1)}, u32[]{:S(2)}, u32[]{:S(2)}) collective-permute-start(f32[2,1,32,128]{3,2,1,0:T(8,128)} %get-tuple-element.28), channel_id=1, source_target_pairs={{0,1020},{4,8},{8,4},{12,16},{16,12},{20,24},{24,20},{28,32},{32,2... | collective-permute-start | bytes 98312 | tf_op jit(solution)/shard_map/ppermute | solution.py:313
  35.6 30.4 %collective-permute-start.1 = (f32[2,1,32,128]{3,2,1,0:T(8,128)}, f32[2,1,32,128]{3,2,1,0:T(8,128)S(1)}, u32[]{:S(2)}, u32[]{:S(2)}) collective-permute-start(f32[2,1,32,128]{3,2,1,0:T(8,128)} %get-tuple-element.29), channel_id=1, source_target_pairs={{0,4},{4,0},{8,12},{12,8},{16,20},{20,16},{24,28},{28,24},{32,36},... | collective-permute-start | bytes 98312 | tf_op jit(solution)/shard_map/ppermute | solution.py:312
  48.2 17.9 %copy-start = (f32[2,16,32,128]{3,2,1,0:T(8,128)S(1)}, f32[2,16,32,128]{3,2,1,0:T(8,128)}, u32[]{:S(2)}) copy-start(f32[2,16,32,128]{3,2,1,0:T(8,128)} %residual_ref.3) | copy-start | bytes 1572868
  56.0 18.9 %all-to-all-start.1 = ((f32[32,16,128]{2,1,0:T(8,128)}), f32[32,16,128]{2,1,0:T(8,128)S(1)}, u32[]{:S(2)}, u32[]{:S(2)}) async-start(f32[32,16,128]{2,1,0:T(8,128)} %shard_map.83), calls=%async_computation.1 | async-start | bytes 524288 | tf_op jit(solution)/shard_map/all_to_all | solution.py:317
  66.0 0.7 copy-start.3
  66.0 0.7 copy-start.4
  66.7 8.2 %copy-start.1 = (f32[16,1024]{1,0:T(8,128)S(1)}, f32[16,1024]{1,0:T(8,128)}, u32[]{:S(2)}) copy-start(f32[16,1024]{1,0:T(8,128)} %matrix_ref.1) | copy-start | bytes 196612
  108.6 12.6 %all-to-all-start.3 = ((f32[32,2,128]{2,1,0:T(2,128)}), f32[32,2,128]{2,1,0:T(2,128)S(1)}, u32[]{:S(2)}, u32[]{:S(2)}) async-start(f32[32,2,128]{2,1,0:T(2,128)} %broadcast_in_dim.2), calls=%async_computation.3 | async-start | bytes 65536 | tf_op jit(solution)/shard_map/all_to_all | solution.py:296
  113.8 7.4 %copy-start.2 = (s32[1,2,8]{2,1,0:T(2,128)S(1)}, s32[1,2,8]{2,1,0:T(2,128)}, u32[]{:S(2)}) copy-start(s32[1,2,8]{2,1,0:T(2,128)} %labels_ref.1) | copy-start | bytes 196

commit v10 on v8

--- a/solution.py
+++ b/solution.py
@@ -254,6 +254,11 @@
         out_ref[v, :, j * SPAN : (j + 1) * SPAN, :] = solved.reshape(SPAN, SPAN, 128)
 
 
+def rows_kernel(parts_ref, out_ref):
+    rows = jnp.sum(parts_ref[:, 0, 0:128].reshape(4, 2, 4, 128), axis=(0, 2))
+    out_ref[...] = jnp.broadcast_to(rows[None], out_ref.shape)
+
+
 def merge_kernel(labels_ref, local_ref, coarse_ref, out_ref):
     lane = iota((1, 128), 1)
     for j in range(2):
@@ -287,11 +292,6 @@
     )(*scalars, *arrays)
 
 
-def to_all(value, axes, size):
-    copies = jnp.broadcast_to(value[None], (size,) + value.shape)
-    return lax.all_to_all(copies, axes, 0, 0)
-
-
 def on_device(
     residual, horiz_vectors, horiz_values, upward_eigen_tables, upward_eigen_values,
     aggregate_map, coarse_inverse,
@@ -325,8 +325,7 @@
         [plane_parts, line_parts, x_low, x_high, coarse_inverse],
     )
     row_parts = lax.all_to_all(terms, LINE, 0, 0)
-    rows = row_parts[:, 0, :128].reshape(4, 2, 4, 128).sum(axis=(0, 2))
-    coarse = to_all(rows, PLANE, PLANE_SIZE)
+    coarse = lax.all_to_all(call(rows_kernel, (PLANE_SIZE, 2, 128), [], [row_parts]), PLANE, 0, 0)
     local = call(
         finish_kernel, residual.shape, [spots],
         [residual, x_low, x_high, row_parts, *prepared, horiz_values,

time: 123 us -> 123 us (level)
    pallas_call x5 -> x6, Pallas kernels: 10.5 us -> 11.1 us  [call(): pl.pallas_call(kernel, out_shape=out_shape, in_specs=[pl.BlockSpec(memory...]
where the time goes in v10:
time: 123 us
  starting transfers between devices  61.4 us (50%)
  blocking collectives  32.4 us (26%)
  waiting for transfers between devices  14.9 us (12%)
  Pallas kernels  13 us (11%)
    all_to_all x1, blocking collectives, on_device(): row_parts = lax.all_to_all(terms, LINE, 0, 0)  32.4 us
    all_to_all x1, starting transfers between devices, on_device(): line_parts = lax.all_to_all(parts, LINE, 0, 0)  29.4 us
    ppermute x1, starting transfers between devices, on_device(): inner = lax.ppermute(inner, GROUP, [(i, i ^ 1) for i in range(256)])  12.4 us
    pallas_call x6, Pallas kernels, call(): pl.pallas_call(kernel, out_shape=out_shape, in_specs=[pl.BlockSpec(memory...  11.1 us
    all_to_all x1, starting transfers between devices, on_device(): plane_parts = lax.all_to_all(dense, PLANE, 0, 0)  9.97 us
    all_to_all x1, waiting for transfers between devices, on_device(): plane_parts = lax.all_to_all(dense, PLANE, 0, 0)  6.91 us
    all_to_all x1, waiting for transfers between devices, on_device(): line_parts = lax.all_to_all(parts, LINE, 0, 0)  5.76 us
    all_to_all x1, starting transfers between devices, on_device(): lax.all_to_all(call(rows_kernel, (PLANE_SIZE, 2, 128), [], [row_parts]),...  5.18 us
  transfers between devices with their start and end apart: 5, of which 3 were waited for; matrix products, arithmetic and copies ran while one was open for 0% of the time, Pallas kernels for 7%

profile of v10, /device:TPU:1, one launch (start us, length us, event | category | flops | bytes accessed | tf_op | source)
XLA Modules:
  0.0 122.7 jit_solution(8263210463907973471)
XLA Ops:
  0.0 1.9 %shard_map.82 = (f32[32,1,384]{2,1,0:T(1,128)}, f32[2,1,32,128]{3,2,1,0:T(8,128)}, f32[2,1,32,128]{3,2,1,0:T(8,128)}) custom-call(s32[1]{0:T(128)} %bitcast.even_ref, s32[1,2,8]{2,1,0:T(2,128)} %labels_ref.1, f32[2,16,32,128]{3,2,1,0:T(8,128)} %residual_ref.3), custom_call_target="tpu_custom_call" | custom-call | tf_op jit(solution)/shard_map/pallas_call | solution.py:110
  1.9 0.0 copy-start.9
  1.9 0.0 copy-start.6
  1.9 29.4 %all-to-all-start = ((f32[32,1,384]{2,1,0:T(1,128)}), f32[32,1,384]{2,1,0:T(1,128)S(1)}, u32[]{:S(2)}, u32[]{:S(2)}) async-start(f32[32,1,384]{2,1,0:T(1,128)} %get-tuple-element.17), calls=%async_computation | async-start | bytes 98304 | tf_op jit(solution)/shard_map/all_to_all | solution.py:307
  31.4 0.0 copy-start
  31.4 4.4 %collective-permute-start = (f32[2,1,32,128]{3,2,1,0:T(8,128)S(1)}, f32[2,1,32,128]{3,2,1,0:T(8,128)S(1)}, u32[]{:S(2)}, u32[]{:S(2)}) collective-permute-start(f32[2,1,32,128]{3,2,1,0:T(8,128)S(1)} %copy-done.8), channel_id=1, source_target_pairs={{0,1020},{4,8},{8,4},{12,16},{16,12},{20,24},{24,20},{28,32},{32,2... | collective-permute-start | bytes 98312 | tf_op jit(solution)/shard_map/ppermute | solution.py:309
  35.8 12.4 %collective-permute-start.1 = (f32[2,1,32,128]{3,2,1,0:T(8,128)S(1)}, f32[2,1,32,128]{3,2,1,0:T(8,128)S(1)}, u32[]{:S(2)}, u32[]{:S(2)}) collective-permute-start(f32[2,1,32,128]{3,2,1,0:T(8,128)S(1)} %copy-done.7), channel_id=1, source_target_pairs={{0,4},{4,0},{8,12},{12,8},{16,20},{20,16},{24,28},{28,24},{32,36},... | collective-permute-start | bytes 98312 | tf_op jit(solution)/shard_map/ppermute | solution.py:308
  48.3 5.8 %all-to-all-done.parts_ref.line_ref = f32[32,1,384]{2,1,0:T(1,128)S(1)} async-done(((f32[32,1,384]{2,1,0:T(1,128)}), f32[32,1,384]{2,1,0:T(1,128)S(1)}, u32[]{:S(2)}, u32[]{:S(2)}) %all-to-all-start) | async-done | bytes 49184 | tf_op jit(solution)/shard_map/all_to_all | solution.py:307
  54.1 1.9 %shard_map.83 = f32[32,16,128]{2,1,0:T(8,128)} custom-call(s32[3]{0:T(128)S(1)} %and_select_fusion.spots_ref, f32[32,1,384]{2,1,0:T(1,128)S(1)} %all-to-all-done.parts_ref.line_ref), custom_call_target="tpu_custom_call" | custom-call | tf_op jit(solution)/shard_map/pallas_call | solution.py:283
  56.0 10.0 %all-to-all-start.1 = ((f32[32,16,128]{2,1,0:T(8,128)}), f32[32,16,128]{2,1,0:T(8,128)S(1)}, u32[]{:S(2)}, u32[]{:S(2)}) async-start(f32[32,16,128]{2,1,0:T(8,128)} %shard_map.83), calls=%async_computation.1 | async-start | bytes 524288 | tf_op jit(solution)/shard_map/all_to_all | solution.py:313
  66.0 0.0 copy-start.1
  66.0 1.9 %shard_map.84 = (bf16[336,336]{1,0:T(8,128)(2,1)S(1)}, bf16[336,336]{1,0:T(8,128)(2,1)S(1)}, f32[336,512]{1,0:T(8,128)S(1)}) custom-call(f32[2,16,32,128]{3,2,1,0:T(8,128)S(1)} %copy-done, f32[2,1,32,128]{3,2,1,0:T(8,128)S(1)} %get-tuple-element.23.x_low_ref, f32[2,1,32,128]{3,2,1,0:T(8,128)S(1)} %get-tuple-element.24.x_high_ref, f32[2,18,18]{2,1,0:T(8,128)S(1)} %copy.9.horiz_ref), custom_call_target="tpu_custom_call" | custom-call | flops 1000000000 | bytes 1048576 | tf_op jit(solution)/shard_map/pallas_call | solution.py:283
  68.0 6.9 %all-to-all-done.1.parts_ref = f32[32,16,128]{2,1,0:T(8,128)S(1)} async-done(((f32[32,16,128]{2,1,0:T(8,128)}), f32[32,16,128]{2,1,0:T(8,128)S(1)}, u32[]{:S(2)}, u32[]{:S(2)}) %all-to-all-start.1) | async-done | bytes 262176 | tf_op jit(solution)/shard_map/all_to_all | solution.py:313
  74.9 0.7 shard_map.85
  75.6 32.4 %all_to_all.20.line_parts_ref.parts_ref = f32[32,1,896]{2,1,0:T(1,128)S(1)} all-to-all(f32[32,1,896]{2,1,0:T(1,128)S(1)} %shard_map.85), channel_id=1, replica_groups=mesh['y'=4,'x'=4,'low'=8,'core'=2,'high'=4] {'high','low'}, dimensions={0} | all-to-all | bytes 229376 | tf_op jit(solution)/shard_map/all_to_all | solution.py:327
  108.0 0.6 shard_map.87
  108.6 5.2 %all-to-all-start.3 = ((f32[32,2,128]{2,1,0:T(2,128)}), f32[32,2,128]{2,1,0:T(2,128)S(1)}, u32[]{:S(2)}, u32[]{:S(2)}) async-start(f32[32,2,128]{2,1,0:T(2,128)} %shard_map.87), calls=%async_computation.3 | async-start | bytes 65536 | tf_op jit(solution)/shard_map/all_to_all | solution.py:328
  113.8 0.0 copy-start.2
  113.8 0.0 copy-start.4
  113.9 0.6 copy-done.2
  114.5 0.0 copy-done.4
  114.5 4.4 %shard_map.86.local_ref = f32[2,16,32,128]{3,2,1,0:T(8,128)S(1)} custom-call(s32[3]{0:T(128)S(1)} %and_select_fusion.spots_ref, f32[2,16,32,128]{3,2,1,0:T(8,128)S(1)} %copy-done, f32[2,1,32,128]{3,2,1,0:T(8,128)S(1)} %get-tuple-element.23.x_low_ref, f32[2,1,32,128]{3,2,1,0:T(8,128)S(1)} %get-tuple-element.24.x_high_ref, ...), custom_call_target="tpu_custom_call" | custom-call | tf_op jit(solution)/shard_map/pallas_call | solution.py:283
  118.9 2.3 %all-to-all-done.3.coarse_ref = f32[32,2,128]{2,1,0:T(2,128)S(1)} async-done(((f32[32,2,128]{2,1,0:T(2,128)}), f32[32,2,128]{2,1,0:T(2,128)S(1)}, u32[]{:S(2)}, u32[]{:S(2)}) %all-to-all-start.3) | async-done | bytes 32800 | tf_op jit(solution)/shard_map/all_to_all | solution.py:328
  121.2 1.5 %shard_map.88 = f32[2,16,32,128]{3,2,1,0:T(8,128)} custom-call(s32[1,2,8]{2,1,0:T(2,128)S(1)} %copy-done.3, f32[2,16,32,128]{3,2,1,0:T(8,128)S(1)} %shard_map.86.local_ref, f32[32,2,128]{2,1,0:T(2,128)S(1)} %all-to-all-done.3.coarse_ref), custom_call_target="tpu_custom_call" | custom-call | tf_op jit(solution)/shard_map/pallas_call | solution.py:283
  (18 shorter events, 0.1 us)
Async XLA Ops:
  1.9 29.5 %copy-start.8 = (f32[2,1,32,128]{3,2,1,0:T(8,128)S(1)}, f32[2,1,32,128]{3,2,1,0:T(8,128)}, u32[]{:S(2)}) copy-start(f32[2,1,32,128]{3,2,1,0:T(8,128)} %get-tuple-element.18) | copy-start | bytes 98308
  1.9 33.9 %copy-start.7 = (f32[2,1,32,128]{3,2,1,0:T(8,128)S(1)}, f32[2,1,32,128]{3,2,1,0:T(8,128)}, u32[]{:S(2)}) copy-start(f32[2,1,32,128]{3,2,1,0:T(8,128)} %get-tuple-element.19) | copy-start | bytes 98308
  1.9 46.3 %copy-start.9 = (s32[3]{0:T(128)S(1)}, s32[3]{0:T(128)}, u32[]{:S(2)}) copy-start(s32[3]{0:T(128)} %constant.33.clone) | copy-start | bytes 40
  1.9 46.4 %copy-start.6 = (f32[2,18,18]{2,0,1:T(2,128)S(1)}, f32[2,18,18]{2,0,1:T(2,128)}, u32[]{:S(2)}) copy-start(f32[2,18,18]{2,0,1:T(2,128)} %param.9) | copy-start | bytes 7780
  1.9 52.1 %all-to-all-start = ((f32[32,1,384]{2,1,0:T(1,128)}), f32[32,1,384]{2,1,0:T(1,128)S(1)}, u32[]{:S(2)}, u32[]{:S(2)}) async-start(f32[32,1,384]{2,1,0:T(1,128)} %get-tuple-element.17), calls=%async_computation | async-start | bytes 98304 | tf_op jit(solution)/shard_map/all_to_all | solution.py:307
  31.4 34.7 %copy-start = (f32[2,16,32,128]{3,2,1,0:T(8,128)S(1)}, f32[2,16,32,128]{3,2,1,0:T(8,128)}, u32[]{:S(2)}) copy-start(f32[2,16,32,128]{3,2,1,0:T(8,128)} %residual_ref.3) | copy-start | bytes 1572868
  31.4 34.6 %collective-permute-start = (f32[2,1,32,128]{3,2,1,0:T(8,128)S(1)}, f32[2,1,32,128]{3,2,1,0:T(8,128)S(1)}, u32[]{:S(2)}, u32[]{:S(2)}) collective-permute-start(f32[2,1,32,128]{3,2,1,0:T(8,128)S(1)} %copy-done.8), channel_id=1, source_target_pairs={{0,1020},{4,8},{8,4},{12,16},{16,12},{20,24},{24,20},{28,32},{32,2... | collective-permute-start | bytes 98312 | tf_op jit(solution)/shard_map/ppermute | solution.py:309
  35.8 30.2 %collective-permute-start.1 = (f32[2,1,32,128]{3,2,1,0:T(8,128)S(1)}, f32[2,1,32,128]{3,2,1,0:T(8,128)S(1)}, u32[]{:S(2)}, u32[]{:S(2)}) collective-permute-start(f32[2,1,32,128]{3,2,1,0:T(8,128)S(1)} %copy-done.7), channel_id=1, source_target_pairs={{0,4},{4,0},{8,12},{12,8},{16,20},{20,16},{24,28},{28,24},{32,36},... | collective-permute-start | bytes 98312 | tf_op jit(solution)/shard_map/ppermute | solution.py:308
  56.0 18.9 %all-to-all-start.1 = ((f32[32,16,128]{2,1,0:T(8,128)}), f32[32,16,128]{2,1,0:T(8,128)S(1)}, u32[]{:S(2)}, u32[]{:S(2)}) async-start(f32[32,16,128]{2,1,0:T(8,128)} %shard_map.83), calls=%async_computation.1 | async-start | bytes 524288 | tf_op jit(solution)/shard_map/all_to_all | solution.py:313
  66.0 8.9 %copy-start.1 = (f32[16,1024]{1,0:T(8,128)S(1)}, f32[16,1024]{1,0:T(8,128)}, u32[]{:S(2)}) copy-start(f32[16,1024]{1,0:T(8,128)} %matrix_ref.1) | copy-start | bytes 196612
  108.0 5.8 %copy-start.5 = (f32[8,18,18]{2,0,1:T(8,128)S(1)}, f32[8,18,18]{2,0,1:T(8,128)}, u32[]{:S(2)}) copy-start(f32[8,18,18]{2,0,1:T(8,128)} %param.11) | copy-start | bytes 31108
  108.6 12.6 %all-to-all-start.3 = ((f32[32,2,128]{2,1,0:T(2,128)}), f32[32,2,128]{2,1,0:T(2,128)S(1)}, u32[]{:S(2)}, u32[]{:S(2)}) async-start(f32[32,2,128]{2,1,0:T(2,128)} %shard_map.87), calls=%async_computation.3 | async-start | bytes 65536 | tf_op jit(solution)/shard_map/all_to_all | solution.py:328
  113.8 0.7 copy-start.2
  113.8 0.7 copy-start.4
  114.5 6.7 %copy-start.3 = (s32[1,2,8]{2,1,0:T(2,128)S(1)}, s32[1,2,8]{2,1,0:T(2,128)}, u32[]{:S(2)}) copy-start(s32[1,2,8]{2,1,0:T(2,128)} %labels_ref.1) | copy-start | bytes 196
